TPU v7x, 128 devices: a whole 4x4x4 slice. The times are simulated.
128 devices in a mesh: pair: 8 (over x, core), ints: 16 (over y, z).
Axes of the slice: x: 4, y: 4, z: 4, core: 2. Of those that a mesh axis runs over, the one named last changes fastest.
Arguments:
- t2: bfloat16 [4096, 8192], P('pair', 'ints'), may hold values from -6 to 6
- t2_live: int32 [8, 64], P('pair', 'ints'), may hold values 0 or 1
- int_tiles: int32 [5120, 2], P('ints'), may hold values from 0 to 63
- integrals: bfloat16 [5120, 128, 128], P('ints'), may hold values from -0.0625 to 0.0625
- cycle_w: bfloat16 [4096, 4096], P('pair'), may hold values from -0.09375 to 0.09375
- res_live: int32 [8, 64], P('pair', 'ints'), may hold values 0 or 1
Outputs:
- residual: float32 [4096, 8192], P('pair', 'ints')
All inputs are finite; a program needn't handle non-finite values. No bound on the sum of `t2_live` or of `res_live` on one device may be relied on, other than what follows from the above.
Results may differ from a plain program's by a relative error of at most 0.0003.
Values may be sent and summed in bfloat16 or wider, within the bound.
No kernel may reach another device: no remote copies, remote signals or barrier semaphores. Data moves between devices by JAX's collectives and lax.ppermute only.
A program may use at most 192 MiB of HBM per device.

v0:
```python
import jax
import jax.numpy as jnp
from jax import lax
from jax.sharding import PartitionSpec as P


def local(t2, t2_live, int_tiles, integrals, cycle_w, res_live):
    rows_here = t2.shape[0]
    tile_size = integrals.shape[1]
    tiles_here = t2.shape[1] // tile_size
    live_mask = t2_live[0].astype(t2.dtype)
    amps = (t2.reshape(rows_here, tiles_here, tile_size) * live_mask[None, :, None]).reshape(
        rows_here, tiles_here * tile_size
    )
    block_amps = lax.all_gather(amps, "ints", axis=1, tiled=True)
    tiles_all = block_amps.shape[1] // tile_size
    amps_tiled = block_amps.reshape(rows_here, tiles_all, tile_size)
    count_here = integrals.shape[0]
    group_size = 64
    tile_groups = int_tiles.reshape(count_here // group_size, group_size, 2)
    int_groups = integrals.reshape(count_here // group_size, group_size, tile_size, tile_size)
    tile_ids = jnp.arange(tiles_all, dtype=jnp.int32)

    def ladder_step(partial_value, entry):
        pairs_uv, blocks = entry
        source_table = (pairs_uv[:, 0:1] == tile_ids[None, :]).astype(jnp.bfloat16)
        target_table = (pairs_uv[:, 1:2] == tile_ids[None, :]).astype(jnp.float32)
        picked = jnp.einsum(
            "jt,ptc->jpc", source_table, amps_tiled, preferred_element_type=jnp.float32
        ).astype(jnp.bfloat16)
        product = jnp.einsum("jpc,jcd->jpd", picked, blocks, preferred_element_type=jnp.float32)
        partial_value = partial_value + jnp.einsum(
            "jv,jpd->vpd", target_table, product, precision=lax.Precision.HIGHEST
        )
        return (partial_value, None)

    start_sum = jnp.zeros((tiles_all, rows_here, tile_size), jnp.float32)
    partial_value, _ = lax.scan(ladder_step, start_sum, (tile_groups, int_groups))
    summed = lax.psum(partial_value, "ints")
    owned = lax.dynamic_slice_in_dim(summed, lax.axis_index("ints") * tiles_here, tiles_here, 0)
    ladder = owned.transpose(1, 0, 2).reshape(rows_here, tiles_here * tile_size)
    cycle_term = jnp.dot(
        cycle_w,
        lax.all_gather(amps, "pair", axis=0, tiled=True),
        preferred_element_type=jnp.float32,
    )
    keep_mask = jnp.repeat(res_live[0], tile_size).astype(jnp.float32)[None, :]
    return keep_mask * (ladder + cycle_term)


def solution(mesh):
    placed = (
        P("pair", "ints"),
        P("pair", "ints"),
        P("ints", None),
        P("ints", None, None),
        P("pair", None),
        P("pair", "ints"),
    )
    return jax.shard_map(
        local, mesh=mesh, in_specs=placed, out_specs=P("pair", "ints"), check_vma=False
    )
```

profile of v0, /device:TPU:0, one launch (start us, length us, event | category | flops | bytes accessed | tf_op | source)
XLA Modules:
  0.0 551.2 jit_solution(12331240370962497261)
XLA Ops:
  8.1 1.9 broadcast_multiply_fusion
  10.1 0.8 reshape.30
  10.8 80.5 %all-gather.3.cloned.1.call-done = bf16[512,8192]{1,0:T(8,128)(2,1)} async-done(((bf16[512,512]{1,0:T(8,128)(2,1)}), bf16[512,8192]{1,0:T(8,128)(2,1)}) %all-gather.3.cloned.1.call-update) | async-done | bytes 8388624 | tf_op jit(solution)/shard_map/all_gather | solution.py:15
  91.3 9.3 %copy.15 = bf16[64,8,64,128]{3,2,1,0:T(8,128)(2,1)} copy(bf16[64,8,64,128]{3,1,2,0:T(8,128)(2,1)} %bitcast.55) | data formatting | bytes 16777216
  100.6 213.6 %while.12 = (s32[]{:T(128)}, f32[64,512,128]{2,0,1:T(8,128)}, s32[5,64,2]{1,0,2:T(8,128)S(1)}, bf16[512,64,128]{2,1,0:T(8,128)(2,1)}, bf16[5,64,128,128]{3,2,1,0:T(8,128)(2,1)}, /*index=5*/s32[]{:T(128)}, s32[]{:T(128)}) while((s32[]{:T(128)}, f32[64,512,128]{2,0,1:T(8,128)}, s32[5,64,2]{1,0,2:T(8,128)S(1)}, ...), condition=%wide.region_1.2_spmd.clone.clone, body=%wide.region_0.1_spmd.clone.clone.sunk | while | flops 4840235008 | bytes 94374496 | solution.py:38
  100.6 5.8 %fusion.34 = bf16[64,512,128]{2,0,1:T(8,128)(2,1)S(1)} fusion(bf16[512,64,128]{2,1,0:T(8,128)(2,1)} %get-tuple-element.146, s32[64]{0:T(128)S(1)} %get-tuple-element.127), kind=kOutput, calls=%fused_computation.12.clone.1 | convolution fusion | flops 536875008 | bytes 16777472 | tf_op jit(solution)/shard_map/while/body/eval_jaxpr/jt,ptc->jpc/dot_general | solution.py:28
  106.4 13.9 %fusion.35 = f32[64,512,128]{2,1,0:T(8,128)} fusion(bf16[64,512,128]{2,0,1:T(8,128)(2,1)S(1)} %fusion.34, bf16[5,64,128,128]{3,2,1,0:T(8,128)(2,1)} %get-tuple-element.147, s32[]{:T(128)S(6)} %copy.28), kind=kOutput, calls=%fused_computation.5.clone.1 | convolution fusion | flops 1073741824 | bytes 27262980 | tf_op jit(solution)/shard_map/while/body/eval_jaxpr/jpc,jcd->jpd/dot_general | solution.py:31
  120.3 20.4 %select_add_fusion.2 = f32[64,512,128]{2,0,1:T(8,128)} fusion(f32[64,512,128]{2,0,1:T(8,128)} %get-tuple-element.137, f32[64,512,128]{2,1,0:T(8,128)} %fusion.35, pred[]{:T(512)S(6)} %compare.3, s32[64]{0:T(128)S(1)} %get-tuple-element.128), kind=kOutput, calls=%fused_computation.4.clone.1 | convolution fusion | flops 3229618176 | bytes 50331904 | tf_op jit(solution)/shard_map/while/body/eval_jaxpr/jv,jpd->vpd/dot_general | solution.py:32
  140.8 5.8 %fusion.34 = bf16[64,512,128]{2,0,1:T(8,128)(2,1)S(1)} fusion(bf16[512,64,128]{2,1,0:T(8,128)(2,1)} %get-tuple-element.146, s32[64]{0:T(128)S(1)} %get-tuple-element.127), kind=kOutput, calls=%fused_computation.12.clone.1 | convolution fusion | flops 536875008 | bytes 16777472 | tf_op jit(solution)/shard_map/while/body/eval_jaxpr/jt,ptc->jpc/dot_general | solution.py:28
  146.5 13.9 %fusion.35 = f32[64,512,128]{2,1,0:T(8,128)} fusion(bf16[64,512,128]{2,0,1:T(8,128)(2,1)S(1)} %fusion.34, bf16[5,64,128,128]{3,2,1,0:T(8,128)(2,1)} %get-tuple-element.147, s32[]{:T(128)S(6)} %copy.28), kind=kOutput, calls=%fused_computation.5.clone.1 | convolution fusion | flops 1073741824 | bytes 27262980 | tf_op jit(solution)/shard_map/while/body/eval_jaxpr/jpc,jcd->jpd/dot_general | solution.py:31
  160.5 23.7 %select_add_fusion.2 = f32[64,512,128]{2,0,1:T(8,128)} fusion(f32[64,512,128]{2,0,1:T(8,128)} %get-tuple-element.137, f32[64,512,128]{2,1,0:T(8,128)} %fusion.35, pred[]{:T(512)S(6)} %compare.3, s32[64]{0:T(128)S(1)} %get-tuple-element.128), kind=kOutput, calls=%fused_computation.4.clone.1 | convolution fusion | flops 3229618176 | bytes 50331904 | tf_op jit(solution)/shard_map/while/body/eval_jaxpr/jv,jpd->vpd/dot_general | solution.py:32
  184.1 5.8 %fusion.34 = bf16[64,512,128]{2,0,1:T(8,128)(2,1)S(1)} fusion(bf16[512,64,128]{2,1,0:T(8,128)(2,1)} %get-tuple-element.146, s32[64]{0:T(128)S(1)} %get-tuple-element.127), kind=kOutput, calls=%fused_computation.12.clone.1 | convolution fusion | flops 536875008 | bytes 16777472 | tf_op jit(solution)/shard_map/while/body/eval_jaxpr/jt,ptc->jpc/dot_general | solution.py:28
  189.9 13.9 %fusion.35 = f32[64,512,128]{2,1,0:T(8,128)} fusion(bf16[64,512,128]{2,0,1:T(8,128)(2,1)S(1)} %fusion.34, bf16[5,64,128,128]{3,2,1,0:T(8,128)(2,1)} %get-tuple-element.147, s32[]{:T(128)S(6)} %copy.28), kind=kOutput, calls=%fused_computation.5.clone.1 | convolution fusion | flops 1073741824 | bytes 27262980 | tf_op jit(solution)/shard_map/while/body/eval_jaxpr/jpc,jcd->jpd/dot_general | solution.py:31
  203.8 23.7 %select_add_fusion.2 = f32[64,512,128]{2,0,1:T(8,128)} fusion(f32[64,512,128]{2,0,1:T(8,128)} %get-tuple-element.137, f32[64,512,128]{2,1,0:T(8,128)} %fusion.35, pred[]{:T(512)S(6)} %compare.3, s32[64]{0:T(128)S(1)} %get-tuple-element.128), kind=kOutput, calls=%fused_computation.4.clone.1 | convolution fusion | flops 3229618176 | bytes 50331904 | tf_op jit(solution)/shard_map/while/body/eval_jaxpr/jv,jpd->vpd/dot_general | solution.py:32
  227.5 5.8 %fusion.34 = bf16[64,512,128]{2,0,1:T(8,128)(2,1)S(1)} fusion(bf16[512,64,128]{2,1,0:T(8,128)(2,1)} %get-tuple-element.146, s32[64]{0:T(128)S(1)} %get-tuple-element.127), kind=kOutput, calls=%fused_computation.12.clone.1 | convolution fusion | flops 536875008 | bytes 16777472 | tf_op jit(solution)/shard_map/while/body/eval_jaxpr/jt,ptc->jpc/dot_general | solution.py:28
  233.3 13.9 %fusion.35 = f32[64,512,128]{2,1,0:T(8,128)} fusion(bf16[64,512,128]{2,0,1:T(8,128)(2,1)S(1)} %fusion.34, bf16[5,64,128,128]{3,2,1,0:T(8,128)(2,1)} %get-tuple-element.147, s32[]{:T(128)S(6)} %copy.28), kind=kOutput, calls=%fused_computation.5.clone.1 | convolution fusion | flops 1073741824 | bytes 27262980 | tf_op jit(solution)/shard_map/while/body/eval_jaxpr/jpc,jcd->jpd/dot_general | solution.py:31
  247.2 23.7 %select_add_fusion.2 = f32[64,512,128]{2,0,1:T(8,128)} fusion(f32[64,512,128]{2,0,1:T(8,128)} %get-tuple-element.137, f32[64,512,128]{2,1,0:T(8,128)} %fusion.35, pred[]{:T(512)S(6)} %compare.3, s32[64]{0:T(128)S(1)} %get-tuple-element.128), kind=kOutput, calls=%fused_computation.4.clone.1 | convolution fusion | flops 3229618176 | bytes 50331904 | tf_op jit(solution)/shard_map/while/body/eval_jaxpr/jv,jpd->vpd/dot_general | solution.py:32
  270.9 5.8 %fusion.34 = bf16[64,512,128]{2,0,1:T(8,128)(2,1)S(1)} fusion(bf16[512,64,128]{2,1,0:T(8,128)(2,1)} %get-tuple-element.146, s32[64]{0:T(128)S(1)} %get-tuple-element.127), kind=kOutput, calls=%fused_computation.12.clone.1 | convolution fusion | flops 536875008 | bytes 16777472 | tf_op jit(solution)/shard_map/while/body/eval_jaxpr/jt,ptc->jpc/dot_general | solution.py:28
  276.6 13.9 %fusion.35 = f32[64,512,128]{2,1,0:T(8,128)} fusion(bf16[64,512,128]{2,0,1:T(8,128)(2,1)S(1)} %fusion.34, bf16[5,64,128,128]{3,2,1,0:T(8,128)(2,1)} %get-tuple-element.147, s32[]{:T(128)S(6)} %copy.28), kind=kOutput, calls=%fused_computation.5.clone.1 | convolution fusion | flops 1073741824 | bytes 27262980 | tf_op jit(solution)/shard_map/while/body/eval_jaxpr/jpc,jcd->jpd/dot_general | solution.py:31
  290.6 23.7 %select_add_fusion.2 = f32[64,512,128]{2,0,1:T(8,128)} fusion(f32[64,512,128]{2,0,1:T(8,128)} %get-tuple-element.137, f32[64,512,128]{2,1,0:T(8,128)} %fusion.35, pred[]{:T(512)S(6)} %compare.3, s32[64]{0:T(128)S(1)} %get-tuple-element.128), kind=kOutput, calls=%fused_computation.4.clone.1 | convolution fusion | flops 3229618176 | bytes 50331904 | tf_op jit(solution)/shard_map/while/body/eval_jaxpr/jv,jpd->vpd/dot_general | solution.py:32
  315.0 219.5 %all-reduce.2.cloned.1.call-done = f32[64,512,128]{2,0,1:T(8,128)} async-done(((f32[64,512,128]{2,0,1:T(8,128)}), f32[64,512,128]{2,0,1:T(8,128)}) %all-reduce.2.cloned.1.call-update) | async-done | bytes 16777232 | tf_op jit(solution)/shard_map/psum | solution.py:39
  534.5 1.8 dynamic-slice_bitcast_fusion
  536.6 5.8 %fusion.18 = f32[512,512]{0,1:T(8,128)S(1)} fusion(f32[512,512]{0,1:T(8,128)S(1)} %bitcast.56, bf16[4096,512]{1,0:T(8,128)(2,1)} %all-gather.5.cloned.1.call-done, bf16[512,4096]{1,0:T(8,128)(2,1)} %param.12, f32[512]{0:T(512)S(1)} %broadcast_bitcast_fusion), kind=kOutput, calls=%fused_computation.21 | convolution fusion | flops 2148007936 | bytes 10487808 | tf_op jit(solution)/shard_map/dot_general | solution.py:42
  542.5 1.3 copy.11
  (25 shorter events, 1.9 us)
Async XLA Ops:
  7.4 84.0 %all-gather.3.cloned.1.call-start = ((), (), s32[]{:S(2)}) async-start(), calls=%async_computation | async-start | bytes 8912896 | tf_op jit(solution)/shard_map/all_gather | solution.py:15
  10.0 524.5 %all-reduce.2.cloned.1.call-start = ((), (), s32[]{:S(2)}) async-start(), calls=%async_computation.1 | async-start | bytes 33554432 | tf_op jit(solution)/shard_map/psum | solution.py:39
  314.2 0.7 copy-start
  314.2 222.4 %all-gather.5.cloned.1.call-start = ((), (), s32[]{:S(2)}) async-start(), calls=%async_computation.2 | async-start | bytes 4718592 | tf_op jit(solution)/shard_map/all_gather | solution.py:44
Sparse Core Ops, SparseCore 0:
  10.3 80.9 all-gather.2
  314.4 220.0 all-reduce.1
Sparse Core Ops, SparseCore 1:
  316.4 31.1 all-gather.4
where the time goes:
time: 552 us; the launch traced here: 551 us
  waiting for transfers between devices  300 us (54%)
  matrix products  219 us (40%)
  between operations  14.9 us (3%)
  local copies, waits for them, and re-layouts  13.7 us (2%)
    psum x1, waiting for transfers between devices, local(): summed = lax.psum(partial_value, 'ints')  220 us
    dot_general x5, matrix products, ladder_step(): jnp.einsum('jv,jpd->vpd', target_table, product, precision=lax.Precision....  115 us
    all_gather x1, waiting for transfers between devices, local(): block_amps = lax.all_gather(amps, 'ints', axis=1, tiled=True)  80.5 us
    dot_general x5, matrix products, ladder_step(): jnp.einsum('jpc,jcd->jpd', picked, blocks, preferred_element_type=jnp.flo...  69.7 us
    dot_general x5, matrix products, ladder_step(): jnp.einsum('jt,ptc->jpc', source_table, amps_tiled, preferred_element_typ...  28.8 us
  transfers between devices with their start and end apart: 3, of which 2 were waited for; matrix products, arithmetic and copies ran while one was open for 1% of the time, Pallas kernels for 0%

commit v1 on v0

v1 whole, which is shorter than its diff:
```python
import jax
import jax.numpy as jnp
import numpy as np
from jax import lax
from jax.experimental import pallas as pl
from jax.experimental.pallas import tpu as pltpu
from jax.sharding import PartitionSpec as P

ROWS = 512
TILE = 128
TILES = 64
SIDE = 4
PAD = 16
ENTRIES = 224
UNROLL = 8
HALF_RANGE = 14.9
VMEM_LIMIT = 58 * 1024 * 1024
NEAR = {0: 0, 1: 1, 3: 2, 2: 3}

VMEM_SPEC = pl.BlockSpec(memory_space=pltpu.VMEM)
SMEM_SPEC = pl.BlockSpec(memory_space=pltpu.SMEM)


def source_table():
    table = np.zeros((SIDE, SIDE, 4), np.int32)
    for dy in range(SIDE):
        for dz in range(SIDE):
            for t in range(2):
                table[dy, dz, t] = NEAR[dy] * 8 + NEAR[dz] * 2 + t
                table[dy, dz, t + 2] = 32 + NEAR[dz] * 8 + NEAR[dy] * 2 + t
    return table.reshape(-1)


def target_table():
    table = np.zeros((SIDE, SIDE, 4), np.int32)
    for far in range(SIDE):
        for other in range(SIDE):
            for t in range(2):
                if far == 2:
                    place = 0 if t == 0 else 8
                elif far == 1:
                    place = 32 if t == 0 else 4
                elif far == 3:
                    place = 12 if t == 0 else 36
                else:
                    place = 40 if t == 0 else 44
                sent = place < 16
                table[other, far, t] = place + other
                table[far, other, t + 2] = place + other + 16
    return table.reshape(-1)


def pick(table, index):
    spread = jnp.arange(TILES, dtype=jnp.int32)
    return jnp.sum(jnp.where(index[:, None] == spread[None, :], jnp.asarray(table)[None, :], 0), axis=1)


def relative(tile, y, z):
    device = tile >> 2
    dy = ((device >> 2) - y) & 3
    dz = ((device & 3) - z) & 3
    return (dy * SIDE + dz) * 4 + (tile & 3)


def work_list(source, target):
    count = source.shape[0]
    order = jnp.arange(count, dtype=jnp.int32)
    ids = jnp.arange(TILES, dtype=jnp.int32)
    same = target[:, None] == ids[None, :]
    held = jnp.sum(same, axis=0, dtype=jnp.int32)
    before = jnp.sum((target[None, :] == target[:, None]) & (order[None, :] < order[:, None]), axis=1, dtype=jnp.int32)
    entries = jnp.maximum((held + 1) // 2, 1)
    start = jnp.sum(jnp.where(ids[None, :] < ids[:, None], entries[None, :], 0), axis=1)
    mine = jnp.sum(jnp.where(same, start[None, :], 0), axis=1)
    slot = (mine + before // 2) * 2 + before % 2
    value = source + (order << 6) + (1 << 15)
    slots = jnp.arange(2 * ENTRIES, dtype=jnp.int32)
    tiles = jnp.sum(jnp.where(slot[:, None] == slots[None, :], value[:, None], 0), axis=0)
    at = jnp.arange(ENTRIES, dtype=jnp.int32)
    owner = jnp.sum(start[None, :] <= at[:, None], axis=1, dtype=jnp.int32) - 1
    fresh = jnp.sum(start[None, :] == at[:, None], axis=1, dtype=jnp.int32)
    bounds = jnp.concatenate([start, jnp.sum(entries)[None]])
    return tiles, owner * 2 + fresh, bounds


def encode(value):
    top = jnp.max(jnp.abs(value), axis=0, keepdims=True)
    power = jnp.floor(jnp.log2(jnp.maximum(top, 2.0**-100))) + 1.0
    whole = jnp.round(value * jnp.exp2(HALF_RANGE - power)).astype(jnp.int32).astype(jnp.int16)
    return whole, jnp.broadcast_to(power, (PAD, TILE)).astype(jnp.int32).astype(jnp.int16)


def put(ref, k, value):
    whole, power = encode(value)
    ref[k, 0:ROWS, :] = whole
    ref[k, ROWS : ROWS + PAD, :] = power


def get(ref, k):
    power = ref[k, ROWS : ROWS + PAD, :].astype(jnp.int32).astype(jnp.float32)[0:1, :]
    return ref[k, 0:ROWS, :].astype(jnp.int32).astype(jnp.float32) * jnp.exp2(power - HALF_RANGE)


def coded(n):
    return jax.ShapeDtypeStruct((n, ROWS + PAD, TILE), jnp.int16)


def plain(n):
    return jax.ShapeDtypeStruct((n, ROWS, TILE), jnp.float32)


def kernel(body, outs, specs, scratch=(), name=None):
    return pl.pallas_call(
        body,
        out_shape=outs,
        in_specs=specs,
        out_specs=jax.tree.map(lambda _: VMEM_SPEC, outs),
        scratch_shapes=list(scratch),
        compiler_params=pltpu.CompilerParams(vmem_limit_bytes=VMEM_LIMIT),
        name=name,
    )


def ladder(tiles, owner, bounds, amps, integrals, first, count, send):
    def body(tiles_ref, owner_ref, bounds_ref, amps_ref, ints_ref, *rest):
        sums = rest[-1] if send else rest[0]
        begin = bounds_ref[first]
        end = bounds_ref[first + count]

        def step(i, carry):
            for k in range(UNROLL):
                at = begin + i * UNROLL + k
                inside = at < end
                at = jnp.minimum(at, ENTRIES - 1)
                left = tiles_ref[2 * at]
                right = tiles_ref[2 * at + 1]
                mark = owner_ref[at]
                place = jnp.where(inside, (mark >> 1) - first, count - 1)
                fresh = jnp.logical_and(inside, (mark & 1) == 1)
                keep_left = jnp.where(inside, left >> 15, 0).astype(jnp.float32).astype(jnp.bfloat16)
                keep_right = jnp.where(inside, right >> 15, 0).astype(jnp.float32).astype(jnp.bfloat16)
                weights = jnp.concatenate(
                    [ints_ref[(left >> 6) & 511] * keep_left, ints_ref[(right >> 6) & 511] * keep_right], axis=0
                )
                values = jnp.concatenate([amps_ref[left & 63], amps_ref[right & 63]], axis=1)
                product = jnp.dot(values, weights, preferred_element_type=jnp.float32)
                sums[place] = product + jnp.where(fresh, 0.0, sums[place])
            return carry

        lax.fori_loop(0, (end - begin + UNROLL - 1) // UNROLL, step, 0)
        if send:
            half = count // 2

            def code(k, carry):
                put(rest[0], k, sums[k])
                put(rest[1], k, sums[k + half])
                return carry

            lax.fori_loop(0, half, code, 0)

    outs = (coded(count // 2), coded(count // 2)) if send else (plain(count),)
    scratch = [pltpu.VMEM((count, ROWS, TILE), jnp.float32)] if send else []
    specs = [SMEM_SPEC] * 3 + [VMEM_SPEC] * 2
    return kernel(body, outs, specs, scratch)(tiles, owner, bounds, amps, integrals)


def merge(sums, got_up, got_down, base):
    def body(sums_ref, up_ref, down_ref, up_out, down_out):
        def step(k, carry):
            put(up_out, k, sums_ref[base + k] + get(up_ref, k))
            put(down_out, k, sums_ref[base + 4 + k] + get(down_ref, k))
            return carry

        lax.fori_loop(0, 4, step, 0)

    return kernel(body, (coded(4), coded(4)), [VMEM_SPEC] * 3)(sums, got_up, got_down)


def row_sum(sums, got_up, got_down, last_up, last_down, base):
    def body(sums_ref, up_ref, down_ref, last_up_ref, last_down_ref, up_out, down_out, kept):
        def low(k):
            return sums_ref[base + 8 + k] + get(down_ref, 4 + k) + get(last_up_ref, k)

        def high(k):
            return sums_ref[base + 12 + k] + get(up_ref, 4 + k) + get(last_down_ref, k)

        put(up_out, 0, low(2))
        put(up_out, 1, high(1))
        put(down_out, 0, high(2))
        put(down_out, 1, low(3))
        kept[0] = low(1)
        kept[1] = high(3)
        kept[2] = low(0)
        kept[3] = high(0)

    return kernel(body, (coded(2), coded(2), plain(4)), [VMEM_SPEC] * 5)(sums, got_up, got_down, last_up, last_down)


def merge_last(kept, got_up, got_down):
    def body(kept_ref, up_ref, down_ref, up_out, down_out):
        put(up_out, 0, kept_ref[0] + get(up_ref, 0))
        put(down_out, 0, kept_ref[1] + get(down_ref, 0))

    return kernel(body, (coded(1), coded(1)), [VMEM_SPEC] * 3)(kept, got_up, got_down)


def finish(res_live, cycle, half_a, half_b):
    def body(live_ref, cycle_ref, *refs):
        out_ref = refs[-1]
        for h in range(2):
            kept, up, down, last_up, last_down = refs[5 * h : 5 * h + 5]
            low = kept[2] + get(down, 1) + get(last_up, 0)
            high = kept[3] + get(up, 1) + get(last_down, 0)
            for t, value in ((2 * h, low), (2 * h + 1, high)):
                cols = slice(t * TILE, (t + 1) * TILE)
                keep = live_ref[0, t].astype(jnp.float32)
                out_ref[:, cols] = keep * (value + cycle_ref[:, cols])

    out = jax.ShapeDtypeStruct((ROWS, 4 * TILE), jnp.float32)
    return kernel(body, out, [SMEM_SPEC] + [VMEM_SPEC] * 11)(res_live, cycle, *half_a, *half_b)


def local(t2, t2_live, int_tiles, integrals, cycle_w, res_live):
    place = lax.axis_index("ints").astype(jnp.int32)
    y, z = place >> 2, place & 3

    def take(value, dy, dz):
        pairs = [
            (((i + dy) % SIDE) * SIDE + (k + dz) % SIDE, i * SIDE + k) for i in range(SIDE) for k in range(SIDE)
        ]
        return lax.ppermute(value, "ints", pairs)

    def along_z(value, d):
        return take(value, 0, d)

    def along_y(value, d):
        return take(value, d, 0)

    mask = jnp.repeat(t2_live[0].astype(t2.dtype), TILE)
    flat = t2 * mask[None, :]
    own = flat.reshape(ROWS, 4, TILE).transpose(1, 0, 2)

    def gather(value, near_axis, far_axis):
        n = value.shape[0] // 2
        up, down = near_axis(value, 1), near_axis(value, 3)
        over = near_axis(up[:n], 1), near_axis(down[n:], 3)
        row = jnp.concatenate([value, up, down, *over], axis=0)
        n = row.shape[0] // 2
        up, down = far_axis(row, 1), far_axis(row, 3)
        over = far_axis(up[:n], 1), far_axis(down[n:], 3)
        return [row, up, down, *over]

    pieces_a = gather(own[:2], along_z, along_y)
    pieces_b = gather(own[2:], along_y, along_z)
    amps = jnp.concatenate(pieces_a + pieces_b, axis=0)

    source = pick(source_table(), relative(int_tiles[:, 0], y, z))
    target = pick(target_table(), relative(int_tiles[:, 1], y, z))
    tiles, owner, bounds = work_list(source, target)

    send_a = ladder(tiles, owner, bounds, amps, integrals, 0, 16, True)
    send_b = ladder(tiles, owner, bounds, amps, integrals, 16, 16, True)

    def first_hop(send, axis):
        return axis(send[0], 3), axis(send[1], 1)

    got_a = first_hop(send_a, along_z)
    got_b = first_hop(send_b, along_y)
    (sums,) = ladder(tiles, owner, bounds, amps, integrals, 32, 32, False)

    cycle = jnp.dot(
        cycle_w, lax.all_gather(flat, "pair", axis=0, tiled=True), preferred_element_type=jnp.float32
    )

    def reduce(got, axis, other, base):
        on = merge(sums, *got, base)
        last = first_hop(on, axis)
        up, down, kept = row_sum(sums, *got, *last, base)
        got = first_hop((up, down), other)
        last = first_hop(merge_last(kept, *got), other)
        return (kept, *got, *last)

    half_a = reduce(got_a, along_z, along_y, 0)
    half_b = reduce(got_b, along_y, along_z, 16)
    return finish(res_live, cycle, half_a, half_b)


def solution(mesh):
    placed = (
        P("pair", "ints"),
        P("pair", "ints"),
        P("ints", None),
        P("ints", None, None),
        P("pair", None),
        P("pair", "ints"),
    )
    return jax.shard_map(local, mesh=mesh, in_specs=placed, out_specs=P("pair", "ints"), check_vma=False)
```

time: 552 us -> 244 us (0.44)
  waiting for transfers between devices: 300 us -> 62.7 us
  matrix products: 219 us -> 6.84 us
  Pallas kernels: 0 us -> 76.1 us
  starting transfers between devices: 0.27 us -> 51.9 us
  local copies, waits for them, and re-layouts: 13.7 us -> 27.3 us
    psum x1 -> x0, waiting for transfers between devices: 220 us -> none  [local(): summed = lax.psum(partial_value, 'ints')]
    dot_general x16 -> x1, matrix products: 219 us -> 6.84 us  [local(): jnp.dot(cycle_w, lax.all_gather(flat, 'pair', axis=0, tiled=True), prefer...]
    all_gather x2 -> x1, waiting for transfers between devices: 80.5 us -> 0.01 us  [local(): lax.all_gather(flat, 'pair', axis=0, tiled=True)]
    pallas_call x0 -> x10, Pallas kernels: none -> 76.1 us  [the longest x3 44.8 us: ladder(): kernel(body, outs, specs, scratch)(tiles, owner, bounds, amps, integrals)]
    ppermute x0 -> x32, waiting for transfers between devices: none -> 62.7 us  [take(): return lax.ppermute(value, 'ints', pairs)]
    ppermute x0 -> x32, starting transfers between devices: none -> 51.9 us  [take(): return lax.ppermute(value, 'ints', pairs)]
    unnamed x3 -> x58, local copies, waits for them, and re-layouts: 9.33 us -> 24.5 us
  transfers between devices with their start and end apart: 3 -> 33, of which waited for: 2 -> 10; matrix products, arithmetic and copies ran while one was open for 1% -> 10% of each run, Pallas kernels for 0% -> 30%
where the time goes in v1:
time: 244 us; the launch traced here: 243 us
  Pallas kernels  76.1 us (31%)
  waiting for transfers between devices  62.7 us (26%)
  starting transfers between devices  51.9 us (21%)
  local copies, waits for them, and re-layouts  27.3 us (11%)
  between operations  13.6 us (6%)
  matrix products  6.84 us (3%)
  other arithmetic  4.7 us (2%)
    ppermute x32, waiting for transfers between devices, take(): return lax.ppermute(value, 'ints', pairs)  62.7 us
    ppermute x32, starting transfers between devices, take(): return lax.ppermute(value, 'ints', pairs)  51.9 us
    pallas_call x3, Pallas kernels, ladder(): kernel(body, outs, specs, scratch)(tiles, owner, bounds, amps, integrals)  44.8 us
    unnamed x58, local copies, waits for them, and re-layouts  24.5 us
    pallas_call x2, Pallas kernels, row_sum(): kernel(body, (coded(2), coded(2), plain(4)), [VMEM_SPEC] * 5)  12.1 us
    pallas_call x2, Pallas kernels, merge(): kernel(body, (coded(4), coded(4)), [VMEM_SPEC] * 3)(sums, got_up, got_down)  11.2 us
    dot_general x1, matrix products, local(): jnp.dot(cycle_w, lax.all_gather(flat, 'pair', axis=0, tiled=True), prefer...  6.84 us
  transfers between devices with their start and end apart: 33, of which 10 were waited for; matrix products, arithmetic and copies ran while one was open for 10% of the time, Pallas kernels for 30%

profile of v1, /device:TPU:0, one launch (start us, length us, event | category | flops | bytes accessed | tf_op | source)
XLA Modules:
  0.0 243.2 jit_solution(6301764606657527871)
XLA Ops:
  10.0 4.1 %collective-permute-start = (bf16[2,512,128]{2,1,0:T(8,128)(2,1)S(1)}, bf16[2,512,128]{2,1,0:T(8,128)(2,1)S(1)}, u32[]{:S(2)}, u32[]{:S(2)}) collective-permute-start(bf16[2,512,128]{2,1,0:T(8,128)(2,1)S(1)} %get-tuple-element.51), channel_id=1, source_target_pairs={{1,0},{2,1},{3,2},{0,3},{5,4},{6,5},{7,6},{4,7},{9,8},{10,9},{11,1... | collective-permute-start | bytes 786440 | tf_op jit(solution)/shard_map/ppermute | solution.py:231
  14.2 5.5 %collective-permute-done = bf16[2,512,128]{2,1,0:T(8,128)(2,1)S(1)} collective-permute-done((bf16[2,512,128]{2,1,0:T(8,128)(2,1)S(1)}, bf16[2,512,128]{2,1,0:T(8,128)(2,1)S(1)}, u32[]{:S(2)}, u32[]{:S(2)}) %collective-permute-start) | collective-permute-done | bytes 262176 | tf_op jit(solution)/shard_map/ppermute | solution.py:231
  19.7 3.8 %collective-permute-start.2 = (bf16[1,512,128]{2,1,0:T(8,128)(2,1)S(1)}, bf16[1,512,128]{2,1,0:T(8,128)(2,1)S(1)}, u32[]{:S(2)}, u32[]{:S(2)}) collective-permute-start(bf16[1,512,128]{2,1,0:T(8,128)(2,1)S(1)} %slice.49), channel_id=1, source_target_pairs={{1,0},{2,1},{3,2},{0,3},{5,4},{6,5},{7,6},{4,7},{9,8},{10,9},{11,1... | collective-permute-start | bytes 393224 | tf_op jit(solution)/shard_map/ppermute | solution.py:231
  33.5 3.2 %collective-permute-start.8 = (bf16[2,512,128]{2,1,0:T(8,128)(2,1)S(1)}, bf16[2,512,128]{2,1,0:T(8,128)(2,1)S(1)}, u32[]{:S(2)}, u32[]{:S(2)}) collective-permute-start(bf16[2,512,128]{2,1,0:T(8,128)(2,1)S(1)} %get-tuple-element.50), channel_id=1, source_target_pairs={{4,0},{5,1},{6,2},{7,3},{8,4},{9,5},{10,6},{11,7},{12,8},{13,9},{1... | collective-permute-start | bytes 786440 | tf_op jit(solution)/shard_map/ppermute | solution.py:231
  36.7 20.7 %collective-permute-done.4 = bf16[8,512,128]{2,1,0:T(8,128)(2,1)S(1)} collective-permute-done((bf16[8,512,128]{2,1,0:T(8,128)(2,1)}, bf16[8,512,128]{2,1,0:T(8,128)(2,1)S(1)}, u32[]{:S(2)}, u32[]{:S(2)}) %collective-permute-start.4) | collective-permute-done | bytes 1048608 | tf_op jit(solution)/shard_map/ppermute | solution.py:231
  57.4 3.7 %collective-permute-start.6 = (bf16[4,512,128]{2,1,0:T(8,128)(2,1)S(1)}, bf16[4,512,128]{2,1,0:T(8,128)(2,1)S(1)}, u32[]{:S(2)}, u32[]{:S(2)}) collective-permute-start(bf16[4,512,128]{2,1,0:T(8,128)(2,1)S(1)} %slice.51), channel_id=1, source_target_pairs={{4,0},{5,1},{6,2},{7,3},{8,4},{9,5},{10,6},{11,7},{12,8},{13,9},{1... | collective-permute-start | bytes 1572872 | tf_op jit(solution)/shard_map/ppermute | solution.py:231
  62.9 3.8 %collective-permute-start.10 = (bf16[1,512,128]{2,1,0:T(8,128)(2,1)S(1)}, bf16[1,512,128]{2,1,0:T(8,128)(2,1)S(1)}, u32[]{:S(2)}, u32[]{:S(2)}) collective-permute-start(bf16[1,512,128]{2,1,0:T(8,128)(2,1)S(1)} %slice.54), channel_id=1, source_target_pairs={{4,0},{5,1},{6,2},{7,3},{8,4},{9,5},{10,6},{11,7},{12,8},{13,9},{1... | collective-permute-start | bytes 393224 | tf_op jit(solution)/shard_map/ppermute | solution.py:231
  83.2 19.9 %collective-permute-done.12 = bf16[8,512,128]{2,1,0:T(8,128)(2,1)S(1)} collective-permute-done((bf16[8,512,128]{2,1,0:T(8,128)(2,1)S(1)}, bf16[8,512,128]{2,1,0:T(8,128)(2,1)S(1)}, u32[]{:S(2)}, u32[]{:S(2)}) %collective-permute-start.12) | collective-permute-done | bytes 1048608 | tf_op jit(solution)/shard_map/ppermute | solution.py:231
  117.3 14.0 %shard_map.87 = (s16[8,528,128]{2,1,0:T(8,128)(2,1)}, s16[8,528,128]{2,1,0:T(8,128)(2,1)}) custom-call(s32[448]{0:T(512)} %select_reduce_fusion.tiles_ref, s32[224]{0:T(256)} %multiply_add_fusion.owner_ref, s32[65]{0:T(128)} %pad_add_fusion.bounds_ref, bf16[64,512,128]{2,1,0:T(8,128)(2,1)} %constant_dynamic-update-slice_fusion.10.amps_ref, ...), custom_call_target="tpu_custom_call" | custom-call | tf_op jit(solution)/shard_map/pallas_call | solution.py:164
  131.3 3.2 %collective-permute-start.25 = (s16[8,528,128]{2,1,0:T(8,128)(2,1)}, s16[8,528,128]{2,1,0:T(8,128)(2,1)S(1)}, u32[]{:S(2)}, u32[]{:S(2)}) collective-permute-start(s16[8,528,128]{2,1,0:T(8,128)(2,1)} %get-tuple-element.33), channel_id=1, source_target_pairs={{4,0},{5,1},{6,2},{7,3},{8,4},{9,5},{10,6},{11,7},{12,8},{13,9},{1... | collective-permute-start | bytes 3244040 | tf_op jit(solution)/shard_map/ppermute | solution.py:231
  134.5 13.3 %shard_map.83 = (s16[8,528,128]{2,1,0:T(8,128)(2,1)}, s16[8,528,128]{2,1,0:T(8,128)(2,1)}) custom-call(s32[448]{0:T(512)} %select_reduce_fusion.tiles_ref, s32[224]{0:T(256)} %multiply_add_fusion.owner_ref, s32[65]{0:T(128)} %pad_add_fusion.bounds_ref, bf16[64,512,128]{2,1,0:T(8,128)(2,1)} %constant_dynamic-update-slice_fusion.10.amps_ref, ...), custom_call_target="tpu_custom_call" | custom-call | tf_op jit(solution)/shard_map/pallas_call | solution.py:164
  147.8 3.2 %collective-permute-start.17 = (s16[8,528,128]{2,1,0:T(8,128)(2,1)}, s16[8,528,128]{2,1,0:T(8,128)(2,1)S(1)}, u32[]{:S(2)}, u32[]{:S(2)}) collective-permute-start(s16[8,528,128]{2,1,0:T(8,128)(2,1)} %get-tuple-element.24), channel_id=1, source_target_pairs={{1,0},{2,1},{3,2},{0,3},{5,4},{6,5},{7,6},{4,7},{9,8},{10,9},{11,1... | collective-permute-start | bytes 3244040 | tf_op jit(solution)/shard_map/ppermute | solution.py:231
  151.0 17.5 %shard_map.82.sums_ref = f32[32,512,128]{2,1,0:T(8,128)} custom-call(s32[448]{0:T(512)} %select_reduce_fusion.tiles_ref, s32[224]{0:T(256)} %multiply_add_fusion.owner_ref, s32[65]{0:T(128)} %pad_add_fusion.bounds_ref, bf16[64,512,128]{2,1,0:T(8,128)(2,1)} %constant_dynamic-update-slice_fusion.10.amps_ref, bf16[320,128,128]{2,1,0:T(8,128)(2,1)} %ints_ref.5), custom_call_target="tpu_custom_call" | custom-call | tf_op jit(solution)/shard_map/pallas_call | solution.py:164
  170.5 5.6 %shard_map.88 = (s16[4,528,128]{2,1,0:T(8,128)(2,1)}, s16[4,528,128]{2,1,0:T(8,128)(2,1)}) custom-call(f32[32,512,128]{2,1,0:T(8,128)} %shard_map.82.sums_ref, s16[8,528,128]{2,1,0:T(8,128)(2,1)} %copy-done.3, s16[8,528,128]{2,1,0:T(8,128)(2,1)} %copy-done.4), custom_call_target="tpu_custom_call" | custom-call | tf_op jit(solution)/shard_map/pallas_call | solution.py:176
  176.1 3.2 %collective-permute-start.27 = (s16[4,528,128]{2,1,0:T(8,128)(2,1)}, s16[4,528,128]{2,1,0:T(8,128)(2,1)S(1)}, u32[]{:S(2)}, u32[]{:S(2)}) collective-permute-start(s16[4,528,128]{2,1,0:T(8,128)(2,1)} %get-tuple-element.35), channel_id=1, source_target_pairs={{4,0},{5,1},{6,2},{7,3},{8,4},{9,5},{10,6},{11,7},{12,8},{13,9},{1... | collective-permute-start | bytes 1622024 | tf_op jit(solution)/shard_map/ppermute | solution.py:231
  181.4 5.6 %shard_map.84 = (s16[4,528,128]{2,1,0:T(8,128)(2,1)}, s16[4,528,128]{2,1,0:T(8,128)(2,1)}) custom-call(f32[32,512,128]{2,1,0:T(8,128)} %shard_map.82.sums_ref, s16[8,528,128]{2,1,0:T(8,128)(2,1)} %copy-done.1, s16[8,528,128]{2,1,0:T(8,128)(2,1)} %copy-done.2), custom_call_target="tpu_custom_call" | custom-call | tf_op jit(solution)/shard_map/pallas_call | solution.py:176
  191.8 6.1 %shard_map.89 = (s16[2,528,128]{2,1,0:T(8,128)(2,1)}, s16[2,528,128]{2,1,0:T(8,128)(2,1)}, f32[4,512,128]{2,1,0:T(8,128)}) custom-call(f32[32,512,128]{2,1,0:T(8,128)} %shard_map.82.sums_ref, s16[8,528,128]{2,1,0:T(8,128)(2,1)} %copy-done.3, s16[8,528,128]{2,1,0:T(8,128)(2,1)} %copy-done.4, s16[4,528,128]{2,1,0:T(8,128)(2,1)} %copy-done.11, ...), custom_call_target="tpu_custom_call" | custom-call | tf_op jit(solution)/shard_map/pallas_call | solution.py:196
  197.9 3.2 %collective-permute-start.29 = (s16[2,528,128]{2,1,0:T(8,128)(2,1)}, s16[2,528,128]{2,1,0:T(8,128)(2,1)S(1)}, u32[]{:S(2)}, u32[]{:S(2)}) collective-permute-start(s16[2,528,128]{2,1,0:T(8,128)(2,1)} %get-tuple-element.38), channel_id=1, source_target_pairs={{1,0},{2,1},{3,2},{0,3},{5,4},{6,5},{7,6},{4,7},{9,8},{10,9},{11,1... | collective-permute-start | bytes 811016 | tf_op jit(solution)/shard_map/ppermute | solution.py:231
  202.7 6.1 %shard_map.85 = (s16[2,528,128]{2,1,0:T(8,128)(2,1)}, s16[2,528,128]{2,1,0:T(8,128)(2,1)}, f32[4,512,128]{2,1,0:T(8,128)}) custom-call(f32[32,512,128]{2,1,0:T(8,128)} %shard_map.82.sums_ref, s16[8,528,128]{2,1,0:T(8,128)(2,1)} %copy-done.1, s16[8,528,128]{2,1,0:T(8,128)(2,1)} %copy-done.2, s16[4,528,128]{2,1,0:T(8,128)(2,1)} %copy-done.9, ...), custom_call_target="tpu_custom_call" | custom-call | tf_op jit(solution)/shard_map/pallas_call | solution.py:196
  208.8 3.2 %collective-permute-start.21 = (s16[2,528,128]{2,1,0:T(8,128)(2,1)}, s16[2,528,128]{2,1,0:T(8,128)(2,1)S(1)}, u32[]{:S(2)}, u32[]{:S(2)}) collective-permute-start(s16[2,528,128]{2,1,0:T(8,128)(2,1)} %get-tuple-element.29), channel_id=1, source_target_pairs={{4,0},{5,1},{6,2},{7,3},{8,4},{9,5},{10,6},{11,7},{12,8},{13,9},{1... | collective-permute-start | bytes 811016 | tf_op jit(solution)/shard_map/ppermute | solution.py:231
  215.0 3.2 %collective-permute-start.31 = (s16[1,528,128]{2,1,0:T(8,128)(2,1)}, s16[1,528,128]{2,1,0:T(8,128)(2,1)S(1)}, u32[]{:S(2)}, u32[]{:S(2)}) collective-permute-start(s16[1,528,128]{2,1,0:T(8,128)(2,1)} %get-tuple-element.40), channel_id=1, source_target_pairs={{1,0},{2,1},{3,2},{0,3},{5,4},{6,5},{7,6},{4,7},{9,8},{10,9},{11,1... | collective-permute-start | bytes 405512 | tf_op jit(solution)/shard_map/ppermute | solution.py:231
  221.2 3.2 %collective-permute-start.23 = (s16[1,528,128]{2,1,0:T(8,128)(2,1)}, s16[1,528,128]{2,1,0:T(8,128)(2,1)S(1)}, u32[]{:S(2)}, u32[]{:S(2)}) collective-permute-start(s16[1,528,128]{2,1,0:T(8,128)(2,1)} %get-tuple-element.31), channel_id=1, source_target_pairs={{4,0},{5,1},{6,2},{7,3},{8,4},{9,5},{10,6},{11,7},{12,8},{13,9},{1... | collective-permute-start | bytes 405512 | tf_op jit(solution)/shard_map/ppermute | solution.py:231
  224.4 6.8 %convolution_bitcast_fusion.cycle_ref = f32[512,512]{1,0:T(8,128)} fusion(bf16[4096,512]{0,1:T(8,128)(2,1)} %all-gather.2.cloned.1.call-done, bf16[512,4096]{1,0:T(8,128)(2,1)} %param.12), kind=kOutput, calls=%fused_computation | convolution fusion | flops 2147483648 | bytes 9437184 | tf_op jit(solution)/shard_map/dot_general | solution.py:271
  232.7 3.7 %shard_map.91 = f32[512,512]{1,0:T(8,128)} custom-call(s32[1,4]{1,0:T(1,128)} %live_ref.1, f32[512,512]{1,0:T(8,128)} %convolution_bitcast_fusion.cycle_ref, f32[4,512,128]{2,1,0:T(8,128)} %get-tuple-element.27.kept_ref.refs_0_, s16[2,528,128]{2,1,0:T(8,128)(2,1)} %copy-done.7, s16[2,528,128]{2,1,0:T(8,128)(2,1)} %copy-done.8, ...), custom_call_target="tpu_custom_call" | custom-call | tf_op jit(solution)/shard_map/pallas_call | solution.py:220
  (140 shorter events, 63.6 us)
Async XLA Ops:
  6.5 217.9 %all-gather.2.cloned.1.call-start = ((), (), s32[]{:S(2)}) async-start(), calls=%async_computation | async-start | bytes 4718592 | tf_op jit(solution)/shard_map/all_gather | solution.py:272
  30.4 26.9 %collective-permute-start.4 = (bf16[8,512,128]{2,1,0:T(8,128)(2,1)}, bf16[8,512,128]{2,1,0:T(8,128)(2,1)S(1)}, u32[]{:S(2)}, u32[]{:S(2)}) collective-permute-start(bf16[8,512,128]{2,1,0:T(8,128)(2,1)} %get-tuple-element.64), channel_id=1, source_target_pairs={{4,0},{5,1},{6,2},{7,3},{8,4},{9,5},{10,6},{11,7},{12,8},{13,9},{1... | collective-permute-start | bytes 3145736 | tf_op jit(solution)/shard_map/ppermute | solution.py:231
  33.5 27.7 %collective-permute-start.5 = (bf16[8,512,128]{2,1,0:T(8,128)(2,1)}, bf16[8,512,128]{2,1,0:T(8,128)(2,1)S(1)}, u32[]{:S(2)}, u32[]{:S(2)}) collective-permute-start(bf16[8,512,128]{2,1,0:T(8,128)(2,1)} %get-tuple-element.64), channel_id=1, source_target_pairs={{12,0},{13,1},{14,2},{15,3},{0,4},{1,5},{2,6},{3,7},{4,8},{5,9},{6... | collective-permute-start | bytes 3145736 | tf_op jit(solution)/shard_map/ppermute | solution.py:231
  33.5 29.4 %collective-permute-start.8 = (bf16[2,512,128]{2,1,0:T(8,128)(2,1)S(1)}, bf16[2,512,128]{2,1,0:T(8,128)(2,1)S(1)}, u32[]{:S(2)}, u32[]{:S(2)}) collective-permute-start(bf16[2,512,128]{2,1,0:T(8,128)(2,1)S(1)} %get-tuple-element.50), channel_id=1, source_target_pairs={{4,0},{5,1},{6,2},{7,3},{8,4},{9,5},{10,6},{11,7},{12,8},{13,9},{1... | collective-permute-start | bytes 786440 | tf_op jit(solution)/shard_map/ppermute | solution.py:231
  36.7 30.0 %collective-permute-start.9 = (bf16[2,512,128]{2,1,0:T(8,128)(2,1)S(1)}, bf16[2,512,128]{2,1,0:T(8,128)(2,1)S(1)}, u32[]{:S(2)}, u32[]{:S(2)}) collective-permute-start(bf16[2,512,128]{2,1,0:T(8,128)(2,1)S(1)} %get-tuple-element.50), channel_id=1, source_target_pairs={{12,0},{13,1},{14,2},{15,3},{0,4},{1,5},{2,6},{3,7},{4,8},{5,9},{6... | collective-permute-start | bytes 786440 | tf_op jit(solution)/shard_map/ppermute | solution.py:231
  57.4 14.6 %collective-permute-start.6 = (bf16[4,512,128]{2,1,0:T(8,128)(2,1)S(1)}, bf16[4,512,128]{2,1,0:T(8,128)(2,1)S(1)}, u32[]{:S(2)}, u32[]{:S(2)}) collective-permute-start(bf16[4,512,128]{2,1,0:T(8,128)(2,1)S(1)} %slice.51), channel_id=1, source_target_pairs={{4,0},{5,1},{6,2},{7,3},{8,4},{9,5},{10,6},{11,7},{12,8},{13,9},{1... | collective-permute-start | bytes 1572872 | tf_op jit(solution)/shard_map/ppermute | solution.py:231
  61.2 14.3 %collective-permute-start.7 = (bf16[4,512,128]{2,1,0:T(8,128)(2,1)S(1)}, bf16[4,512,128]{2,1,0:T(8,128)(2,1)S(1)}, u32[]{:S(2)}, u32[]{:S(2)}) collective-permute-start(bf16[4,512,128]{2,1,0:T(8,128)(2,1)S(1)} %slice.52), channel_id=1, source_target_pairs={{12,0},{13,1},{14,2},{15,3},{0,4},{1,5},{2,6},{3,7},{4,8},{5,9},{6... | collective-permute-start | bytes 1572872 | tf_op jit(solution)/shard_map/ppermute | solution.py:231
  62.9 15.7 %collective-permute-start.10 = (bf16[1,512,128]{2,1,0:T(8,128)(2,1)S(1)}, bf16[1,512,128]{2,1,0:T(8,128)(2,1)S(1)}, u32[]{:S(2)}, u32[]{:S(2)}) collective-permute-start(bf16[1,512,128]{2,1,0:T(8,128)(2,1)S(1)} %slice.54), channel_id=1, source_target_pairs={{4,0},{5,1},{6,2},{7,3},{8,4},{9,5},{10,6},{11,7},{12,8},{13,9},{1... | collective-permute-start | bytes 393224 | tf_op jit(solution)/shard_map/ppermute | solution.py:231
  66.7 12.6 %collective-permute-start.11 = (bf16[1,512,128]{2,1,0:T(8,128)(2,1)S(1)}, bf16[1,512,128]{2,1,0:T(8,128)(2,1)S(1)}, u32[]{:S(2)}, u32[]{:S(2)}) collective-permute-start(bf16[1,512,128]{2,1,0:T(8,128)(2,1)S(1)} %slice.55), channel_id=1, source_target_pairs={{12,0},{13,1},{14,2},{15,3},{0,4},{1,5},{2,6},{3,7},{4,8},{5,9},{6... | collective-permute-start | bytes 393224 | tf_op jit(solution)/shard_map/ppermute | solution.py:231
  80.0 23.2 %collective-permute-start.12 = (bf16[8,512,128]{2,1,0:T(8,128)(2,1)S(1)}, bf16[8,512,128]{2,1,0:T(8,128)(2,1)S(1)}, u32[]{:S(2)}, u32[]{:S(2)}) collective-permute-start(bf16[8,512,128]{2,1,0:T(8,128)(2,1)S(1)} %get-tuple-element.60), channel_id=1, source_target_pairs={{1,0},{2,1},{3,2},{0,3},{5,4},{6,5},{7,6},{4,7},{9,8},{10,9},{11,1... | collective-permute-start | bytes 3145736 | tf_op jit(solution)/shard_map/ppermute | solution.py:231
  81.6 24.3 %collective-permute-start.13 = (bf16[8,512,128]{2,1,0:T(8,128)(2,1)S(1)}, bf16[8,512,128]{2,1,0:T(8,128)(2,1)S(1)}, u32[]{:S(2)}, u32[]{:S(2)}) collective-permute-start(bf16[8,512,128]{2,1,0:T(8,128)(2,1)S(1)} %get-tuple-element.60), channel_id=1, source_target_pairs={{3,0},{0,1},{1,2},{2,3},{7,4},{4,5},{5,6},{6,7},{11,8},{8,9},{9,10... | collective-permute-start | bytes 3145736 | tf_op jit(solution)/shard_map/ppermute | solution.py:231
  106.0 10.5 %collective-permute-start.15 = (bf16[4,512,128]{2,1,0:T(8,128)(2,1)S(1)}, bf16[4,512,128]{2,1,0:T(8,128)(2,1)S(1)}, u32[]{:S(2)}, u32[]{:S(2)}) collective-permute-start(bf16[4,512,128]{2,1,0:T(8,128)(2,1)S(1)} %slice.57), channel_id=1, source_target_pairs={{3,0},{0,1},{1,2},{2,3},{7,4},{4,5},{5,6},{6,7},{11,8},{8,9},{9,10... | collective-permute-start | bytes 1572872 | tf_op jit(solution)/shard_map/ppermute | solution.py:231
  131.3 37.2 %collective-permute-start.24 = (s16[8,528,128]{2,1,0:T(8,128)(2,1)}, s16[8,528,128]{2,1,0:T(8,128)(2,1)S(1)}, u32[]{:S(2)}, u32[]{:S(2)}) collective-permute-start(s16[8,528,128]{2,1,0:T(8,128)(2,1)} %get-tuple-element.32), channel_id=1, source_target_pairs={{12,0},{13,1},{14,2},{15,3},{0,4},{1,5},{2,6},{3,7},{4,8},{5,9},{6... | collective-permute-start | bytes 3244040 | tf_op jit(solution)/shard_map/ppermute | solution.py:231
  131.3 37.2 %collective-permute-start.25 = (s16[8,528,128]{2,1,0:T(8,128)(2,1)}, s16[8,528,128]{2,1,0:T(8,128)(2,1)S(1)}, u32[]{:S(2)}, u32[]{:S(2)}) collective-permute-start(s16[8,528,128]{2,1,0:T(8,128)(2,1)} %get-tuple-element.33), channel_id=1, source_target_pairs={{4,0},{5,1},{6,2},{7,3},{8,4},{9,5},{10,6},{11,7},{12,8},{13,9},{1... | collective-permute-start | bytes 3244040 | tf_op jit(solution)/shard_map/ppermute | solution.py:231
  147.8 31.6 %collective-permute-start.16 = (s16[8,528,128]{2,1,0:T(8,128)(2,1)}, s16[8,528,128]{2,1,0:T(8,128)(2,1)S(1)}, u32[]{:S(2)}, u32[]{:S(2)}) collective-permute-start(s16[8,528,128]{2,1,0:T(8,128)(2,1)} %get-tuple-element.23), channel_id=1, source_target_pairs={{3,0},{0,1},{1,2},{2,3},{7,4},{4,5},{5,6},{6,7},{11,8},{8,9},{9,10... | collective-permute-start | bytes 3244040 | tf_op jit(solution)/shard_map/ppermute | solution.py:231
  147.8 31.6 %collective-permute-start.17 = (s16[8,528,128]{2,1,0:T(8,128)(2,1)}, s16[8,528,128]{2,1,0:T(8,128)(2,1)S(1)}, u32[]{:S(2)}, u32[]{:S(2)}) collective-permute-start(s16[8,528,128]{2,1,0:T(8,128)(2,1)} %get-tuple-element.24), channel_id=1, source_target_pairs={{1,0},{2,1},{3,2},{0,3},{5,4},{6,5},{7,6},{4,7},{9,8},{10,9},{11,1... | collective-permute-start | bytes 3244040 | tf_op jit(solution)/shard_map/ppermute | solution.py:231
  176.1 14.0 %collective-permute-start.26 = (s16[4,528,128]{2,1,0:T(8,128)(2,1)}, s16[4,528,128]{2,1,0:T(8,128)(2,1)S(1)}, u32[]{:S(2)}, u32[]{:S(2)}) collective-permute-start(s16[4,528,128]{2,1,0:T(8,128)(2,1)} %get-tuple-element.34), channel_id=1, source_target_pairs={{12,0},{13,1},{14,2},{15,3},{0,4},{1,5},{2,6},{3,7},{4,8},{5,9},{6... | collective-permute-start | bytes 1622024 | tf_op jit(solution)/shard_map/ppermute | solution.py:231
  176.1 14.0 %collective-permute-start.27 = (s16[4,528,128]{2,1,0:T(8,128)(2,1)}, s16[4,528,128]{2,1,0:T(8,128)(2,1)S(1)}, u32[]{:S(2)}, u32[]{:S(2)}) collective-permute-start(s16[4,528,128]{2,1,0:T(8,128)(2,1)} %get-tuple-element.35), channel_id=1, source_target_pairs={{4,0},{5,1},{6,2},{7,3},{8,4},{9,5},{10,6},{11,7},{12,8},{13,9},{1... | collective-permute-start | bytes 1622024 | tf_op jit(solution)/shard_map/ppermute | solution.py:231
  186.9 14.2 %collective-permute-start.18 = (s16[4,528,128]{2,1,0:T(8,128)(2,1)}, s16[4,528,128]{2,1,0:T(8,128)(2,1)S(1)}, u32[]{:S(2)}, u32[]{:S(2)}) collective-permute-start(s16[4,528,128]{2,1,0:T(8,128)(2,1)} %get-tuple-element.25), channel_id=1, source_target_pairs={{3,0},{0,1},{1,2},{2,3},{7,4},{4,5},{5,6},{6,7},{11,8},{8,9},{9,10... | collective-permute-start | bytes 1622024 | tf_op jit(solution)/shard_map/ppermute | solution.py:231
  187.3 13.8 %collective-permute-start.19 = (s16[4,528,128]{2,1,0:T(8,128)(2,1)}, s16[4,528,128]{2,1,0:T(8,128)(2,1)S(1)}, u32[]{:S(2)}, u32[]{:S(2)}) collective-permute-start(s16[4,528,128]{2,1,0:T(8,128)(2,1)} %get-tuple-element.26), channel_id=1, source_target_pairs={{1,0},{2,1},{3,2},{0,3},{5,4},{6,5},{7,6},{4,7},{9,8},{10,9},{11,1... | collective-permute-start | bytes 1622024 | tf_op jit(solution)/shard_map/ppermute | solution.py:231
  197.9 14.1 %collective-permute-start.28 = (s16[2,528,128]{2,1,0:T(8,128)(2,1)}, s16[2,528,128]{2,1,0:T(8,128)(2,1)S(1)}, u32[]{:S(2)}, u32[]{:S(2)}) collective-permute-start(s16[2,528,128]{2,1,0:T(8,128)(2,1)} %get-tuple-element.37), channel_id=1, source_target_pairs={{3,0},{0,1},{1,2},{2,3},{7,4},{4,5},{5,6},{6,7},{11,8},{8,9},{9,10... | collective-permute-start | bytes 811016 | tf_op jit(solution)/shard_map/ppermute | solution.py:231
  197.9 14.1 %collective-permute-start.29 = (s16[2,528,128]{2,1,0:T(8,128)(2,1)}, s16[2,528,128]{2,1,0:T(8,128)(2,1)S(1)}, u32[]{:S(2)}, u32[]{:S(2)}) collective-permute-start(s16[2,528,128]{2,1,0:T(8,128)(2,1)} %get-tuple-element.38), channel_id=1, source_target_pairs={{1,0},{2,1},{3,2},{0,3},{5,4},{6,5},{7,6},{4,7},{9,8},{10,9},{11,1... | collective-permute-start | bytes 811016 | tf_op jit(solution)/shard_map/ppermute | solution.py:231
  215.0 16.3 %collective-permute-start.30 = (s16[1,528,128]{2,1,0:T(8,128)(2,1)}, s16[1,528,128]{2,1,0:T(8,128)(2,1)S(1)}, u32[]{:S(2)}, u32[]{:S(2)}) collective-permute-start(s16[1,528,128]{2,1,0:T(8,128)(2,1)} %get-tuple-element.39), channel_id=1, source_target_pairs={{3,0},{0,1},{1,2},{2,3},{7,4},{4,5},{5,6},{6,7},{11,8},{8,9},{9,10... | collective-permute-start | bytes 405512 | tf_op jit(solution)/shard_map/ppermute | solution.py:231
  215.0 16.3 %collective-permute-start.31 = (s16[1,528,128]{2,1,0:T(8,128)(2,1)}, s16[1,528,128]{2,1,0:T(8,128)(2,1)S(1)}, u32[]{:S(2)}, u32[]{:S(2)}) collective-permute-start(s16[1,528,128]{2,1,0:T(8,128)(2,1)} %get-tuple-element.40), channel_id=1, source_target_pairs={{1,0},{2,1},{3,2},{0,3},{5,4},{6,5},{7,6},{4,7},{9,8},{10,9},{11,1... | collective-permute-start | bytes 405512 | tf_op jit(solution)/shard_map/ppermute | solution.py:231
  (30 other events, 302.6 us)
Sparse Core Ops, SparseCore 0:
  14.3 33.6 all-gather.1

commit v2 on v1

--- a/solution.py
+++ b/solution.py
@@ -14,7 +14,6 @@
 ENTRIES = 224
 UNROLL = 8
 HALF_RANGE = 14.9
-VMEM_LIMIT = 58 * 1024 * 1024
 NEAR = {0: 0, 1: 1, 3: 2, 2: 3}
 
 VMEM_SPEC = pl.BlockSpec(memory_space=pltpu.VMEM)
@@ -109,15 +108,14 @@
     return jax.ShapeDtypeStruct((n, ROWS, TILE), jnp.float32)
 
 
-def kernel(body, outs, specs, scratch=(), name=None):
+def kernel(body, outs, specs, scratch=(), grant=4):
     return pl.pallas_call(
         body,
         out_shape=outs,
         in_specs=specs,
         out_specs=jax.tree.map(lambda _: VMEM_SPEC, outs),
         scratch_shapes=list(scratch),
-        compiler_params=pltpu.CompilerParams(vmem_limit_bytes=VMEM_LIMIT),
-        name=name,
+        compiler_params=pltpu.CompilerParams(vmem_limit_bytes=grant * 1024 * 1024),
     )
 
 
@@ -161,7 +159,53 @@
     outs = (coded(count // 2), coded(count // 2)) if send else (plain(count),)
     scratch = [pltpu.VMEM((count, ROWS, TILE), jnp.float32)] if send else []
     specs = [SMEM_SPEC] * 3 + [VMEM_SPEC] * 2
-    return kernel(body, outs, specs, scratch)(tiles, owner, bounds, amps, integrals)
+    return kernel(body, outs, specs, scratch, 8)(tiles, owner, bounds, amps, integrals)
+
+
+def masked_tiles(t2, t2_live):
+    def body(live_ref, t2_ref, out_ref):
+        for t in range(4):
+            keep = live_ref[0, t].astype(jnp.float32).astype(jnp.bfloat16)
+            out_ref[t] = t2_ref[:, t * TILE : (t + 1) * TILE] * keep
+
+    out = jax.ShapeDtypeStruct((4, ROWS, TILE), jnp.bfloat16)
+    return kernel(body, out, [SMEM_SPEC, VMEM_SPEC])(t2_live, t2)
+
+
+def join(*groups):
+    sizes = [[piece.shape[0] for piece in group] for group in groups]
+
+    def body(*refs):
+        pieces = refs[: -len(groups)]
+        for g, out_ref in enumerate(refs[-len(groups) :]):
+            at = 0
+            for size in sizes[g]:
+                for k in range(size):
+                    out_ref[at + k] = pieces[0][k]
+                pieces = pieces[1:]
+                at += size
+
+    outs = tuple(jax.ShapeDtypeStruct((sum(size), ROWS, TILE), jnp.bfloat16) for size in sizes)
+    flat = [piece for group in groups for piece in group]
+    return kernel(body, outs, [VMEM_SPEC] * len(flat))(*flat)
+
+
+def cycle_part(blocks, weights, tiles, base=None):
+    def body(blocks_ref, weights_ref, tiles_ref, *rest):
+        out_ref = rest[-1]
+        for half in range(2):
+            cols = slice(half * 2 * TILE, (half + 1) * 2 * TILE)
+            total = None if base is None else rest[0][:, cols]
+            for k in range(4):
+                at = pl.multiple_of(blocks_ref[k] * ROWS, ROWS)
+                value = jnp.concatenate([tiles_ref[4 * k + 2 * half], tiles_ref[4 * k + 2 * half + 1]], axis=1)
+                part = jnp.dot(weights_ref[:, pl.ds(at, ROWS)], value, preferred_element_type=jnp.float32)
+                total = part if total is None else total + part
+            out_ref[:, cols] = total
+
+    out = jax.ShapeDtypeStruct((ROWS, 4 * TILE), jnp.float32)
+    args = (blocks, weights, tiles) if base is None else (blocks, weights, tiles, base)
+    return kernel(body, out, [SMEM_SPEC] + [VMEM_SPEC] * (len(args) - 1))(*args)
 
 
 def merge(sums, got_up, got_down, base):
@@ -236,41 +280,54 @@
     def along_y(value, d):
         return take(value, d, 0)
 
-    mask = jnp.repeat(t2_live[0].astype(t2.dtype), TILE)
-    flat = t2 * mask[None, :]
-    own = flat.reshape(ROWS, 4, TILE).transpose(1, 0, 2)
-
-    def gather(value, near_axis, far_axis):
-        n = value.shape[0] // 2
-        up, down = near_axis(value, 1), near_axis(value, 3)
-        over = near_axis(up[:n], 1), near_axis(down[n:], 3)
-        row = jnp.concatenate([value, up, down, *over], axis=0)
-        n = row.shape[0] // 2
-        up, down = far_axis(row, 1), far_axis(row, 3)
-        over = far_axis(up[:n], 1), far_axis(down[n:], 3)
-        return [row, up, down, *over]
-
-    pieces_a = gather(own[:2], along_z, along_y)
-    pieces_b = gather(own[2:], along_y, along_z)
-    amps = jnp.concatenate(pieces_a + pieces_b, axis=0)
+    own = masked_tiles(t2, t2_live)
+    pair = lax.axis_index("pair").astype(jnp.int32)
+
+    def along_x(value, d, core=0):
+        pairs = [(((i + d) % SIDE) * 2 + (c ^ core), i * 2 + c) for i in range(SIDE) for c in range(2)]
+        return lax.ppermute(value, "pair", pairs)
+
+    def blocks(core):
+        ahead = (pair >> 1) + jnp.array([0, 1, 3, 2], jnp.int32)
+        return ((ahead & 3) << 1) | ((pair & 1) ^ core)
+
+    def both(value, axis):
+        return axis(value, 1), axis(value, 3)
+
+    def far(value, axis):
+        up, down = value
+        n = up.shape[0] // 2
+        return axis(up[:n], 1), axis(down[n:], 3)
 
     source = pick(source_table(), relative(int_tiles[:, 0], y, z))
     target = pick(target_table(), relative(int_tiles[:, 1], y, z))
-    tiles, owner, bounds = work_list(source, target)
-
-    send_a = ladder(tiles, owner, bounds, amps, integrals, 0, 16, True)
-    send_b = ladder(tiles, owner, bounds, amps, integrals, 16, 16, True)
+    work = work_list(source, target)
+
+    low, high = own[:2], own[2:]
+    near_x = both(own, along_x)
+    near_low, near_high, work = lax.optimization_barrier((both(low, along_z), both(high, along_y), work))
+    over_low, over_high, near_x = lax.optimization_barrier((far(near_low, along_z), far(near_high, along_y), near_x))
+    low, high = join((low, *near_low, *over_low), (high, *near_high, *over_high))
+    near_low, near_high, over_x = lax.optimization_barrier(
+        (both(low, along_y), both(high, along_z), far(near_x, along_x))
+    )
+    over_low, over_high = far(near_low, along_y), far(near_high, along_z)
+    (mine,) = join((own, *near_x, *over_x))
+    other = along_x(mine, 0, 1)
+    cycle = cycle_part(blocks(0), cycle_w, mine)
+    (amps,) = join((low, *near_low, *over_low, high, *near_high, *over_high))
+    amps, cycle = lax.optimization_barrier((amps, cycle))
+    cycle = cycle_part(blocks(1), cycle_w, other, cycle)
+
+    send_a = ladder(*work, amps, integrals, 0, 16, True)
+    send_b = ladder(*work, amps, integrals, 16, 16, True)
 
     def first_hop(send, axis):
         return axis(send[0], 3), axis(send[1], 1)
 
     got_a = first_hop(send_a, along_z)
     got_b = first_hop(send_b, along_y)
-    (sums,) = ladder(tiles, owner, bounds, amps, integrals, 32, 32, False)
-
-    cycle = jnp.dot(
-        cycle_w, lax.all_gather(flat, "pair", axis=0, tiled=True), preferred_element_type=jnp.float32
-    )
+    (sums,) = ladder(*work, amps, integrals, 32, 32, False)
 
     def reduce(got, axis, other, base):
         on = merge(sums, *got, base)

time: 244 us -> 150 us (0.61)
  Pallas kernels: 76.1 us -> 33.8 us
  waiting for transfers between devices: 62.7 us -> 40 us
  local copies, waits for them, and re-layouts: 27.3 us -> 11.9 us
  between operations: 13.6 us -> 0.44 us
  starting transfers between devices: 51.9 us -> 61.1 us
  matrix products: 6.84 us -> 0 us
    ppermute x32, waiting for transfers between devices: 62.7 us -> 27.6 us  [take(): return lax.ppermute(value, 'ints', pairs)]
    pallas_call x3 -> x9, Pallas kernels: 44.8 us -> 28.5 us  [the longest x3 21.9 us: ladder(): kernel(body, outs, specs, scratch, 8)(tiles, owner, bounds, amps, integrals)]
    unnamed x58 -> x46, local copies, waits for them, and re-layouts: 24.5 us -> 8.29 us
    ppermute x0 -> x5, waiting for transfers between devices: none -> 12.4 us  [along_x(): return lax.ppermute(value, 'pair', pairs)]
    pallas_call x2, Pallas kernels: 12.1 us -> 1.78 us  [row_sum(): kernel(body, (coded(2), coded(2), plain(4)), [VMEM_SPEC] * 5)]
    pallas_call x2, Pallas kernels: 11.2 us -> 1.33 us  [merge(): kernel(body, (coded(4), coded(4)), [VMEM_SPEC] * 3)(sums, got_up, got_down)]
    dot_general x1 -> x0, matrix products: 6.84 us -> none  [local(): jnp.dot(cycle_w, lax.all_gather(flat, 'pair', axis=0, tiled=True), prefer...]
    ppermute x0 -> x5, starting transfers between devices: none -> 5 us  [along_x(): return lax.ppermute(value, 'pair', pairs)]
  transfers between devices with their start and end apart: 33 -> 37, of which waited for: 10 -> 14; matrix products, arithmetic and copies ran while one was open for 10% -> 2% of each run, Pallas kernels for 30% -> 21%
where the time goes in v2:
time: 150 us
  starting transfers between devices  61.1 us (41%)
  waiting for transfers between devices  40 us (27%)
  Pallas kernels  33.8 us (23%)
  local copies, waits for them, and re-layouts  11.9 us (8%)
  other arithmetic  2.34 us (2%)
    ppermute x32, starting transfers between devices, take(): return lax.ppermute(value, 'ints', pairs)  56.1 us
    ppermute x32, waiting for transfers between devices, take(): return lax.ppermute(value, 'ints', pairs)  27.6 us
    pallas_call x3, Pallas kernels, ladder(): kernel(body, outs, specs, scratch, 8)(tiles, owner, bounds, amps, integrals)  21.9 us
    ppermute x5, waiting for transfers between devices, along_x(): return lax.ppermute(value, 'pair', pairs)  12.4 us
    unnamed x46, local copies, waits for them, and re-layouts  8.29 us
    ppermute x5, starting transfers between devices, along_x(): return lax.ppermute(value, 'pair', pairs)  5 us
    pallas_call x2, Pallas kernels, cycle_part(): return kernel(body, out, [SMEM_SPEC] + [VMEM_SPEC] * (len(args) - 1))(*args)  3.59 us
    slice x10, local copies, waits for them, and re-layouts, far(): return (axis(up[:n], 1), axis(down[n:], 3))  3.57 us
  transfers between devices with their start and end apart: 37, of which 14 were waited for; matrix products, arithmetic and copies ran while one was open for 2% of the time, Pallas kernels for 21%

profile of v2, /device:TPU:0, one launch (start us, length us, event | category | flops | bytes accessed | tf_op | source)
XLA Modules:
  0.0 149.5 jit_solution(16764290541425203847)
XLA Ops:
  16.1 3.1 %collective-permute-start.6 = (bf16[1,512,128]{2,1,0:T(8,128)(2,1)S(1)}, bf16[1,512,128]{2,1,0:T(8,128)(2,1)S(1)}, u32[]{:S(2)}, u32[]{:S(2)}) collective-permute-start(bf16[1,512,128]{2,1,0:T(8,128)(2,1)S(1)} %slice.48), channel_id=1, source_target_pairs={{4,0},{5,1},{6,2},{7,3},{8,4},{9,5},{10,6},{11,7},{12,8},{13,9},{1... | collective-permute-start | bytes 393224 | tf_op jit(solution)/shard_map/ppermute | solution.py:275
  22.0 3.7 %collective-permute-start.4 = (bf16[1,512,128]{2,1,0:T(8,128)(2,1)S(1)}, bf16[1,512,128]{2,1,0:T(8,128)(2,1)S(1)}, u32[]{:S(2)}, u32[]{:S(2)}) collective-permute-start(bf16[1,512,128]{2,1,0:T(8,128)(2,1)S(1)} %slice.46), channel_id=1, source_target_pairs={{1,0},{2,1},{3,2},{0,3},{5,4},{6,5},{7,6},{4,7},{9,8},{10,9},{11,1... | collective-permute-start | bytes 393224 | tf_op jit(solution)/shard_map/ppermute | solution.py:275
  25.8 2.4 %collective-permute-done.4.refs_3_ = bf16[1,512,128]{2,1,0:T(8,128)(2,1)S(1)} collective-permute-done((bf16[1,512,128]{2,1,0:T(8,128)(2,1)S(1)}, bf16[1,512,128]{2,1,0:T(8,128)(2,1)S(1)}, u32[]{:S(2)}, u32[]{:S(2)}) %collective-permute-start.4) | collective-permute-done | bytes 131104 | tf_op jit(solution)/shard_map/ppermute | solution.py:275
  28.5 3.2 %collective-permute-start.10 = (bf16[8,512,128]{2,1,0:T(8,128)(2,1)S(1)}, bf16[8,512,128]{2,1,0:T(8,128)(2,1)S(1)}, u32[]{:S(2)}, u32[]{:S(2)}) collective-permute-start(bf16[8,512,128]{2,1,0:T(8,128)(2,1)S(1)} %get-tuple-element.56.refs_0_), channel_id=1, source_target_pairs={{4,0},{5,1},{6,2},{7,3},{8,4},{9,5},{10,6},{11,7},{12,8},{13,9},{1... | collective-permute-start | bytes 3145736 | tf_op jit(solution)/shard_map/ppermute | solution.py:275
  32.0 3.3 %collective-permute-start.12 = (bf16[8,512,128]{2,1,0:T(8,128)(2,1)S(1)}, bf16[8,512,128]{2,1,0:T(8,128)(2,1)S(1)}, u32[]{:S(2)}, u32[]{:S(2)}) collective-permute-start(bf16[8,512,128]{2,1,0:T(8,128)(2,1)S(1)} %get-tuple-element.57.refs_5_), channel_id=1, source_target_pairs={{1,0},{2,1},{3,2},{0,3},{5,4},{6,5},{7,6},{4,7},{9,8},{10,9},{11,1... | collective-permute-start | bytes 3145736 | tf_op jit(solution)/shard_map/ppermute | solution.py:275
  36.2 6.8 %collective-permute-done.15.refs_4_ = bf16[2,512,128]{2,1,0:T(8,128)(2,1)S(1)} collective-permute-done((bf16[2,512,128]{2,1,0:T(8,128)(2,1)S(1)}, bf16[2,512,128]{2,1,0:T(8,128)(2,1)S(1)}, u32[]{:S(2)}, u32[]{:S(2)}) %collective-permute-start.15) | collective-permute-done | bytes 262176 | tf_op jit(solution)/shard_map/ppermute | solution.py:288
  43.8 5.6 %collective-permute-done.14.refs_3_ = bf16[2,512,128]{2,1,0:T(8,128)(2,1)S(1)} collective-permute-done((bf16[2,512,128]{2,1,0:T(8,128)(2,1)S(1)}, bf16[2,512,128]{2,1,0:T(8,128)(2,1)S(1)}, u32[]{:S(2)}, u32[]{:S(2)}) %collective-permute-start.14) | collective-permute-done | bytes 262176 | tf_op jit(solution)/shard_map/ppermute | solution.py:288
  51.8 3.1 %collective-permute-done.13.refs_7_ = bf16[8,512,128]{2,1,0:T(8,128)(2,1)S(1)} collective-permute-done((bf16[8,512,128]{2,1,0:T(8,128)(2,1)S(1)}, bf16[8,512,128]{2,1,0:T(8,128)(2,1)S(1)}, u32[]{:S(2)}, u32[]{:S(2)}) %collective-permute-start.13) | collective-permute-done | bytes 1048608 | tf_op jit(solution)/shard_map/ppermute | solution.py:275
  59.5 2.1 %collective-permute-start.19 = (bf16[4,512,128]{2,1,0:T(8,128)(2,1)}, bf16[4,512,128]{2,1,0:T(8,128)(2,1)}, u32[]{:S(2)}, u32[]{:S(2)}) collective-permute-start(bf16[4,512,128]{2,1,0:T(8,128)(2,1)} %slice.54), channel_id=1, source_target_pairs={{1,0},{2,1},{3,2},{0,3},{5,4},{6,5},{7,6},{4,7},{9,8},{10,9},{11,1... | collective-permute-start | bytes 1572872 | tf_op jit(solution)/shard_map/ppermute | solution.py:275
  61.6 3.2 %collective-permute-start.17 = (bf16[4,512,128]{2,1,0:T(8,128)(2,1)}, bf16[4,512,128]{2,1,0:T(8,128)(2,1)}, u32[]{:S(2)}, u32[]{:S(2)}) collective-permute-start(bf16[4,512,128]{2,1,0:T(8,128)(2,1)} %slice.52), channel_id=1, source_target_pairs={{4,0},{5,1},{6,2},{7,3},{8,4},{9,5},{10,6},{11,7},{12,8},{13,9},{1... | collective-permute-start | bytes 1572872 | tf_op jit(solution)/shard_map/ppermute | solution.py:275
  76.3 6.3 %shard_map.111 = (s16[8,528,128]{2,1,0:T(8,128)(2,1)S(1)}, s16[8,528,128]{2,1,0:T(8,128)(2,1)S(1)}) custom-call(s32[448]{0:T(512)S(1)} %select_reduce_fusion.tiles_ref, s32[224]{0:T(256)S(1)} %multiply_add_fusion.owner_ref, s32[65]{0:T(128)S(1)} %pad_add_fusion.bounds_ref, bf16[64,512,128]{2,1,0:T(8,128)(2,1)S(1)} %shard_map.103.amps_ref, ...), custom_call_target="tpu_custom_call" | custom-call | tf_op jit(solution)/shard_map/pallas_call | solution.py:162
  82.9 3.2 %collective-permute-start.30 = (s16[8,528,128]{2,1,0:T(8,128)(2,1)S(1)}, s16[8,528,128]{2,1,0:T(8,128)(2,1)S(1)}, u32[]{:S(2)}, u32[]{:S(2)}) collective-permute-start(s16[8,528,128]{2,1,0:T(8,128)(2,1)S(1)} %get-tuple-element.79), channel_id=1, source_target_pairs={{4,0},{5,1},{6,2},{7,3},{8,4},{9,5},{10,6},{11,7},{12,8},{13,9},{1... | collective-permute-start | bytes 3244040 | tf_op jit(solution)/shard_map/ppermute | solution.py:275
  86.1 6.3 %shard_map.107 = (s16[8,528,128]{2,1,0:T(8,128)(2,1)S(1)}, s16[8,528,128]{2,1,0:T(8,128)(2,1)S(1)}) custom-call(s32[448]{0:T(512)S(1)} %select_reduce_fusion.tiles_ref, s32[224]{0:T(256)S(1)} %multiply_add_fusion.owner_ref, s32[65]{0:T(128)S(1)} %pad_add_fusion.bounds_ref, bf16[64,512,128]{2,1,0:T(8,128)(2,1)S(1)} %shard_map.103.amps_ref, ...), custom_call_target="tpu_custom_call" | custom-call | tf_op jit(solution)/shard_map/pallas_call | solution.py:162
  93.2 2.5 %collective-permute-start.22 = (s16[8,528,128]{2,1,0:T(8,128)(2,1)S(1)}, s16[8,528,128]{2,1,0:T(8,128)(2,1)S(1)}, u32[]{:S(2)}, u32[]{:S(2)}) collective-permute-start(s16[8,528,128]{2,1,0:T(8,128)(2,1)S(1)} %get-tuple-element.70), channel_id=1, source_target_pairs={{1,0},{2,1},{3,2},{0,3},{5,4},{6,5},{7,6},{4,7},{9,8},{10,9},{11,1... | collective-permute-start | bytes 3244040 | tf_op jit(solution)/shard_map/ppermute | solution.py:275
  95.7 9.3 %shard_map.106.sums_ref = f32[32,512,128]{2,1,0:T(8,128)S(1)} custom-call(s32[448]{0:T(512)S(1)} %select_reduce_fusion.tiles_ref, s32[224]{0:T(256)S(1)} %multiply_add_fusion.owner_ref, s32[65]{0:T(128)S(1)} %pad_add_fusion.bounds_ref, bf16[64,512,128]{2,1,0:T(8,128)(2,1)S(1)} %shard_map.103.amps_ref, bf16[320,128,128]{2,1,0:T(8,128)(2,1)S(1)} %bitcast.2), custom_call_target="tpu_custom_call" | custom-call | tf_op jit(solution)/shard_map/pallas_call | solution.py:162
  105.0 2.4 %collective-permute-done.29.up_ref = s16[8,528,128]{2,1,0:T(8,128)(2,1)S(1)} collective-permute-done((s16[8,528,128]{2,1,0:T(8,128)(2,1)S(1)}, s16[8,528,128]{2,1,0:T(8,128)(2,1)S(1)}, u32[]{:S(2)}, u32[]{:S(2)}) %collective-permute-start.29) | collective-permute-done | bytes 1081376 | tf_op jit(solution)/shard_map/ppermute | solution.py:275
  108.2 3.2 %collective-permute-start.32 = (s16[4,528,128]{2,1,0:T(8,128)(2,1)S(1)}, s16[4,528,128]{2,1,0:T(8,128)(2,1)S(1)}, u32[]{:S(2)}, u32[]{:S(2)}) collective-permute-start(s16[4,528,128]{2,1,0:T(8,128)(2,1)S(1)} %get-tuple-element.81), channel_id=1, source_target_pairs={{4,0},{5,1},{6,2},{7,3},{8,4},{9,5},{10,6},{11,7},{12,8},{13,9},{1... | collective-permute-start | bytes 1622024 | tf_op jit(solution)/shard_map/ppermute | solution.py:275
  111.5 5.1 %collective-permute-done.21.up_ref = s16[8,528,128]{2,1,0:T(8,128)(2,1)S(1)} collective-permute-done((s16[8,528,128]{2,1,0:T(8,128)(2,1)S(1)}, s16[8,528,128]{2,1,0:T(8,128)(2,1)S(1)}, u32[]{:S(2)}, u32[]{:S(2)}) %collective-permute-start.21) | collective-permute-done | bytes 1081376 | tf_op jit(solution)/shard_map/ppermute | solution.py:275
  117.4 3.1 %collective-permute-start.24 = (s16[4,528,128]{2,1,0:T(8,128)(2,1)S(1)}, s16[4,528,128]{2,1,0:T(8,128)(2,1)S(1)}, u32[]{:S(2)}, u32[]{:S(2)}) collective-permute-start(s16[4,528,128]{2,1,0:T(8,128)(2,1)S(1)} %get-tuple-element.72), channel_id=1, source_target_pairs={{1,0},{2,1},{3,2},{0,3},{5,4},{6,5},{7,6},{4,7},{9,8},{10,9},{11,1... | collective-permute-start | bytes 1622024 | tf_op jit(solution)/shard_map/ppermute | solution.py:275
  121.5 3.2 %collective-permute-start.34 = (s16[2,528,128]{2,1,0:T(8,128)(2,1)S(1)}, s16[2,528,128]{2,1,0:T(8,128)(2,1)S(1)}, u32[]{:S(2)}, u32[]{:S(2)}) collective-permute-start(s16[2,528,128]{2,1,0:T(8,128)(2,1)S(1)} %get-tuple-element.84), channel_id=1, source_target_pairs={{1,0},{2,1},{3,2},{0,3},{5,4},{6,5},{7,6},{4,7},{9,8},{10,9},{11,1... | collective-permute-start | bytes 811016 | tf_op jit(solution)/shard_map/ppermute | solution.py:275
  124.7 7.0 %collective-permute-done.23.last_up_ref = s16[4,528,128]{2,1,0:T(8,128)(2,1)S(1)} collective-permute-done((s16[4,528,128]{2,1,0:T(8,128)(2,1)S(1)}, s16[4,528,128]{2,1,0:T(8,128)(2,1)S(1)}, u32[]{:S(2)}, u32[]{:S(2)}) %collective-permute-start.23) | collective-permute-done | bytes 540704 | tf_op jit(solution)/shard_map/ppermute | solution.py:275
  132.7 3.2 %collective-permute-start.26 = (s16[2,528,128]{2,1,0:T(8,128)(2,1)S(1)}, s16[2,528,128]{2,1,0:T(8,128)(2,1)S(1)}, u32[]{:S(2)}, u32[]{:S(2)}) collective-permute-start(s16[2,528,128]{2,1,0:T(8,128)(2,1)S(1)} %get-tuple-element.75), channel_id=1, source_target_pairs={{4,0},{5,1},{6,2},{7,3},{8,4},{9,5},{10,6},{11,7},{12,8},{13,9},{1... | collective-permute-start | bytes 811016 | tf_op jit(solution)/shard_map/ppermute | solution.py:275
  137.0 2.4 %collective-permute-start.36 = (s16[1,528,128]{2,1,0:T(8,128)(2,1)S(1)}, s16[1,528,128]{2,1,0:T(8,128)(2,1)S(1)}, u32[]{:S(2)}, u32[]{:S(2)}) collective-permute-start(s16[1,528,128]{2,1,0:T(8,128)(2,1)S(1)} %get-tuple-element.86), channel_id=1, source_target_pairs={{1,0},{2,1},{3,2},{0,3},{5,4},{6,5},{7,6},{4,7},{9,8},{10,9},{11,1... | collective-permute-start | bytes 405512 | tf_op jit(solution)/shard_map/ppermute | solution.py:275
  141.4 3.2 %collective-permute-start.28 = (s16[1,528,128]{2,1,0:T(8,128)(2,1)S(1)}, s16[1,528,128]{2,1,0:T(8,128)(2,1)S(1)}, u32[]{:S(2)}, u32[]{:S(2)}) collective-permute-start(s16[1,528,128]{2,1,0:T(8,128)(2,1)S(1)} %get-tuple-element.77), channel_id=1, source_target_pairs={{4,0},{5,1},{6,2},{7,3},{8,4},{9,5},{10,6},{11,7},{12,8},{13,9},{1... | collective-permute-start | bytes 405512 | tf_op jit(solution)/shard_map/ppermute | solution.py:275
  (138 shorter events, 52.0 us)
Async XLA Ops:
  2.4 10.6 %collective-permute-start.3 = (bf16[2,512,128]{2,1,0:T(8,128)(2,1)S(1)}, bf16[2,512,128]{2,1,0:T(8,128)(2,1)S(1)}, u32[]{:S(2)}, u32[]{:S(2)}) collective-permute-start(bf16[2,512,128]{2,1,0:T(8,128)(2,1)S(1)} %get-tuple-element.93.refs_5_), channel_id=1, source_target_pairs={{12,0},{13,1},{14,2},{15,3},{0,4},{1,5},{2,6},{3,7},{4,8},{5,9},{6... | collective-permute-start | bytes 786440 | tf_op jit(solution)/shard_map/ppermute | solution.py:275
  4.1 11.4 %collective-permute-start.2 = (bf16[2,512,128]{2,1,0:T(8,128)(2,1)S(1)}, bf16[2,512,128]{2,1,0:T(8,128)(2,1)S(1)}, u32[]{:S(2)}, u32[]{:S(2)}) collective-permute-start(bf16[2,512,128]{2,1,0:T(8,128)(2,1)S(1)} %get-tuple-element.93.refs_5_), channel_id=1, source_target_pairs={{4,0},{5,1},{6,2},{7,3},{8,4},{9,5},{10,6},{11,7},{12,8},{13,9},{1... | collective-permute-start | bytes 786440 | tf_op jit(solution)/shard_map/ppermute | solution.py:275
  9.8 18.4 %collective-permute-start.9 = (bf16[4,512,128]{2,1,0:T(8,128)(2,1)S(1)}, bf16[4,512,128]{2,1,0:T(8,128)(2,1)S(1)}, u32[]{:S(2)}, u32[]{:S(2)}) collective-permute-start(bf16[4,512,128]{2,1,0:T(8,128)(2,1)S(1)} %shard_map.100.refs_0_), channel_id=1, source_target_pairs={{96,0},{112,16},{0,32},{16,48},{32,64},{48,80},{64,96},{80,112},{9... | collective-permute-start | bytes 1572872 | tf_op jit(solution)/shard_map/ppermute | solution.py:288
  13.0 15.2 %collective-permute-start.8 = (bf16[4,512,128]{2,1,0:T(8,128)(2,1)S(1)}, bf16[4,512,128]{2,1,0:T(8,128)(2,1)S(1)}, u32[]{:S(2)}, u32[]{:S(2)}) collective-permute-start(bf16[4,512,128]{2,1,0:T(8,128)(2,1)S(1)} %shard_map.100.refs_0_), channel_id=1, source_target_pairs={{32,0},{48,16},{64,32},{80,48},{96,64},{112,80},{0,96},{16,112},{3... | collective-permute-start | bytes 1572872 | tf_op jit(solution)/shard_map/ppermute | solution.py:288
  28.4 23.4 %collective-permute-start.11 = (bf16[8,512,128]{2,1,0:T(8,128)(2,1)S(1)}, bf16[8,512,128]{2,1,0:T(8,128)(2,1)S(1)}, u32[]{:S(2)}, u32[]{:S(2)}) collective-permute-start(bf16[8,512,128]{2,1,0:T(8,128)(2,1)S(1)} %get-tuple-element.56.refs_0_), channel_id=1, source_target_pairs={{12,0},{13,1},{14,2},{15,3},{0,4},{1,5},{2,6},{3,7},{4,8},{5,9},{6... | collective-permute-start | bytes 3145736 | tf_op jit(solution)/shard_map/ppermute | solution.py:275
  28.5 23.3 %collective-permute-start.10 = (bf16[8,512,128]{2,1,0:T(8,128)(2,1)S(1)}, bf16[8,512,128]{2,1,0:T(8,128)(2,1)S(1)}, u32[]{:S(2)}, u32[]{:S(2)}) collective-permute-start(bf16[8,512,128]{2,1,0:T(8,128)(2,1)S(1)} %get-tuple-element.56.refs_0_), channel_id=1, source_target_pairs={{4,0},{5,1},{6,2},{7,3},{8,4},{9,5},{10,6},{11,7},{12,8},{13,9},{1... | collective-permute-start | bytes 3145736 | tf_op jit(solution)/shard_map/ppermute | solution.py:275
  31.7 23.2 %collective-permute-start.13 = (bf16[8,512,128]{2,1,0:T(8,128)(2,1)S(1)}, bf16[8,512,128]{2,1,0:T(8,128)(2,1)S(1)}, u32[]{:S(2)}, u32[]{:S(2)}) collective-permute-start(bf16[8,512,128]{2,1,0:T(8,128)(2,1)S(1)} %get-tuple-element.57.refs_5_), channel_id=1, source_target_pairs={{3,0},{0,1},{1,2},{2,3},{7,4},{4,5},{5,6},{6,7},{11,8},{8,9},{9,10... | collective-permute-start | bytes 3145736 | tf_op jit(solution)/shard_map/ppermute | solution.py:275
  32.0 22.8 %collective-permute-start.12 = (bf16[8,512,128]{2,1,0:T(8,128)(2,1)S(1)}, bf16[8,512,128]{2,1,0:T(8,128)(2,1)S(1)}, u32[]{:S(2)}, u32[]{:S(2)}) collective-permute-start(bf16[8,512,128]{2,1,0:T(8,128)(2,1)S(1)} %get-tuple-element.57.refs_5_), channel_id=1, source_target_pairs={{1,0},{2,1},{3,2},{0,3},{5,4},{6,5},{7,6},{4,7},{9,8},{10,9},{11,1... | collective-permute-start | bytes 3145736 | tf_op jit(solution)/shard_map/ppermute | solution.py:275
  58.4 12.5 %collective-permute-start.20 = (bf16[4,512,128]{2,1,0:T(8,128)(2,1)}, bf16[4,512,128]{2,1,0:T(8,128)(2,1)}, u32[]{:S(2)}, u32[]{:S(2)}) collective-permute-start(bf16[4,512,128]{2,1,0:T(8,128)(2,1)} %slice.55), channel_id=1, source_target_pairs={{3,0},{0,1},{1,2},{2,3},{7,4},{4,5},{5,6},{6,7},{11,8},{8,9},{9,10... | collective-permute-start | bytes 1572872 | tf_op jit(solution)/shard_map/ppermute | solution.py:275
  59.5 11.4 %collective-permute-start.19 = (bf16[4,512,128]{2,1,0:T(8,128)(2,1)}, bf16[4,512,128]{2,1,0:T(8,128)(2,1)}, u32[]{:S(2)}, u32[]{:S(2)}) collective-permute-start(bf16[4,512,128]{2,1,0:T(8,128)(2,1)} %slice.54), channel_id=1, source_target_pairs={{1,0},{2,1},{3,2},{0,3},{5,4},{6,5},{7,6},{4,7},{9,8},{10,9},{11,1... | collective-permute-start | bytes 1572872 | tf_op jit(solution)/shard_map/ppermute | solution.py:275
  61.6 10.7 %collective-permute-start.18 = (bf16[4,512,128]{2,1,0:T(8,128)(2,1)}, bf16[4,512,128]{2,1,0:T(8,128)(2,1)}, u32[]{:S(2)}, u32[]{:S(2)}) collective-permute-start(bf16[4,512,128]{2,1,0:T(8,128)(2,1)} %slice.53), channel_id=1, source_target_pairs={{12,0},{13,1},{14,2},{15,3},{0,4},{1,5},{2,6},{3,7},{4,8},{5,9},{6... | collective-permute-start | bytes 1572872 | tf_op jit(solution)/shard_map/ppermute | solution.py:275
  61.6 10.7 %collective-permute-start.17 = (bf16[4,512,128]{2,1,0:T(8,128)(2,1)}, bf16[4,512,128]{2,1,0:T(8,128)(2,1)}, u32[]{:S(2)}, u32[]{:S(2)}) collective-permute-start(bf16[4,512,128]{2,1,0:T(8,128)(2,1)} %slice.52), channel_id=1, source_target_pairs={{4,0},{5,1},{6,2},{7,3},{8,4},{9,5},{10,6},{11,7},{12,8},{13,9},{1... | collective-permute-start | bytes 1572872 | tf_op jit(solution)/shard_map/ppermute | solution.py:275
  67.0 77.7 %collective-permute-start.16 = (bf16[16,512,128]{2,1,0:T(8,128)(2,1)S(1)}, bf16[16,512,128]{2,1,0:T(8,128)(2,1)S(1)}, u32[]{:S(2)}, u32[]{:S(2)}) collective-permute-start(bf16[16,512,128]{2,1,0:T(8,128)(2,1)S(1)} %shard_map.102.tiles_ref), channel_id=1, source_target_pairs={{16,0},{0,16},{48,32},{32,48},{80,64},{64,80},{112,96},{96,112},{1... | collective-permute-start | bytes 6291464 | tf_op jit(solution)/shard_map/ppermute | solution.py:288
  82.6 24.9 %collective-permute-start.29 = (s16[8,528,128]{2,1,0:T(8,128)(2,1)S(1)}, s16[8,528,128]{2,1,0:T(8,128)(2,1)S(1)}, u32[]{:S(2)}, u32[]{:S(2)}) collective-permute-start(s16[8,528,128]{2,1,0:T(8,128)(2,1)S(1)} %get-tuple-element.78), channel_id=1, source_target_pairs={{12,0},{13,1},{14,2},{15,3},{0,4},{1,5},{2,6},{3,7},{4,8},{5,9},{6... | collective-permute-start | bytes 3244040 | tf_op jit(solution)/shard_map/ppermute | solution.py:275
  82.9 24.6 %collective-permute-start.30 = (s16[8,528,128]{2,1,0:T(8,128)(2,1)S(1)}, s16[8,528,128]{2,1,0:T(8,128)(2,1)S(1)}, u32[]{:S(2)}, u32[]{:S(2)}) collective-permute-start(s16[8,528,128]{2,1,0:T(8,128)(2,1)S(1)} %get-tuple-element.79), channel_id=1, source_target_pairs={{4,0},{5,1},{6,2},{7,3},{8,4},{9,5},{10,6},{11,7},{12,8},{13,9},{1... | collective-permute-start | bytes 3244040 | tf_op jit(solution)/shard_map/ppermute | solution.py:275
  92.4 24.1 %collective-permute-start.21 = (s16[8,528,128]{2,1,0:T(8,128)(2,1)S(1)}, s16[8,528,128]{2,1,0:T(8,128)(2,1)S(1)}, u32[]{:S(2)}, u32[]{:S(2)}) collective-permute-start(s16[8,528,128]{2,1,0:T(8,128)(2,1)S(1)} %get-tuple-element.69), channel_id=1, source_target_pairs={{3,0},{0,1},{1,2},{2,3},{7,4},{4,5},{5,6},{6,7},{11,8},{8,9},{9,10... | collective-permute-start | bytes 3244040 | tf_op jit(solution)/shard_map/ppermute | solution.py:275
  93.2 23.3 %collective-permute-start.22 = (s16[8,528,128]{2,1,0:T(8,128)(2,1)S(1)}, s16[8,528,128]{2,1,0:T(8,128)(2,1)S(1)}, u32[]{:S(2)}, u32[]{:S(2)}) collective-permute-start(s16[8,528,128]{2,1,0:T(8,128)(2,1)S(1)} %get-tuple-element.70), channel_id=1, source_target_pairs={{1,0},{2,1},{3,2},{0,3},{5,4},{6,5},{7,6},{4,7},{9,8},{10,9},{11,1... | collective-permute-start | bytes 3244040 | tf_op jit(solution)/shard_map/ppermute | solution.py:275
  108.2 12.3 %collective-permute-start.31 = (s16[4,528,128]{2,1,0:T(8,128)(2,1)S(1)}, s16[4,528,128]{2,1,0:T(8,128)(2,1)S(1)}, u32[]{:S(2)}, u32[]{:S(2)}) collective-permute-start(s16[4,528,128]{2,1,0:T(8,128)(2,1)S(1)} %get-tuple-element.80), channel_id=1, source_target_pairs={{12,0},{13,1},{14,2},{15,3},{0,4},{1,5},{2,6},{3,7},{4,8},{5,9},{6... | collective-permute-start | bytes 1622024 | tf_op jit(solution)/shard_map/ppermute | solution.py:275
  108.2 12.3 %collective-permute-start.32 = (s16[4,528,128]{2,1,0:T(8,128)(2,1)S(1)}, s16[4,528,128]{2,1,0:T(8,128)(2,1)S(1)}, u32[]{:S(2)}, u32[]{:S(2)}) collective-permute-start(s16[4,528,128]{2,1,0:T(8,128)(2,1)S(1)} %get-tuple-element.81), channel_id=1, source_target_pairs={{4,0},{5,1},{6,2},{7,3},{8,4},{9,5},{10,6},{11,7},{12,8},{13,9},{1... | collective-permute-start | bytes 1622024 | tf_op jit(solution)/shard_map/ppermute | solution.py:275
  117.2 14.5 %collective-permute-start.23 = (s16[4,528,128]{2,1,0:T(8,128)(2,1)S(1)}, s16[4,528,128]{2,1,0:T(8,128)(2,1)S(1)}, u32[]{:S(2)}, u32[]{:S(2)}) collective-permute-start(s16[4,528,128]{2,1,0:T(8,128)(2,1)S(1)} %get-tuple-element.71), channel_id=1, source_target_pairs={{3,0},{0,1},{1,2},{2,3},{7,4},{4,5},{5,6},{6,7},{11,8},{8,9},{9,10... | collective-permute-start | bytes 1622024 | tf_op jit(solution)/shard_map/ppermute | solution.py:275
  117.4 14.3 %collective-permute-start.24 = (s16[4,528,128]{2,1,0:T(8,128)(2,1)S(1)}, s16[4,528,128]{2,1,0:T(8,128)(2,1)S(1)}, u32[]{:S(2)}, u32[]{:S(2)}) collective-permute-start(s16[4,528,128]{2,1,0:T(8,128)(2,1)S(1)} %get-tuple-element.72), channel_id=1, source_target_pairs={{1,0},{2,1},{3,2},{0,3},{5,4},{6,5},{7,6},{4,7},{9,8},{10,9},{11,1... | collective-permute-start | bytes 1622024 | tf_op jit(solution)/shard_map/ppermute | solution.py:275
  121.4 14.5 %collective-permute-start.33 = (s16[2,528,128]{2,1,0:T(8,128)(2,1)S(1)}, s16[2,528,128]{2,1,0:T(8,128)(2,1)S(1)}, u32[]{:S(2)}, u32[]{:S(2)}) collective-permute-start(s16[2,528,128]{2,1,0:T(8,128)(2,1)S(1)} %get-tuple-element.83), channel_id=1, source_target_pairs={{3,0},{0,1},{1,2},{2,3},{7,4},{4,5},{5,6},{6,7},{11,8},{8,9},{9,10... | collective-permute-start | bytes 811016 | tf_op jit(solution)/shard_map/ppermute | solution.py:275
  121.5 14.4 %collective-permute-start.34 = (s16[2,528,128]{2,1,0:T(8,128)(2,1)S(1)}, s16[2,528,128]{2,1,0:T(8,128)(2,1)S(1)}, u32[]{:S(2)}, u32[]{:S(2)}) collective-permute-start(s16[2,528,128]{2,1,0:T(8,128)(2,1)S(1)} %get-tuple-element.84), channel_id=1, source_target_pairs={{1,0},{2,1},{3,2},{0,3},{5,4},{6,5},{7,6},{4,7},{9,8},{10,9},{11,1... | collective-permute-start | bytes 811016 | tf_op jit(solution)/shard_map/ppermute | solution.py:275
  136.1 10.4 %collective-permute-start.35 = (s16[1,528,128]{2,1,0:T(8,128)(2,1)S(1)}, s16[1,528,128]{2,1,0:T(8,128)(2,1)S(1)}, u32[]{:S(2)}, u32[]{:S(2)}) collective-permute-start(s16[1,528,128]{2,1,0:T(8,128)(2,1)S(1)} %get-tuple-element.85), channel_id=1, source_target_pairs={{3,0},{0,1},{1,2},{2,3},{7,4},{4,5},{5,6},{6,7},{11,8},{8,9},{9,10... | collective-permute-start | bytes 405512 | tf_op jit(solution)/shard_map/ppermute | solution.py:275
  (36 other events, 249.1 us)

commit v3 on v2

--- a/solution.py
+++ b/solution.py
@@ -9,10 +9,12 @@
 ROWS = 512
 TILE = 128
 TILES = 64
+EARLY = 48
 SIDE = 4
 PAD = 16
 ENTRIES = 224
 UNROLL = 8
+CODE_UNROLL = 2
 HALF_RANGE = 14.9
 NEAR = {0: 0, 1: 1, 3: 2, 2: 3}
 
@@ -25,8 +27,9 @@
     for dy in range(SIDE):
         for dz in range(SIDE):
             for t in range(2):
-                table[dy, dz, t] = NEAR[dy] * 8 + NEAR[dz] * 2 + t
-                table[dy, dz, t + 2] = 32 + NEAR[dz] * 8 + NEAR[dy] * 2 + t
+                for half, (first, second, tile) in enumerate(((dz, dy, t), (dy, dz, t + 2))):
+                    row = EARLY + 8 * half if second == 2 else 24 * half + NEAR[second] * 8
+                    table[dy, dz, tile] = row + NEAR[first] * 2 + t
     return table.reshape(-1)
 
 
@@ -61,23 +64,24 @@
     return (dy * SIDE + dz) * 4 + (tile & 3)
 
 
-def work_list(source, target):
+def work_list(source, target, late):
+    member = (source >= EARLY) == late
     count = source.shape[0]
     order = jnp.arange(count, dtype=jnp.int32)
     ids = jnp.arange(TILES, dtype=jnp.int32)
-    same = target[:, None] == ids[None, :]
+    same = (target[:, None] == ids[None, :]) & member[:, None]
     held = jnp.sum(same, axis=0, dtype=jnp.int32)
-    before = jnp.sum((target[None, :] == target[:, None]) & (order[None, :] < order[:, None]), axis=1, dtype=jnp.int32)
+    before = jnp.sum((target[None, :] == target[:, None]) & (order[None, :] < order[:, None]) & member[None, :], axis=1, dtype=jnp.int32)
     entries = jnp.maximum((held + 1) // 2, 1)
     start = jnp.sum(jnp.where(ids[None, :] < ids[:, None], entries[None, :], 0), axis=1)
     mine = jnp.sum(jnp.where(same, start[None, :], 0), axis=1)
-    slot = (mine + before // 2) * 2 + before % 2
-    value = source + (order << 6) + (1 << 15)
+    slot = jnp.where(member, (mine + before // 2) * 2 + before % 2, -1)
+    value = source - EARLY * late + (order << 6) + (1 << 15)
     slots = jnp.arange(2 * ENTRIES, dtype=jnp.int32)
     tiles = jnp.sum(jnp.where(slot[:, None] == slots[None, :], value[:, None], 0), axis=0)
     at = jnp.arange(ENTRIES, dtype=jnp.int32)
     owner = jnp.sum(start[None, :] <= at[:, None], axis=1, dtype=jnp.int32) - 1
-    fresh = jnp.sum(start[None, :] == at[:, None], axis=1, dtype=jnp.int32)
+    fresh = (at == jnp.sum(jnp.where(owner[:, None] == ids[None, :], start[None, :], 0), axis=1)).astype(jnp.int32)
     bounds = jnp.concatenate([start, jnp.sum(entries)[None]])
     return tiles, owner * 2 + fresh, bounds
 
@@ -108,7 +112,7 @@
     return jax.ShapeDtypeStruct((n, ROWS, TILE), jnp.float32)
 
 
-def kernel(body, outs, specs, scratch=(), grant=4):
+def kernel(body, outs, specs, scratch=(), grant=3):
     return pl.pallas_call(
         body,
         out_shape=outs,
@@ -119,47 +123,56 @@
     )
 
 
-def ladder(tiles, owner, bounds, amps, integrals, first, count, send):
-    def body(tiles_ref, owner_ref, bounds_ref, amps_ref, ints_ref, *rest):
-        sums = rest[-1] if send else rest[0]
-        begin = bounds_ref[first]
-        end = bounds_ref[first + count]
-
-        def step(i, carry):
-            for k in range(UNROLL):
-                at = begin + i * UNROLL + k
-                inside = at < end
-                at = jnp.minimum(at, ENTRIES - 1)
-                left = tiles_ref[2 * at]
-                right = tiles_ref[2 * at + 1]
-                mark = owner_ref[at]
-                place = jnp.where(inside, (mark >> 1) - first, count - 1)
-                fresh = jnp.logical_and(inside, (mark & 1) == 1)
-                keep_left = jnp.where(inside, left >> 15, 0).astype(jnp.float32).astype(jnp.bfloat16)
-                keep_right = jnp.where(inside, right >> 15, 0).astype(jnp.float32).astype(jnp.bfloat16)
-                weights = jnp.concatenate(
-                    [ints_ref[(left >> 6) & 511] * keep_left, ints_ref[(right >> 6) & 511] * keep_right], axis=0
-                )
-                values = jnp.concatenate([amps_ref[left & 63], amps_ref[right & 63]], axis=1)
-                product = jnp.dot(values, weights, preferred_element_type=jnp.float32)
-                sums[place] = product + jnp.where(fresh, 0.0, sums[place])
-            return carry
-
-        lax.fori_loop(0, (end - begin + UNROLL - 1) // UNROLL, step, 0)
-        if send:
+def ladder(parts, integrals, first, count, so_far=None):
+    def body(*refs):
+        ints_ref = refs[4 * len(parts)]
+        rest = refs[4 * len(parts) + 1 :]
+        sums = rest[-1]
+        for p in range(len(parts)):
+            tiles_ref, owner_ref, bounds_ref, amps_ref = refs[4 * p : 4 * p + 4]
+            begin = bounds_ref[first]
+            end = bounds_ref[first + count]
+            starts = p == 0
+
+            def step(i, carry):
+                for k in range(UNROLL):
+                    at = begin + i * UNROLL + k
+                    inside = at < end
+                    at = jnp.minimum(at, ENTRIES - 1)
+                    left = tiles_ref[2 * at]
+                    right = tiles_ref[2 * at + 1]
+                    mark = owner_ref[at]
+                    place = jnp.where(inside, (mark >> 1) - first, count - 1)
+                    keep_left = jnp.where(inside, left >> 15, 0).astype(jnp.float32).astype(jnp.bfloat16)
+                    keep_right = jnp.where(inside, right >> 15, 0).astype(jnp.float32).astype(jnp.bfloat16)
+                    weights = jnp.concatenate(
+                        [ints_ref[(left >> 6) & 511] * keep_left, ints_ref[(right >> 6) & 511] * keep_right], axis=0
+                    )
+                    values = jnp.concatenate([amps_ref[left & 63], amps_ref[right & 63]], axis=1)
+                    product = jnp.dot(values, weights, preferred_element_type=jnp.float32)
+                    before = sums[place]
+                    if starts:
+                        before = jnp.where(jnp.logical_and(inside, (mark & 1) == 1), 0.0, before)
+                    sums[place] = product + before
+                return carry
+
+            lax.fori_loop(0, (end - begin + UNROLL - 1) // UNROLL, step, 0)
+        if so_far is not None:
             half = count // 2
 
             def code(k, carry):
-                put(rest[0], k, sums[k])
-                put(rest[1], k, sums[k + half])
+                put(rest[1], k, sums[k] + rest[0][k])
+                put(rest[2], k, sums[k + half] + rest[0][k + half])
                 return carry
 
-            lax.fori_loop(0, half, code, 0)
-
-    outs = (coded(count // 2), coded(count // 2)) if send else (plain(count),)
-    scratch = [pltpu.VMEM((count, ROWS, TILE), jnp.float32)] if send else []
-    specs = [SMEM_SPEC] * 3 + [VMEM_SPEC] * 2
-    return kernel(body, outs, specs, scratch, 8)(tiles, owner, bounds, amps, integrals)
+            lax.fori_loop(0, half, code, 0, unroll=CODE_UNROLL)
+
+    args = [value for work, amps in parts for value in (*work, amps)] + [integrals]
+    specs = ([SMEM_SPEC] * 3 + [VMEM_SPEC]) * len(parts) + [VMEM_SPEC]
+    if so_far is None:
+        return kernel(body, plain(count), specs)(*args)
+    sums = pltpu.VMEM((count, ROWS, TILE), jnp.float32)
+    return kernel(body, (coded(count // 2),) * 2, specs + [VMEM_SPEC], (sums,), 7)(*args, so_far)
 
 
 def masked_tiles(t2, t2_live):
@@ -208,25 +221,25 @@
     return kernel(body, out, [SMEM_SPEC] + [VMEM_SPEC] * (len(args) - 1))(*args)
 
 
-def merge(sums, got_up, got_down, base):
+def merge(sums, got_up, got_down):
     def body(sums_ref, up_ref, down_ref, up_out, down_out):
         def step(k, carry):
-            put(up_out, k, sums_ref[base + k] + get(up_ref, k))
-            put(down_out, k, sums_ref[base + 4 + k] + get(down_ref, k))
+            put(up_out, k, sums_ref[k] + get(up_ref, k))
+            put(down_out, k, sums_ref[4 + k] + get(down_ref, k))
             return carry
 
-        lax.fori_loop(0, 4, step, 0)
+        lax.fori_loop(0, 4, step, 0, unroll=CODE_UNROLL)
 
     return kernel(body, (coded(4), coded(4)), [VMEM_SPEC] * 3)(sums, got_up, got_down)
 
 
-def row_sum(sums, got_up, got_down, last_up, last_down, base):
+def row_sum(sums, got_up, got_down, last_up, last_down):
     def body(sums_ref, up_ref, down_ref, last_up_ref, last_down_ref, up_out, down_out, kept):
         def low(k):
-            return sums_ref[base + 8 + k] + get(down_ref, 4 + k) + get(last_up_ref, k)
+            return sums_ref[8 + k] + get(down_ref, 4 + k) + get(last_up_ref, k)
 
         def high(k):
-            return sums_ref[base + 12 + k] + get(up_ref, 4 + k) + get(last_down_ref, k)
+            return sums_ref[12 + k] + get(up_ref, 4 + k) + get(last_down_ref, k)
 
         put(up_out, 0, low(2))
         put(up_out, 1, high(1))
@@ -301,44 +314,61 @@
 
     source = pick(source_table(), relative(int_tiles[:, 0], y, z))
     target = pick(target_table(), relative(int_tiles[:, 1], y, z))
-    work = work_list(source, target)
 
     low, high = own[:2], own[2:]
     near_x = both(own, along_x)
-    near_low, near_high, work = lax.optimization_barrier((both(low, along_z), both(high, along_y), work))
-    over_low, over_high, near_x = lax.optimization_barrier((far(near_low, along_z), far(near_high, along_y), near_x))
-    low, high = join((low, *near_low, *over_low), (high, *near_high, *over_high))
-    near_low, near_high, over_x = lax.optimization_barrier(
-        (both(low, along_y), both(high, along_z), far(near_x, along_x))
-    )
-    over_low, over_high = far(near_low, along_y), far(near_high, along_z)
+    near_low, near_high, work_1, blocks_1, blocks_2 = lax.optimization_barrier(
+        (both(low, along_z), both(high, along_y), work_list(source, target, False), blocks(0), blocks(1))
+    )
+    low_1, high_1 = join((low, near_low[0]), (high, near_high[0]))
+    near_low_1, near_high_1 = both(low_1, along_y), both(high_1, along_z)
+    over_low, over_high, near_x, work_2 = lax.optimization_barrier(
+        (far(near_low, along_z), far(near_high, along_y), near_x, work_list(source, target, True))
+    )
+    low_2, high_2 = join((near_low[1], *over_low), (near_high[1], *over_high))
+    near_low_2, near_high_2 = both(low_2, along_y), both(high_2, along_z)
+    near_low_1, near_high_1, over_x = lax.optimization_barrier((near_low_1, near_high_1, far(near_x, along_x)))
+    far_low_1, far_high_1 = along_y(near_low_1[0], 1), along_z(near_high_1[0], 1)
+    near_low_2, near_high_2 = lax.optimization_barrier((near_low_2, near_high_2))
+    far_low_2, far_high_2 = along_y(near_low_2[1], 3), along_z(near_high_2[1], 3)
+
+
     (mine,) = join((own, *near_x, *over_x))
     other = along_x(mine, 0, 1)
-    cycle = cycle_part(blocks(0), cycle_w, mine)
-    (amps,) = join((low, *near_low, *over_low, high, *near_high, *over_high))
-    amps, cycle = lax.optimization_barrier((amps, cycle))
-    cycle = cycle_part(blocks(1), cycle_w, other, cycle)
-
-    send_a = ladder(*work, amps, integrals, 0, 16, True)
-    send_b = ladder(*work, amps, integrals, 16, 16, True)
+    (amps,) = join(
+        (low_1, low_2, near_low_1[0], near_low_2[0], near_low_1[1], near_low_2[1])
+        + (high_1, high_2, near_high_1[0], near_high_2[0], near_high_1[1], near_high_2[1])
+    )
+    sums_a = ladder([(work_1, amps)], integrals, 0, 16)
+    sums_b = ladder([(work_1, amps)], integrals, 16, 16)
+    sums_a, sums_b, *arrived = lax.optimization_barrier(
+        (sums_a, sums_b, far_low_1, far_low_2, far_high_1, far_high_2)
+    )
+    (rest,) = join(arrived)
+    send_a = ladder([(work_2, rest)], integrals, 0, 16, sums_a)
+    send_b = ladder([(work_2, rest)], integrals, 16, 16, sums_b)
 
     def first_hop(send, axis):
         return axis(send[0], 3), axis(send[1], 1)
 
     got_a = first_hop(send_a, along_z)
     got_b = first_hop(send_b, along_y)
-    (sums,) = ladder(*work, amps, integrals, 32, 32, False)
-
-    def reduce(got, axis, other, base):
-        on = merge(sums, *got, base)
+    parts = [(work_1, amps), (work_2, rest)]
+    sums_a = ladder(parts, integrals, 32, 16)
+    sums_b = ladder(parts, integrals, 48, 16)
+    cycle = cycle_part(blocks_2, cycle_w, other, cycle_part(blocks_1, cycle_w, mine))
+    got_b, cycle = lax.optimization_barrier((got_b, cycle))
+
+    def reduce(sums, got, axis, other):
+        on = merge(sums, *got)
         last = first_hop(on, axis)
-        up, down, kept = row_sum(sums, *got, *last, base)
+        up, down, kept = row_sum(sums, *got, *last)
         got = first_hop((up, down), other)
         last = first_hop(merge_last(kept, *got), other)
         return (kept, *got, *last)
 
-    half_a = reduce(got_a, along_z, along_y, 0)
-    half_b = reduce(got_b, along_y, along_z, 16)
+    half_a = reduce(sums_a, got_a, along_z, along_y)
+    half_b = reduce(sums_b, got_b, along_y, along_z)
     return finish(res_live, cycle, half_a, half_b)
 
 

time: 150 us -> 139 us (0.927)
  waiting for transfers between devices: 40 us -> 29.9 us
  local copies, waits for them, and re-layouts: 11.9 us -> 1.88 us
  Pallas kernels: 33.8 us -> 41.2 us
  other arithmetic: 2.34 us -> 4.23 us
    ppermute x5, waiting for transfers between devices: 12.4 us -> 0.01 us  [along_x(): return lax.ppermute(value, 'pair', pairs)]
    pallas_call x3 -> x6, Pallas kernels: 21.9 us -> 30.9 us  [the longest x4 22.7 us: ladder(): return kernel(body, plain(count), specs)(*args)]
    unnamed x46 -> x22, local copies, waits for them, and re-layouts: 8.29 us -> 1.76 us
    slice x10 -> x6, local copies, waits for them, and re-layouts: 3.57 us -> 0.08 us  [far(): return (axis(up[:n], 1), axis(down[n:], 3))]
    ppermute x32 -> x36, starting transfers between devices: 56.1 us -> 53.1 us  [take(): return lax.ppermute(value, 'ints', pairs)]
    ppermute x32 -> x36, waiting for transfers between devices: 27.6 us -> 29.9 us  [take(): return lax.ppermute(value, 'ints', pairs)]
    ppermute x5, starting transfers between devices: 5 us -> 7.35 us  [along_x(): return lax.ppermute(value, 'pair', pairs)]
    pallas_call x3 -> x5, Pallas kernels: 2.33 us -> 0.82 us  [join(): return kernel(body, outs, [VMEM_SPEC] * len(flat))(*flat)]
  transfers between devices with their start and end apart: 37 -> 41, of which waited for: 14 -> 16; matrix products, arithmetic and copies ran while one was open for 2% -> 3% of each run, Pallas kernels for 21% -> 28%
where the time goes in v3:
time: 139 us; the launch traced here: 138 us
  starting transfers between devices  60.5 us (44%)
  Pallas kernels  41.2 us (30%)
  waiting for transfers between devices  29.9 us (22%)
  other arithmetic  4.23 us (3%)
  local copies, waits for them, and re-layouts  1.88 us (1%)
    ppermute x36, starting transfers between devices, take(): return lax.ppermute(value, 'ints', pairs)  53.1 us
    ppermute x36, waiting for transfers between devices, take(): return lax.ppermute(value, 'ints', pairs)  29.9 us
    pallas_call x4, Pallas kernels, ladder(): return kernel(body, plain(count), specs)(*args)  22.7 us
    pallas_call x2, Pallas kernels, ladder(): kernel(body, (coded(count // 2),) * 2, specs + [VMEM_SPEC], (sums,), 7)  8.15 us
    ppermute x5, starting transfers between devices, along_x(): return lax.ppermute(value, 'pair', pairs)  7.35 us
    pallas_call x2, Pallas kernels, cycle_part(): return kernel(body, out, [SMEM_SPEC] + [VMEM_SPEC] * (len(args) - 1))(*args)  3.6 us
  transfers between devices with their start and end apart: 41, of which 16 were waited for; matrix products, arithmetic and copies ran while one was open for 3% of the time, Pallas kernels for 28%

profile of v3, /device:TPU:0, one launch (start us, length us, event | category | flops | bytes accessed | tf_op | source)
XLA Modules:
  0.0 138.2 jit_solution(15779225739369680094)
XLA Ops:
  16.9 2.9 %collective-permute-start.6 = (bf16[1,512,128]{2,1,0:T(8,128)(2,1)S(1)}, bf16[1,512,128]{2,1,0:T(8,128)(2,1)S(1)}, u32[]{:S(2)}, u32[]{:S(2)}) collective-permute-start(bf16[1,512,128]{2,1,0:T(8,128)(2,1)S(1)} %slice.36), channel_id=1, source_target_pairs={{4,0},{5,1},{6,2},{7,3},{8,4},{9,5},{10,6},{11,7},{12,8},{13,9},{1... | collective-permute-start | bytes 393224 | tf_op jit(solution)/shard_map/ppermute | solution.py:288
  26.1 2.4 %collective-permute-start.10 = (bf16[4,512,128]{2,1,0:T(8,128)(2,1)S(1)}, bf16[4,512,128]{2,1,0:T(8,128)(2,1)S(1)}, u32[]{:S(2)}, u32[]{:S(2)}) collective-permute-start(bf16[4,512,128]{2,1,0:T(8,128)(2,1)S(1)} %get-tuple-element.74.refs_0_), channel_id=1, source_target_pairs={{4,0},{5,1},{6,2},{7,3},{8,4},{9,5},{10,6},{11,7},{12,8},{13,9},{1... | collective-permute-start | bytes 1572872 | tf_op jit(solution)/shard_map/ppermute | solution.py:288
  28.6 3.2 %collective-permute-start.12 = (bf16[4,512,128]{2,1,0:T(8,128)(2,1)S(1)}, bf16[4,512,128]{2,1,0:T(8,128)(2,1)S(1)}, u32[]{:S(2)}, u32[]{:S(2)}) collective-permute-start(bf16[4,512,128]{2,1,0:T(8,128)(2,1)S(1)} %get-tuple-element.80.refs_6_), channel_id=1, source_target_pairs={{1,0},{2,1},{3,2},{0,3},{5,4},{6,5},{7,6},{4,7},{9,8},{10,9},{11,1... | collective-permute-start | bytes 1572872 | tf_op jit(solution)/shard_map/ppermute | solution.py:288
  34.1 3.5 %collective-permute-done.11.refs_4_ = bf16[4,512,128]{2,1,0:T(8,128)(2,1)S(1)} collective-permute-done((bf16[4,512,128]{2,1,0:T(8,128)(2,1)S(1)}, bf16[4,512,128]{2,1,0:T(8,128)(2,1)S(1)}, u32[]{:S(2)}, u32[]{:S(2)}) %collective-permute-start.11) | collective-permute-done | bytes 524320 | tf_op jit(solution)/shard_map/ppermute | solution.py:288
  37.6 2.5 %collective-permute-start.14 = (bf16[2,512,128]{2,1,0:T(8,128)(2,1)S(1)}, bf16[2,512,128]{2,1,0:T(8,128)(2,1)S(1)}, u32[]{:S(2)}, u32[]{:S(2)}) collective-permute-start(bf16[2,512,128]{2,1,0:T(8,128)(2,1)S(1)} %slice.38), channel_id=1, source_target_pairs={{32,0},{48,16},{64,32},{80,48},{96,64},{112,80},{0,96},{16,112},{3... | collective-permute-start | bytes 786440 | tf_op jit(solution)/shard_map/ppermute | solution.py:301
  40.6 2.8 %collective-permute-start.16 = (bf16[4,512,128]{2,1,0:T(8,128)(2,1)S(1)}, bf16[4,512,128]{2,1,0:T(8,128)(2,1)S(1)}, u32[]{:S(2)}, u32[]{:S(2)}) collective-permute-start(bf16[4,512,128]{2,1,0:T(8,128)(2,1)S(1)} %get-tuple-element.79.refs_1_), channel_id=1, source_target_pairs={{4,0},{5,1},{6,2},{7,3},{8,4},{9,5},{10,6},{11,7},{12,8},{13,9},{1... | collective-permute-start | bytes 1572872 | tf_op jit(solution)/shard_map/ppermute | solution.py:288
  43.5 3.2 %collective-permute-start.18 = (bf16[4,512,128]{2,1,0:T(8,128)(2,1)S(1)}, bf16[4,512,128]{2,1,0:T(8,128)(2,1)S(1)}, u32[]{:S(2)}, u32[]{:S(2)}) collective-permute-start(bf16[4,512,128]{2,1,0:T(8,128)(2,1)S(1)} %get-tuple-element.84.refs_7_), channel_id=1, source_target_pairs={{1,0},{2,1},{3,2},{0,3},{5,4},{6,5},{7,6},{4,7},{9,8},{10,9},{11,1... | collective-permute-start | bytes 1572872 | tf_op jit(solution)/shard_map/ppermute | solution.py:288
  47.0 4.5 %collective-permute-done.17.refs_5_ = bf16[4,512,128]{2,1,0:T(8,128)(2,1)S(1)} collective-permute-done((bf16[4,512,128]{2,1,0:T(8,128)(2,1)S(1)}, bf16[4,512,128]{2,1,0:T(8,128)(2,1)S(1)}, u32[]{:S(2)}, u32[]{:S(2)}) %collective-permute-start.17) | collective-permute-done | bytes 524320 | tf_op jit(solution)/shard_map/ppermute | solution.py:288
  55.3 3.6 %collective-permute-done.18.refs_9_ = bf16[4,512,128]{2,1,0:T(8,128)(2,1)S(1)} collective-permute-done((bf16[4,512,128]{2,1,0:T(8,128)(2,1)S(1)}, bf16[4,512,128]{2,1,0:T(8,128)(2,1)S(1)}, u32[]{:S(2)}, u32[]{:S(2)}) %collective-permute-start.18) | collective-permute-done | bytes 524320 | tf_op jit(solution)/shard_map/ppermute | solution.py:288
  59.4 4.8 %shard_map.105.refs_5_ = f32[16,512,128]{2,1,0:T(8,128)S(1)} custom-call(s32[448]{0:T(512)S(1)} %select_reduce_fusion.1.refs_0_, s32[224]{0:T(256)S(1)} %fusion.15.refs_1_, s32[65]{0:T(128)S(1)} %pad_add_fusion.refs_2_, bf16[48,512,128]{2,1,0:T(8,128)(2,1)S(1)} %shard_map.103.refs_3_, bf16[320,128,128]{2,1,0:T(8,128)(2,1)S(1)} %bitcast.3), custom_call_target="tpu_custom_call" | custom-call | tf_op jit(solution)/shard_map/pallas_call | solution.py:173
  64.2 4.6 %shard_map.104.refs_5_ = f32[16,512,128]{2,1,0:T(8,128)S(1)} custom-call(s32[448]{0:T(512)S(1)} %select_reduce_fusion.1.refs_0_, s32[224]{0:T(256)S(1)} %fusion.15.refs_1_, s32[65]{0:T(128)S(1)} %pad_add_fusion.refs_2_, bf16[48,512,128]{2,1,0:T(8,128)(2,1)S(1)} %shard_map.103.refs_3_, bf16[320,128,128]{2,1,0:T(8,128)(2,1)S(1)} %bitcast.3), custom_call_target="tpu_custom_call" | custom-call | tf_op jit(solution)/shard_map/pallas_call | solution.py:173
  71.2 4.1 %shard_map.112 = (s16[8,528,128]{2,1,0:T(8,128)(2,1)S(1)}, s16[8,528,128]{2,1,0:T(8,128)(2,1)S(1)}) custom-call(s32[448]{0:T(512)S(1)} %select_reduce_fusion.refs_0_.refs_4_, s32[224]{0:T(256)S(1)} %fusion.16.refs_1_.refs_5_, s32[65]{0:T(128)S(1)} %pad_add_fusion.1.refs_2_.refs_6_, bf16[16,512,128]{2,1,0:T(8,128)(2,1)S(1)} %shard_map.106.refs_3_.refs_7_, ...), custom_call_target="tpu_custom_call" | custom-call | tf_op jit(solution)/shard_map/pallas_call | solution.py:175
  75.3 3.2 %collective-permute-start.28 = (s16[8,528,128]{2,1,0:T(8,128)(2,1)S(1)}, s16[8,528,128]{2,1,0:T(8,128)(2,1)S(1)}, u32[]{:S(2)}, u32[]{:S(2)}) collective-permute-start(s16[8,528,128]{2,1,0:T(8,128)(2,1)S(1)} %get-tuple-element.106), channel_id=1, source_target_pairs={{1,0},{2,1},{3,2},{0,3},{5,4},{6,5},{7,6},{4,7},{9,8},{10,9},{11,1... | collective-permute-start | bytes 3244040 | tf_op jit(solution)/shard_map/ppermute | solution.py:288
  78.6 4.1 %shard_map.107 = (s16[8,528,128]{2,1,0:T(8,128)(2,1)S(1)}, s16[8,528,128]{2,1,0:T(8,128)(2,1)S(1)}) custom-call(s32[448]{0:T(512)S(1)} %select_reduce_fusion.refs_0_.refs_4_, s32[224]{0:T(256)S(1)} %fusion.16.refs_1_.refs_5_, s32[65]{0:T(128)S(1)} %pad_add_fusion.1.refs_2_.refs_6_, bf16[16,512,128]{2,1,0:T(8,128)(2,1)S(1)} %shard_map.106.refs_3_.refs_7_, ...), custom_call_target="tpu_custom_call" | custom-call | tf_op jit(solution)/shard_map/pallas_call | solution.py:175
  82.7 4.4 %collective-permute-start.25 = (s16[8,528,128]{2,1,0:T(8,128)(2,1)S(1)}, s16[8,528,128]{2,1,0:T(8,128)(2,1)S(1)}, u32[]{:S(2)}, u32[]{:S(2)}) collective-permute-start(s16[8,528,128]{2,1,0:T(8,128)(2,1)S(1)} %get-tuple-element.98), channel_id=1, source_target_pairs={{4,0},{5,1},{6,2},{7,3},{8,4},{9,5},{10,6},{11,7},{12,8},{13,9},{1... | collective-permute-start | bytes 3244040 | tf_op jit(solution)/shard_map/ppermute | solution.py:288
  88.9 7.1 %shard_map.116.sums_ref = f32[16,512,128]{2,1,0:T(8,128)S(1)} custom-call(s32[448]{0:T(512)S(1)} %select_reduce_fusion.1.refs_0_, s32[224]{0:T(256)S(1)} %fusion.15.refs_1_, s32[65]{0:T(128)S(1)} %pad_add_fusion.refs_2_, bf16[48,512,128]{2,1,0:T(8,128)(2,1)S(1)} %shard_map.103.refs_3_, s32[448]{0:T(512)S(1)} %select_reduce_fusion.refs_0_.refs_4_, ...), custom_call_target="tpu_custom_call" | custom-call | tf_op jit(solution)/shard_map/pallas_call | solution.py:173
  96.0 6.3 %shard_map.111.sums_ref = f32[16,512,128]{2,1,0:T(8,128)S(1)} custom-call(s32[448]{0:T(512)S(1)} %select_reduce_fusion.1.refs_0_, s32[224]{0:T(256)S(1)} %fusion.15.refs_1_, s32[65]{0:T(128)S(1)} %pad_add_fusion.refs_2_, bf16[48,512,128]{2,1,0:T(8,128)(2,1)S(1)} %shard_map.103.refs_3_, s32[448]{0:T(512)S(1)} %select_reduce_fusion.refs_0_.refs_4_, ...), custom_call_target="tpu_custom_call" | custom-call | tf_op jit(solution)/shard_map/pallas_call | solution.py:173
  103.0 3.2 %collective-permute-start.30 = (s16[4,528,128]{2,1,0:T(8,128)(2,1)S(1)}, s16[4,528,128]{2,1,0:T(8,128)(2,1)S(1)}, u32[]{:S(2)}, u32[]{:S(2)}) collective-permute-start(s16[4,528,128]{2,1,0:T(8,128)(2,1)S(1)} %get-tuple-element.108), channel_id=1, source_target_pairs={{1,0},{2,1},{3,2},{0,3},{5,4},{6,5},{7,6},{4,7},{9,8},{10,9},{11,1... | collective-permute-start | bytes 1622024 | tf_op jit(solution)/shard_map/ppermute | solution.py:288
  108.8 3.2 %collective-permute-start.36 = (s16[4,528,128]{2,1,0:T(8,128)(2,1)S(1)}, s16[4,528,128]{2,1,0:T(8,128)(2,1)S(1)}, u32[]{:S(2)}, u32[]{:S(2)}) collective-permute-start(s16[4,528,128]{2,1,0:T(8,128)(2,1)S(1)} %get-tuple-element.117), channel_id=1, source_target_pairs={{4,0},{5,1},{6,2},{7,3},{8,4},{9,5},{10,6},{11,7},{12,8},{13,9},{1... | collective-permute-start | bytes 1622024 | tf_op jit(solution)/shard_map/ppermute | solution.py:288
  112.0 4.4 %collective-permute-done.29.last_up_ref = s16[4,528,128]{2,1,0:T(8,128)(2,1)S(1)} collective-permute-done((s16[4,528,128]{2,1,0:T(8,128)(2,1)S(1)}, s16[4,528,128]{2,1,0:T(8,128)(2,1)S(1)}, u32[]{:S(2)}, u32[]{:S(2)}) %collective-permute-start.29) | collective-permute-done | bytes 540704 | tf_op jit(solution)/shard_map/ppermute | solution.py:288
  117.4 3.2 %collective-permute-start.32 = (s16[2,528,128]{2,1,0:T(8,128)(2,1)S(1)}, s16[2,528,128]{2,1,0:T(8,128)(2,1)S(1)}, u32[]{:S(2)}, u32[]{:S(2)}) collective-permute-start(s16[2,528,128]{2,1,0:T(8,128)(2,1)S(1)} %get-tuple-element.111), channel_id=1, source_target_pairs={{4,0},{5,1},{6,2},{7,3},{8,4},{9,5},{10,6},{11,7},{12,8},{13,9},{1... | collective-permute-start | bytes 811016 | tf_op jit(solution)/shard_map/ppermute | solution.py:288
  122.6 2.4 %collective-permute-start.38 = (s16[2,528,128]{2,1,0:T(8,128)(2,1)S(1)}, s16[2,528,128]{2,1,0:T(8,128)(2,1)S(1)}, u32[]{:S(2)}, u32[]{:S(2)}) collective-permute-start(s16[2,528,128]{2,1,0:T(8,128)(2,1)S(1)} %get-tuple-element.120), channel_id=1, source_target_pairs={{1,0},{2,1},{3,2},{0,3},{5,4},{6,5},{7,6},{4,7},{9,8},{10,9},{11,1... | collective-permute-start | bytes 811016 | tf_op jit(solution)/shard_map/ppermute | solution.py:288
  126.2 2.4 %collective-permute-start.34 = (s16[1,528,128]{2,1,0:T(8,128)(2,1)S(1)}, s16[1,528,128]{2,1,0:T(8,128)(2,1)S(1)}, u32[]{:S(2)}, u32[]{:S(2)}) collective-permute-start(s16[1,528,128]{2,1,0:T(8,128)(2,1)S(1)} %get-tuple-element.113), channel_id=1, source_target_pairs={{4,0},{5,1},{6,2},{7,3},{8,4},{9,5},{10,6},{11,7},{12,8},{13,9},{1... | collective-permute-start | bytes 405512 | tf_op jit(solution)/shard_map/ppermute | solution.py:288
  133.0 2.9 %collective-permute-done.39.refs_8_ = s16[1,528,128]{2,1,0:T(8,128)(2,1)S(1)} collective-permute-done((s16[1,528,128]{2,1,0:T(8,128)(2,1)S(1)}, s16[1,528,128]{2,1,0:T(8,128)(2,1)S(1)}, u32[]{:S(2)}, u32[]{:S(2)}) %collective-permute-start.39) | collective-permute-done | bytes 135200 | tf_op jit(solution)/shard_map/ppermute | solution.py:288
  (134 shorter events, 48.9 us)
Async XLA Ops:
  2.4 12.3 %collective-permute-start.3 = (bf16[2,512,128]{2,1,0:T(8,128)(2,1)S(1)}, bf16[2,512,128]{2,1,0:T(8,128)(2,1)S(1)}, u32[]{:S(2)}, u32[]{:S(2)}) collective-permute-start(bf16[2,512,128]{2,1,0:T(8,128)(2,1)S(1)} %get-tuple-element.137.refs_2_), channel_id=1, source_target_pairs={{12,0},{13,1},{14,2},{15,3},{0,4},{1,5},{2,6},{3,7},{4,8},{5,9},{6... | collective-permute-start | bytes 786440 | tf_op jit(solution)/shard_map/ppermute | solution.py:288
  4.1 12.3 %collective-permute-start.2 = (bf16[2,512,128]{2,1,0:T(8,128)(2,1)S(1)}, bf16[2,512,128]{2,1,0:T(8,128)(2,1)S(1)}, u32[]{:S(2)}, u32[]{:S(2)}) collective-permute-start(bf16[2,512,128]{2,1,0:T(8,128)(2,1)S(1)} %get-tuple-element.137.refs_2_), channel_id=1, source_target_pairs={{4,0},{5,1},{6,2},{7,3},{8,4},{9,5},{10,6},{11,7},{12,8},{13,9},{1... | collective-permute-start | bytes 786440 | tf_op jit(solution)/shard_map/ppermute | solution.py:288
  9.8 18.7 %collective-permute-start.9 = (bf16[4,512,128]{2,1,0:T(8,128)(2,1)S(1)}, bf16[4,512,128]{2,1,0:T(8,128)(2,1)S(1)}, u32[]{:S(2)}, u32[]{:S(2)}) collective-permute-start(bf16[4,512,128]{2,1,0:T(8,128)(2,1)S(1)} %shard_map.100.refs_0_), channel_id=1, source_target_pairs={{96,0},{112,16},{0,32},{16,48},{32,64},{48,80},{64,96},{80,112},{9... | collective-permute-start | bytes 1572872 | tf_op jit(solution)/shard_map/ppermute | solution.py:301
  14.7 17.9 %collective-permute-start.8 = (bf16[4,512,128]{2,1,0:T(8,128)(2,1)S(1)}, bf16[4,512,128]{2,1,0:T(8,128)(2,1)S(1)}, u32[]{:S(2)}, u32[]{:S(2)}) collective-permute-start(bf16[4,512,128]{2,1,0:T(8,128)(2,1)S(1)} %shard_map.100.refs_0_), channel_id=1, source_target_pairs={{32,0},{48,16},{64,32},{80,48},{96,64},{112,80},{0,96},{16,112},{3... | collective-permute-start | bytes 1572872 | tf_op jit(solution)/shard_map/ppermute | solution.py:301
  25.0 12.7 %collective-permute-start.11 = (bf16[4,512,128]{2,1,0:T(8,128)(2,1)S(1)}, bf16[4,512,128]{2,1,0:T(8,128)(2,1)S(1)}, u32[]{:S(2)}, u32[]{:S(2)}) collective-permute-start(bf16[4,512,128]{2,1,0:T(8,128)(2,1)S(1)} %get-tuple-element.74.refs_0_), channel_id=1, source_target_pairs={{12,0},{13,1},{14,2},{15,3},{0,4},{1,5},{2,6},{3,7},{4,8},{5,9},{6... | collective-permute-start | bytes 1572872 | tf_op jit(solution)/shard_map/ppermute | solution.py:288
  26.1 14.0 %collective-permute-start.10 = (bf16[4,512,128]{2,1,0:T(8,128)(2,1)S(1)}, bf16[4,512,128]{2,1,0:T(8,128)(2,1)S(1)}, u32[]{:S(2)}, u32[]{:S(2)}) collective-permute-start(bf16[4,512,128]{2,1,0:T(8,128)(2,1)S(1)} %get-tuple-element.74.refs_0_), channel_id=1, source_target_pairs={{4,0},{5,1},{6,2},{7,3},{8,4},{9,5},{10,6},{11,7},{12,8},{13,9},{1... | collective-permute-start | bytes 1572872 | tf_op jit(solution)/shard_map/ppermute | solution.py:288
  28.5 12.1 %collective-permute-start.13 = (bf16[4,512,128]{2,1,0:T(8,128)(2,1)S(1)}, bf16[4,512,128]{2,1,0:T(8,128)(2,1)S(1)}, u32[]{:S(2)}, u32[]{:S(2)}) collective-permute-start(bf16[4,512,128]{2,1,0:T(8,128)(2,1)S(1)} %get-tuple-element.80.refs_6_), channel_id=1, source_target_pairs={{3,0},{0,1},{1,2},{2,3},{7,4},{4,5},{5,6},{6,7},{11,8},{8,9},{9,10... | collective-permute-start | bytes 1572872 | tf_op jit(solution)/shard_map/ppermute | solution.py:288
  28.6 14.9 %collective-permute-start.12 = (bf16[4,512,128]{2,1,0:T(8,128)(2,1)S(1)}, bf16[4,512,128]{2,1,0:T(8,128)(2,1)S(1)}, u32[]{:S(2)}, u32[]{:S(2)}) collective-permute-start(bf16[4,512,128]{2,1,0:T(8,128)(2,1)S(1)} %get-tuple-element.80.refs_6_), channel_id=1, source_target_pairs={{1,0},{2,1},{3,2},{0,3},{5,4},{6,5},{7,6},{4,7},{9,8},{10,9},{11,1... | collective-permute-start | bytes 1572872 | tf_op jit(solution)/shard_map/ppermute | solution.py:288
  40.2 11.3 %collective-permute-start.17 = (bf16[4,512,128]{2,1,0:T(8,128)(2,1)S(1)}, bf16[4,512,128]{2,1,0:T(8,128)(2,1)S(1)}, u32[]{:S(2)}, u32[]{:S(2)}) collective-permute-start(bf16[4,512,128]{2,1,0:T(8,128)(2,1)S(1)} %get-tuple-element.79.refs_1_), channel_id=1, source_target_pairs={{12,0},{13,1},{14,2},{15,3},{0,4},{1,5},{2,6},{3,7},{4,8},{5,9},{6... | collective-permute-start | bytes 1572872 | tf_op jit(solution)/shard_map/ppermute | solution.py:288
  40.6 12.8 %collective-permute-start.16 = (bf16[4,512,128]{2,1,0:T(8,128)(2,1)S(1)}, bf16[4,512,128]{2,1,0:T(8,128)(2,1)S(1)}, u32[]{:S(2)}, u32[]{:S(2)}) collective-permute-start(bf16[4,512,128]{2,1,0:T(8,128)(2,1)S(1)} %get-tuple-element.79.refs_1_), channel_id=1, source_target_pairs={{4,0},{5,1},{6,2},{7,3},{8,4},{9,5},{10,6},{11,7},{12,8},{13,9},{1... | collective-permute-start | bytes 1572872 | tf_op jit(solution)/shard_map/ppermute | solution.py:288
  43.5 11.8 %collective-permute-start.19 = (bf16[4,512,128]{2,1,0:T(8,128)(2,1)S(1)}, bf16[4,512,128]{2,1,0:T(8,128)(2,1)S(1)}, u32[]{:S(2)}, u32[]{:S(2)}) collective-permute-start(bf16[4,512,128]{2,1,0:T(8,128)(2,1)S(1)} %get-tuple-element.84.refs_7_), channel_id=1, source_target_pairs={{3,0},{0,1},{1,2},{2,3},{7,4},{4,5},{5,6},{6,7},{11,8},{8,9},{9,10... | collective-permute-start | bytes 1572872 | tf_op jit(solution)/shard_map/ppermute | solution.py:288
  43.5 15.4 %collective-permute-start.18 = (bf16[4,512,128]{2,1,0:T(8,128)(2,1)S(1)}, bf16[4,512,128]{2,1,0:T(8,128)(2,1)S(1)}, u32[]{:S(2)}, u32[]{:S(2)}) collective-permute-start(bf16[4,512,128]{2,1,0:T(8,128)(2,1)S(1)} %get-tuple-element.84.refs_7_), channel_id=1, source_target_pairs={{1,0},{2,1},{3,2},{0,3},{5,4},{6,5},{7,6},{4,7},{9,8},{10,9},{11,1... | collective-permute-start | bytes 1572872 | tf_op jit(solution)/shard_map/ppermute | solution.py:288
  46.9 59.3 %collective-permute-start.26 = (bf16[16,512,128]{2,1,0:T(8,128)(2,1)S(1)}, bf16[16,512,128]{2,1,0:T(8,128)(2,1)S(1)}, u32[]{:S(2)}, u32[]{:S(2)}) collective-permute-start(bf16[16,512,128]{2,1,0:T(8,128)(2,1)S(1)} %shard_map.108.tiles_ref), channel_id=1, source_target_pairs={{16,0},{0,16},{48,32},{32,48},{80,64},{64,80},{112,96},{96,112},{1... | collective-permute-start | bytes 6291464 | tf_op jit(solution)/shard_map/ppermute | solution.py:301
  51.4 17.3 %collective-permute-start.20 = (bf16[4,512,128]{2,1,0:T(8,128)(2,1)S(1)}, bf16[4,512,128]{2,1,0:T(8,128)(2,1)S(1)}, u32[]{:S(2)}, u32[]{:S(2)}) collective-permute-start(bf16[4,512,128]{2,1,0:T(8,128)(2,1)S(1)} %collective-permute-done.10.refs_2_), channel_id=1, source_target_pairs={{4,0},{5,1},{6,2},{7,3},{8,4},{9,5},{10,6},{11,7},{12,8},{13,9},{1... | collective-permute-start | bytes 1572872 | tf_op jit(solution)/shard_map/ppermute | solution.py:288
  53.5 15.3 %collective-permute-start.22 = (bf16[4,512,128]{2,1,0:T(8,128)(2,1)S(1)}, bf16[4,512,128]{2,1,0:T(8,128)(2,1)S(1)}, u32[]{:S(2)}, u32[]{:S(2)}) collective-permute-start(bf16[4,512,128]{2,1,0:T(8,128)(2,1)S(1)} %collective-permute-done.12.refs_8_), channel_id=1, source_target_pairs={{1,0},{2,1},{3,2},{0,3},{5,4},{6,5},{7,6},{4,7},{9,8},{10,9},{11,1... | collective-permute-start | bytes 1572872 | tf_op jit(solution)/shard_map/ppermute | solution.py:288
  58.9 12.1 %collective-permute-start.23 = (bf16[4,512,128]{2,1,0:T(8,128)(2,1)S(1)}, bf16[4,512,128]{2,1,0:T(8,128)(2,1)S(1)}, u32[]{:S(2)}, u32[]{:S(2)}) collective-permute-start(bf16[4,512,128]{2,1,0:T(8,128)(2,1)S(1)} %collective-permute-done.19.refs_11_), channel_id=1, source_target_pairs={{3,0},{0,1},{1,2},{2,3},{7,4},{4,5},{5,6},{6,7},{11,8},{8,9},{9,10... | collective-permute-start | bytes 1572872 | tf_op jit(solution)/shard_map/ppermute | solution.py:288
  75.3 27.0 %collective-permute-start.27 = (s16[8,528,128]{2,1,0:T(8,128)(2,1)S(1)}, s16[8,528,128]{2,1,0:T(8,128)(2,1)S(1)}, u32[]{:S(2)}, u32[]{:S(2)}) collective-permute-start(s16[8,528,128]{2,1,0:T(8,128)(2,1)S(1)} %get-tuple-element.105), channel_id=1, source_target_pairs={{3,0},{0,1},{1,2},{2,3},{7,4},{4,5},{5,6},{6,7},{11,8},{8,9},{9,10... | collective-permute-start | bytes 3244040 | tf_op jit(solution)/shard_map/ppermute | solution.py:288
  75.3 26.9 %collective-permute-start.28 = (s16[8,528,128]{2,1,0:T(8,128)(2,1)S(1)}, s16[8,528,128]{2,1,0:T(8,128)(2,1)S(1)}, u32[]{:S(2)}, u32[]{:S(2)}) collective-permute-start(s16[8,528,128]{2,1,0:T(8,128)(2,1)S(1)} %get-tuple-element.106), channel_id=1, source_target_pairs={{1,0},{2,1},{3,2},{0,3},{5,4},{6,5},{7,6},{4,7},{9,8},{10,9},{11,1... | collective-permute-start | bytes 3244040 | tf_op jit(solution)/shard_map/ppermute | solution.py:288
  82.6 25.4 %collective-permute-start.24 = (s16[8,528,128]{2,1,0:T(8,128)(2,1)S(1)}, s16[8,528,128]{2,1,0:T(8,128)(2,1)S(1)}, u32[]{:S(2)}, u32[]{:S(2)}) collective-permute-start(s16[8,528,128]{2,1,0:T(8,128)(2,1)S(1)} %get-tuple-element.97), channel_id=1, source_target_pairs={{12,0},{13,1},{14,2},{15,3},{0,4},{1,5},{2,6},{3,7},{4,8},{5,9},{6... | collective-permute-start | bytes 3244040 | tf_op jit(solution)/shard_map/ppermute | solution.py:288
  82.7 25.3 %collective-permute-start.25 = (s16[8,528,128]{2,1,0:T(8,128)(2,1)S(1)}, s16[8,528,128]{2,1,0:T(8,128)(2,1)S(1)}, u32[]{:S(2)}, u32[]{:S(2)}) collective-permute-start(s16[8,528,128]{2,1,0:T(8,128)(2,1)S(1)} %get-tuple-element.98), channel_id=1, source_target_pairs={{4,0},{5,1},{6,2},{7,3},{8,4},{9,5},{10,6},{11,7},{12,8},{13,9},{1... | collective-permute-start | bytes 3244040 | tf_op jit(solution)/shard_map/ppermute | solution.py:288
  102.9 13.5 %collective-permute-start.29 = (s16[4,528,128]{2,1,0:T(8,128)(2,1)S(1)}, s16[4,528,128]{2,1,0:T(8,128)(2,1)S(1)}, u32[]{:S(2)}, u32[]{:S(2)}) collective-permute-start(s16[4,528,128]{2,1,0:T(8,128)(2,1)S(1)} %get-tuple-element.107), channel_id=1, source_target_pairs={{3,0},{0,1},{1,2},{2,3},{7,4},{4,5},{5,6},{6,7},{11,8},{8,9},{9,10... | collective-permute-start | bytes 1622024 | tf_op jit(solution)/shard_map/ppermute | solution.py:288
  103.0 13.5 %collective-permute-start.30 = (s16[4,528,128]{2,1,0:T(8,128)(2,1)S(1)}, s16[4,528,128]{2,1,0:T(8,128)(2,1)S(1)}, u32[]{:S(2)}, u32[]{:S(2)}) collective-permute-start(s16[4,528,128]{2,1,0:T(8,128)(2,1)S(1)} %get-tuple-element.108), channel_id=1, source_target_pairs={{1,0},{2,1},{3,2},{0,3},{5,4},{6,5},{7,6},{4,7},{9,8},{10,9},{11,1... | collective-permute-start | bytes 1622024 | tf_op jit(solution)/shard_map/ppermute | solution.py:288
  108.7 12.1 %collective-permute-start.35 = (s16[4,528,128]{2,1,0:T(8,128)(2,1)S(1)}, s16[4,528,128]{2,1,0:T(8,128)(2,1)S(1)}, u32[]{:S(2)}, u32[]{:S(2)}) collective-permute-start(s16[4,528,128]{2,1,0:T(8,128)(2,1)S(1)} %get-tuple-element.116), channel_id=1, source_target_pairs={{12,0},{13,1},{14,2},{15,3},{0,4},{1,5},{2,6},{3,7},{4,8},{5,9},{6... | collective-permute-start | bytes 1622024 | tf_op jit(solution)/shard_map/ppermute | solution.py:288
  108.8 12.0 %collective-permute-start.36 = (s16[4,528,128]{2,1,0:T(8,128)(2,1)S(1)}, s16[4,528,128]{2,1,0:T(8,128)(2,1)S(1)}, u32[]{:S(2)}, u32[]{:S(2)}) collective-permute-start(s16[4,528,128]{2,1,0:T(8,128)(2,1)S(1)} %get-tuple-element.117), channel_id=1, source_target_pairs={{4,0},{5,1},{6,2},{7,3},{8,4},{9,5},{10,6},{11,7},{12,8},{13,9},{1... | collective-permute-start | bytes 1622024 | tf_op jit(solution)/shard_map/ppermute | solution.py:288
  (28 other events, 256.5 us)

commit v4 on v3

--- a/solution.py
+++ b/solution.py
@@ -178,11 +178,11 @@
 def masked_tiles(t2, t2_live):
     def body(live_ref, t2_ref, out_ref):
         for t in range(4):
-            keep = live_ref[0, t].astype(jnp.float32).astype(jnp.bfloat16)
+            keep = live_ref[0:1, t : t + 1].astype(jnp.float32).astype(jnp.bfloat16)
             out_ref[t] = t2_ref[:, t * TILE : (t + 1) * TILE] * keep
 
     out = jax.ShapeDtypeStruct((4, ROWS, TILE), jnp.bfloat16)
-    return kernel(body, out, [SMEM_SPEC, VMEM_SPEC])(t2_live, t2)
+    return kernel(body, out, [VMEM_SPEC] * 2)(t2_live, t2)
 
 
 def join(*groups):
@@ -261,20 +261,26 @@
     return kernel(body, (coded(1), coded(1)), [VMEM_SPEC] * 3)(kept, got_up, got_down)
 
 
+def add_direct(kept, got_up, got_down):
+    def body(kept_ref, up_ref, down_ref, out_ref):
+        out_ref[0] = kept_ref[2] + get(down_ref, 1)
+        out_ref[1] = kept_ref[3] + get(up_ref, 1)
+
+    return kernel(body, plain(2), [VMEM_SPEC] * 3)(kept, got_up, got_down)
+
+
 def finish(res_live, cycle, half_a, half_b):
     def body(live_ref, cycle_ref, *refs):
         out_ref = refs[-1]
         for h in range(2):
-            kept, up, down, last_up, last_down = refs[5 * h : 5 * h + 5]
-            low = kept[2] + get(down, 1) + get(last_up, 0)
-            high = kept[3] + get(up, 1) + get(last_down, 0)
-            for t, value in ((2 * h, low), (2 * h + 1, high)):
-                cols = slice(t * TILE, (t + 1) * TILE)
-                keep = live_ref[0, t].astype(jnp.float32)
-                out_ref[:, cols] = keep * (value + cycle_ref[:, cols])
+            own, last_up, last_down = refs[3 * h : 3 * h + 3]
+            for t, last in ((0, last_up), (1, last_down)):
+                cols = slice((2 * h + t) * TILE, (2 * h + t + 1) * TILE)
+                keep = live_ref[0:1, 2 * h + t : 2 * h + t + 1].astype(jnp.float32)
+                out_ref[:, cols] = keep * (own[t] + get(last, 0) + cycle_ref[:, cols])
 
     out = jax.ShapeDtypeStruct((ROWS, 4 * TILE), jnp.float32)
-    return kernel(body, out, [SMEM_SPEC] + [VMEM_SPEC] * 11)(res_live, cycle, *half_a, *half_b)
+    return kernel(body, out, [VMEM_SPEC] * 8)(res_live, cycle, *half_a, *half_b)
 
 
 def local(t2, t2_live, int_tiles, integrals, cycle_w, res_live):
@@ -365,7 +371,7 @@
         up, down, kept = row_sum(sums, *got, *last)
         got = first_hop((up, down), other)
         last = first_hop(merge_last(kept, *got), other)
-        return (kept, *got, *last)
+        return (add_direct(kept, *got), *last)
 
     half_a = reduce(sums_a, got_a, along_z, along_y)
     half_b = reduce(sums_b, got_b, along_y, along_z)

time: 139 us -> 138 us (level)
  Pallas kernels: 41.2 us -> 39.6 us
  transfers between devices with their start and end apart: 41 -> 41, of which waited for: 16 -> 15; matrix products, arithmetic and copies ran while one was open for 3% -> 3% of each run, Pallas kernels for 28% -> 28%
where the time goes in v4:
time: 138 us; the launch traced here: 137 us
  starting transfers between devices  60.1 us (44%)
  Pallas kernels  39.6 us (29%)
  waiting for transfers between devices  31 us (22%)
  other arithmetic  4.23 us (3%)
  local copies, waits for them, and re-layouts  1.87 us (1%)
    ppermute x36, starting transfers between devices, take(): return lax.ppermute(value, 'ints', pairs)  52.7 us
    ppermute x36, waiting for transfers between devices, take(): return lax.ppermute(value, 'ints', pairs)  31 us
    pallas_call x4, Pallas kernels, ladder(): return kernel(body, plain(count), specs)(*args)  21.9 us
    pallas_call x2, Pallas kernels, ladder(): kernel(body, (coded(count // 2),) * 2, specs + [VMEM_SPEC], (sums,), 7)  8.15 us
    ppermute x5, starting transfers between devices, along_x(): return lax.ppermute(value, 'pair', pairs)  7.35 us
    pallas_call x2, Pallas kernels, cycle_part(): return kernel(body, out, [SMEM_SPEC] + [VMEM_SPEC] * (len(args) - 1))(*args)  3.61 us
  transfers between devices with their start and end apart: 41, of which 15 were waited for; matrix products, arithmetic and copies ran while one was open for 3% of the time, Pallas kernels for 28%

profile of v4, /device:TPU:0, one launch (start us, length us, event | category | flops | bytes accessed | tf_op | source)
XLA Modules:
  0.0 137.3 jit_solution(1122784412474895815)
XLA Ops:
  16.5 2.9 %collective-permute-start.6 = (bf16[1,512,128]{2,1,0:T(8,128)(2,1)S(1)}, bf16[1,512,128]{2,1,0:T(8,128)(2,1)S(1)}, u32[]{:S(2)}, u32[]{:S(2)}) collective-permute-start(bf16[1,512,128]{2,1,0:T(8,128)(2,1)S(1)} %slice.36), channel_id=1, source_target_pairs={{4,0},{5,1},{6,2},{7,3},{8,4},{9,5},{10,6},{11,7},{12,8},{13,9},{1... | collective-permute-start | bytes 393224 | tf_op jit(solution)/shard_map/ppermute | solution.py:294
  22.3 2.2 %collective-permute-start.4 = (bf16[1,512,128]{2,1,0:T(8,128)(2,1)S(1)}, bf16[1,512,128]{2,1,0:T(8,128)(2,1)S(1)}, u32[]{:S(2)}, u32[]{:S(2)}) collective-permute-start(bf16[1,512,128]{2,1,0:T(8,128)(2,1)S(1)} %slice.34), channel_id=1, source_target_pairs={{1,0},{2,1},{3,2},{0,3},{5,4},{6,5},{7,6},{4,7},{9,8},{10,9},{11,1... | collective-permute-start | bytes 393224 | tf_op jit(solution)/shard_map/ppermute | solution.py:294
  25.7 2.4 %collective-permute-start.10 = (bf16[4,512,128]{2,1,0:T(8,128)(2,1)S(1)}, bf16[4,512,128]{2,1,0:T(8,128)(2,1)S(1)}, u32[]{:S(2)}, u32[]{:S(2)}) collective-permute-start(bf16[4,512,128]{2,1,0:T(8,128)(2,1)S(1)} %get-tuple-element.74.refs_0_), channel_id=1, source_target_pairs={{4,0},{5,1},{6,2},{7,3},{8,4},{9,5},{10,6},{11,7},{12,8},{13,9},{1... | collective-permute-start | bytes 1572872 | tf_op jit(solution)/shard_map/ppermute | solution.py:294
  28.1 3.2 %collective-permute-start.12 = (bf16[4,512,128]{2,1,0:T(8,128)(2,1)S(1)}, bf16[4,512,128]{2,1,0:T(8,128)(2,1)S(1)}, u32[]{:S(2)}, u32[]{:S(2)}) collective-permute-start(bf16[4,512,128]{2,1,0:T(8,128)(2,1)S(1)} %get-tuple-element.80.refs_6_), channel_id=1, source_target_pairs={{1,0},{2,1},{3,2},{0,3},{5,4},{6,5},{7,6},{4,7},{9,8},{10,9},{11,1... | collective-permute-start | bytes 1572872 | tf_op jit(solution)/shard_map/ppermute | solution.py:294
  33.7 3.5 %collective-permute-done.11.refs_4_ = bf16[4,512,128]{2,1,0:T(8,128)(2,1)S(1)} collective-permute-done((bf16[4,512,128]{2,1,0:T(8,128)(2,1)S(1)}, bf16[4,512,128]{2,1,0:T(8,128)(2,1)S(1)}, u32[]{:S(2)}, u32[]{:S(2)}) %collective-permute-start.11) | collective-permute-done | bytes 524320 | tf_op jit(solution)/shard_map/ppermute | solution.py:294
  37.2 2.5 %collective-permute-start.14 = (bf16[2,512,128]{2,1,0:T(8,128)(2,1)S(1)}, bf16[2,512,128]{2,1,0:T(8,128)(2,1)S(1)}, u32[]{:S(2)}, u32[]{:S(2)}) collective-permute-start(bf16[2,512,128]{2,1,0:T(8,128)(2,1)S(1)} %slice.38), channel_id=1, source_target_pairs={{32,0},{48,16},{64,32},{80,48},{96,64},{112,80},{0,96},{16,112},{3... | collective-permute-start | bytes 786440 | tf_op jit(solution)/shard_map/ppermute | solution.py:307
  40.2 2.8 %collective-permute-start.16 = (bf16[4,512,128]{2,1,0:T(8,128)(2,1)S(1)}, bf16[4,512,128]{2,1,0:T(8,128)(2,1)S(1)}, u32[]{:S(2)}, u32[]{:S(2)}) collective-permute-start(bf16[4,512,128]{2,1,0:T(8,128)(2,1)S(1)} %get-tuple-element.79.refs_1_), channel_id=1, source_target_pairs={{4,0},{5,1},{6,2},{7,3},{8,4},{9,5},{10,6},{11,7},{12,8},{13,9},{1... | collective-permute-start | bytes 1572872 | tf_op jit(solution)/shard_map/ppermute | solution.py:294
  43.1 3.2 %collective-permute-start.18 = (bf16[4,512,128]{2,1,0:T(8,128)(2,1)S(1)}, bf16[4,512,128]{2,1,0:T(8,128)(2,1)S(1)}, u32[]{:S(2)}, u32[]{:S(2)}) collective-permute-start(bf16[4,512,128]{2,1,0:T(8,128)(2,1)S(1)} %get-tuple-element.84.refs_7_), channel_id=1, source_target_pairs={{1,0},{2,1},{3,2},{0,3},{5,4},{6,5},{7,6},{4,7},{9,8},{10,9},{11,1... | collective-permute-start | bytes 1572872 | tf_op jit(solution)/shard_map/ppermute | solution.py:294
  46.5 4.5 %collective-permute-done.17.refs_5_ = bf16[4,512,128]{2,1,0:T(8,128)(2,1)S(1)} collective-permute-done((bf16[4,512,128]{2,1,0:T(8,128)(2,1)S(1)}, bf16[4,512,128]{2,1,0:T(8,128)(2,1)S(1)}, u32[]{:S(2)}, u32[]{:S(2)}) %collective-permute-start.17) | collective-permute-done | bytes 524320 | tf_op jit(solution)/shard_map/ppermute | solution.py:294
  54.9 3.6 %collective-permute-done.18.refs_9_ = bf16[4,512,128]{2,1,0:T(8,128)(2,1)S(1)} collective-permute-done((bf16[4,512,128]{2,1,0:T(8,128)(2,1)S(1)}, bf16[4,512,128]{2,1,0:T(8,128)(2,1)S(1)}, u32[]{:S(2)}, u32[]{:S(2)}) %collective-permute-start.18) | collective-permute-done | bytes 524320 | tf_op jit(solution)/shard_map/ppermute | solution.py:294
  58.9 4.8 %shard_map.105.refs_5_ = f32[16,512,128]{2,1,0:T(8,128)S(1)} custom-call(s32[448]{0:T(512)S(1)} %select_reduce_fusion.1.refs_0_, s32[224]{0:T(256)S(1)} %fusion.15.refs_1_, s32[65]{0:T(128)S(1)} %pad_add_fusion.refs_2_, bf16[48,512,128]{2,1,0:T(8,128)(2,1)S(1)} %shard_map.103.refs_3_, bf16[320,128,128]{2,1,0:T(8,128)(2,1)S(1)} %bitcast.3), custom_call_target="tpu_custom_call" | custom-call | tf_op jit(solution)/shard_map/pallas_call | solution.py:173
  63.7 3.8 %shard_map.104.refs_5_ = f32[16,512,128]{2,1,0:T(8,128)S(1)} custom-call(s32[448]{0:T(512)S(1)} %select_reduce_fusion.1.refs_0_, s32[224]{0:T(256)S(1)} %fusion.15.refs_1_, s32[65]{0:T(128)S(1)} %pad_add_fusion.refs_2_, bf16[48,512,128]{2,1,0:T(8,128)(2,1)S(1)} %shard_map.103.refs_3_, bf16[320,128,128]{2,1,0:T(8,128)(2,1)S(1)} %bitcast.3), custom_call_target="tpu_custom_call" | custom-call | tf_op jit(solution)/shard_map/pallas_call | solution.py:173
  70.8 4.1 %shard_map.112 = (s16[8,528,128]{2,1,0:T(8,128)(2,1)S(1)}, s16[8,528,128]{2,1,0:T(8,128)(2,1)S(1)}) custom-call(s32[448]{0:T(512)S(1)} %select_reduce_fusion.refs_0_.refs_4_, s32[224]{0:T(256)S(1)} %fusion.16.refs_1_.refs_5_, s32[65]{0:T(128)S(1)} %pad_add_fusion.1.refs_2_.refs_6_, bf16[16,512,128]{2,1,0:T(8,128)(2,1)S(1)} %shard_map.106.refs_3_.refs_7_, ...), custom_call_target="tpu_custom_call" | custom-call | tf_op jit(solution)/shard_map/pallas_call | solution.py:175
  75.0 3.2 %collective-permute-start.28 = (s16[8,528,128]{2,1,0:T(8,128)(2,1)S(1)}, s16[8,528,128]{2,1,0:T(8,128)(2,1)S(1)}, u32[]{:S(2)}, u32[]{:S(2)}) collective-permute-start(s16[8,528,128]{2,1,0:T(8,128)(2,1)S(1)} %get-tuple-element.106), channel_id=1, source_target_pairs={{1,0},{2,1},{3,2},{0,3},{5,4},{6,5},{7,6},{4,7},{9,8},{10,9},{11,1... | collective-permute-start | bytes 3244040 | tf_op jit(solution)/shard_map/ppermute | solution.py:294
  78.2 4.1 %shard_map.107 = (s16[8,528,128]{2,1,0:T(8,128)(2,1)S(1)}, s16[8,528,128]{2,1,0:T(8,128)(2,1)S(1)}) custom-call(s32[448]{0:T(512)S(1)} %select_reduce_fusion.refs_0_.refs_4_, s32[224]{0:T(256)S(1)} %fusion.16.refs_1_.refs_5_, s32[65]{0:T(128)S(1)} %pad_add_fusion.1.refs_2_.refs_6_, bf16[16,512,128]{2,1,0:T(8,128)(2,1)S(1)} %shard_map.106.refs_3_.refs_7_, ...), custom_call_target="tpu_custom_call" | custom-call | tf_op jit(solution)/shard_map/pallas_call | solution.py:175
  82.3 3.5 %collective-permute-start.25 = (s16[8,528,128]{2,1,0:T(8,128)(2,1)S(1)}, s16[8,528,128]{2,1,0:T(8,128)(2,1)S(1)}, u32[]{:S(2)}, u32[]{:S(2)}) collective-permute-start(s16[8,528,128]{2,1,0:T(8,128)(2,1)S(1)} %get-tuple-element.98), channel_id=1, source_target_pairs={{4,0},{5,1},{6,2},{7,3},{8,4},{9,5},{10,6},{11,7},{12,8},{13,9},{1... | collective-permute-start | bytes 3244040 | tf_op jit(solution)/shard_map/ppermute | solution.py:294
  87.7 7.1 %shard_map.117.sums_ref = f32[16,512,128]{2,1,0:T(8,128)S(1)} custom-call(s32[448]{0:T(512)S(1)} %select_reduce_fusion.1.refs_0_, s32[224]{0:T(256)S(1)} %fusion.15.refs_1_, s32[65]{0:T(128)S(1)} %pad_add_fusion.refs_2_, bf16[48,512,128]{2,1,0:T(8,128)(2,1)S(1)} %shard_map.103.refs_3_, s32[448]{0:T(512)S(1)} %select_reduce_fusion.refs_0_.refs_4_, ...), custom_call_target="tpu_custom_call" | custom-call | tf_op jit(solution)/shard_map/pallas_call | solution.py:173
  94.7 6.3 %shard_map.111.sums_ref = f32[16,512,128]{2,1,0:T(8,128)S(1)} custom-call(s32[448]{0:T(512)S(1)} %select_reduce_fusion.1.refs_0_, s32[224]{0:T(256)S(1)} %fusion.15.refs_1_, s32[65]{0:T(128)S(1)} %pad_add_fusion.refs_2_, bf16[48,512,128]{2,1,0:T(8,128)(2,1)S(1)} %shard_map.103.refs_3_, s32[448]{0:T(512)S(1)} %select_reduce_fusion.refs_0_.refs_4_, ...), custom_call_target="tpu_custom_call" | custom-call | tf_op jit(solution)/shard_map/pallas_call | solution.py:173
  101.8 3.6 %collective-permute-start.30 = (s16[4,528,128]{2,1,0:T(8,128)(2,1)S(1)}, s16[4,528,128]{2,1,0:T(8,128)(2,1)S(1)}, u32[]{:S(2)}, u32[]{:S(2)}) collective-permute-start(s16[4,528,128]{2,1,0:T(8,128)(2,1)S(1)} %get-tuple-element.108), channel_id=1, source_target_pairs={{1,0},{2,1},{3,2},{0,3},{5,4},{6,5},{7,6},{4,7},{9,8},{10,9},{11,1... | collective-permute-start | bytes 1622024 | tf_op jit(solution)/shard_map/ppermute | solution.py:294
  108.0 3.2 %collective-permute-start.36 = (s16[4,528,128]{2,1,0:T(8,128)(2,1)S(1)}, s16[4,528,128]{2,1,0:T(8,128)(2,1)S(1)}, u32[]{:S(2)}, u32[]{:S(2)}) collective-permute-start(s16[4,528,128]{2,1,0:T(8,128)(2,1)S(1)} %get-tuple-element.117), channel_id=1, source_target_pairs={{4,0},{5,1},{6,2},{7,3},{8,4},{9,5},{10,6},{11,7},{12,8},{13,9},{1... | collective-permute-start | bytes 1622024 | tf_op jit(solution)/shard_map/ppermute | solution.py:294
  111.2 4.3 %collective-permute-done.29.last_up_ref = s16[4,528,128]{2,1,0:T(8,128)(2,1)S(1)} collective-permute-done((s16[4,528,128]{2,1,0:T(8,128)(2,1)S(1)}, s16[4,528,128]{2,1,0:T(8,128)(2,1)S(1)}, u32[]{:S(2)}, u32[]{:S(2)}) %collective-permute-start.29) | collective-permute-done | bytes 540704 | tf_op jit(solution)/shard_map/ppermute | solution.py:294
  116.5 3.2 %collective-permute-start.32 = (s16[2,528,128]{2,1,0:T(8,128)(2,1)S(1)}, s16[2,528,128]{2,1,0:T(8,128)(2,1)S(1)}, u32[]{:S(2)}, u32[]{:S(2)}) collective-permute-start(s16[2,528,128]{2,1,0:T(8,128)(2,1)S(1)} %get-tuple-element.111), channel_id=1, source_target_pairs={{4,0},{5,1},{6,2},{7,3},{8,4},{9,5},{10,6},{11,7},{12,8},{13,9},{1... | collective-permute-start | bytes 811016 | tf_op jit(solution)/shard_map/ppermute | solution.py:294
  125.0 2.7 %collective-permute-start.34 = (s16[1,528,128]{2,1,0:T(8,128)(2,1)S(1)}, s16[1,528,128]{2,1,0:T(8,128)(2,1)S(1)}, u32[]{:S(2)}, u32[]{:S(2)}) collective-permute-start(s16[1,528,128]{2,1,0:T(8,128)(2,1)S(1)} %get-tuple-element.113), channel_id=1, source_target_pairs={{4,0},{5,1},{6,2},{7,3},{8,4},{9,5},{10,6},{11,7},{12,8},{13,9},{1... | collective-permute-start | bytes 405512 | tf_op jit(solution)/shard_map/ppermute | solution.py:294
  132.4 2.7 %collective-permute-done.39.refs_4_ = s16[1,528,128]{2,1,0:T(8,128)(2,1)S(1)} collective-permute-done((s16[1,528,128]{2,1,0:T(8,128)(2,1)S(1)}, s16[1,528,128]{2,1,0:T(8,128)(2,1)S(1)}, u32[]{:S(2)}, u32[]{:S(2)}) %collective-permute-start.39) | collective-permute-done | bytes 135200 | tf_op jit(solution)/shard_map/ppermute | solution.py:294
  (136 shorter events, 49.3 us)
Async XLA Ops:
  1.9 12.3 %collective-permute-start.3 = (bf16[2,512,128]{2,1,0:T(8,128)(2,1)S(1)}, bf16[2,512,128]{2,1,0:T(8,128)(2,1)S(1)}, u32[]{:S(2)}, u32[]{:S(2)}) collective-permute-start(bf16[2,512,128]{2,1,0:T(8,128)(2,1)S(1)} %get-tuple-element.137.refs_2_), channel_id=1, source_target_pairs={{12,0},{13,1},{14,2},{15,3},{0,4},{1,5},{2,6},{3,7},{4,8},{5,9},{6... | collective-permute-start | bytes 786440 | tf_op jit(solution)/shard_map/ppermute | solution.py:294
  3.7 12.3 %collective-permute-start.2 = (bf16[2,512,128]{2,1,0:T(8,128)(2,1)S(1)}, bf16[2,512,128]{2,1,0:T(8,128)(2,1)S(1)}, u32[]{:S(2)}, u32[]{:S(2)}) collective-permute-start(bf16[2,512,128]{2,1,0:T(8,128)(2,1)S(1)} %get-tuple-element.137.refs_2_), channel_id=1, source_target_pairs={{4,0},{5,1},{6,2},{7,3},{8,4},{9,5},{10,6},{11,7},{12,8},{13,9},{1... | collective-permute-start | bytes 786440 | tf_op jit(solution)/shard_map/ppermute | solution.py:294
  9.4 18.7 %collective-permute-start.9 = (bf16[4,512,128]{2,1,0:T(8,128)(2,1)S(1)}, bf16[4,512,128]{2,1,0:T(8,128)(2,1)S(1)}, u32[]{:S(2)}, u32[]{:S(2)}) collective-permute-start(bf16[4,512,128]{2,1,0:T(8,128)(2,1)S(1)} %shard_map.100.refs_0_), channel_id=1, source_target_pairs={{96,0},{112,16},{0,32},{16,48},{32,64},{48,80},{64,96},{80,112},{9... | collective-permute-start | bytes 1572872 | tf_op jit(solution)/shard_map/ppermute | solution.py:307
  14.2 17.9 %collective-permute-start.8 = (bf16[4,512,128]{2,1,0:T(8,128)(2,1)S(1)}, bf16[4,512,128]{2,1,0:T(8,128)(2,1)S(1)}, u32[]{:S(2)}, u32[]{:S(2)}) collective-permute-start(bf16[4,512,128]{2,1,0:T(8,128)(2,1)S(1)} %shard_map.100.refs_0_), channel_id=1, source_target_pairs={{32,0},{48,16},{64,32},{80,48},{96,64},{112,80},{0,96},{16,112},{3... | collective-permute-start | bytes 1572872 | tf_op jit(solution)/shard_map/ppermute | solution.py:307
  24.5 12.7 %collective-permute-start.11 = (bf16[4,512,128]{2,1,0:T(8,128)(2,1)S(1)}, bf16[4,512,128]{2,1,0:T(8,128)(2,1)S(1)}, u32[]{:S(2)}, u32[]{:S(2)}) collective-permute-start(bf16[4,512,128]{2,1,0:T(8,128)(2,1)S(1)} %get-tuple-element.74.refs_0_), channel_id=1, source_target_pairs={{12,0},{13,1},{14,2},{15,3},{0,4},{1,5},{2,6},{3,7},{4,8},{5,9},{6... | collective-permute-start | bytes 1572872 | tf_op jit(solution)/shard_map/ppermute | solution.py:294
  25.7 14.0 %collective-permute-start.10 = (bf16[4,512,128]{2,1,0:T(8,128)(2,1)S(1)}, bf16[4,512,128]{2,1,0:T(8,128)(2,1)S(1)}, u32[]{:S(2)}, u32[]{:S(2)}) collective-permute-start(bf16[4,512,128]{2,1,0:T(8,128)(2,1)S(1)} %get-tuple-element.74.refs_0_), channel_id=1, source_target_pairs={{4,0},{5,1},{6,2},{7,3},{8,4},{9,5},{10,6},{11,7},{12,8},{13,9},{1... | collective-permute-start | bytes 1572872 | tf_op jit(solution)/shard_map/ppermute | solution.py:294
  28.1 12.1 %collective-permute-start.13 = (bf16[4,512,128]{2,1,0:T(8,128)(2,1)S(1)}, bf16[4,512,128]{2,1,0:T(8,128)(2,1)S(1)}, u32[]{:S(2)}, u32[]{:S(2)}) collective-permute-start(bf16[4,512,128]{2,1,0:T(8,128)(2,1)S(1)} %get-tuple-element.80.refs_6_), channel_id=1, source_target_pairs={{3,0},{0,1},{1,2},{2,3},{7,4},{4,5},{5,6},{6,7},{11,8},{8,9},{9,10... | collective-permute-start | bytes 1572872 | tf_op jit(solution)/shard_map/ppermute | solution.py:294
  28.1 14.9 %collective-permute-start.12 = (bf16[4,512,128]{2,1,0:T(8,128)(2,1)S(1)}, bf16[4,512,128]{2,1,0:T(8,128)(2,1)S(1)}, u32[]{:S(2)}, u32[]{:S(2)}) collective-permute-start(bf16[4,512,128]{2,1,0:T(8,128)(2,1)S(1)} %get-tuple-element.80.refs_6_), channel_id=1, source_target_pairs={{1,0},{2,1},{3,2},{0,3},{5,4},{6,5},{7,6},{4,7},{9,8},{10,9},{11,1... | collective-permute-start | bytes 1572872 | tf_op jit(solution)/shard_map/ppermute | solution.py:294
  39.7 11.3 %collective-permute-start.17 = (bf16[4,512,128]{2,1,0:T(8,128)(2,1)S(1)}, bf16[4,512,128]{2,1,0:T(8,128)(2,1)S(1)}, u32[]{:S(2)}, u32[]{:S(2)}) collective-permute-start(bf16[4,512,128]{2,1,0:T(8,128)(2,1)S(1)} %get-tuple-element.79.refs_1_), channel_id=1, source_target_pairs={{12,0},{13,1},{14,2},{15,3},{0,4},{1,5},{2,6},{3,7},{4,8},{5,9},{6... | collective-permute-start | bytes 1572872 | tf_op jit(solution)/shard_map/ppermute | solution.py:294
  40.2 12.8 %collective-permute-start.16 = (bf16[4,512,128]{2,1,0:T(8,128)(2,1)S(1)}, bf16[4,512,128]{2,1,0:T(8,128)(2,1)S(1)}, u32[]{:S(2)}, u32[]{:S(2)}) collective-permute-start(bf16[4,512,128]{2,1,0:T(8,128)(2,1)S(1)} %get-tuple-element.79.refs_1_), channel_id=1, source_target_pairs={{4,0},{5,1},{6,2},{7,3},{8,4},{9,5},{10,6},{11,7},{12,8},{13,9},{1... | collective-permute-start | bytes 1572872 | tf_op jit(solution)/shard_map/ppermute | solution.py:294
  43.1 11.8 %collective-permute-start.19 = (bf16[4,512,128]{2,1,0:T(8,128)(2,1)S(1)}, bf16[4,512,128]{2,1,0:T(8,128)(2,1)S(1)}, u32[]{:S(2)}, u32[]{:S(2)}) collective-permute-start(bf16[4,512,128]{2,1,0:T(8,128)(2,1)S(1)} %get-tuple-element.84.refs_7_), channel_id=1, source_target_pairs={{3,0},{0,1},{1,2},{2,3},{7,4},{4,5},{5,6},{6,7},{11,8},{8,9},{9,10... | collective-permute-start | bytes 1572872 | tf_op jit(solution)/shard_map/ppermute | solution.py:294
  43.1 15.4 %collective-permute-start.18 = (bf16[4,512,128]{2,1,0:T(8,128)(2,1)S(1)}, bf16[4,512,128]{2,1,0:T(8,128)(2,1)S(1)}, u32[]{:S(2)}, u32[]{:S(2)}) collective-permute-start(bf16[4,512,128]{2,1,0:T(8,128)(2,1)S(1)} %get-tuple-element.84.refs_7_), channel_id=1, source_target_pairs={{1,0},{2,1},{3,2},{0,3},{5,4},{6,5},{7,6},{4,7},{9,8},{10,9},{11,1... | collective-permute-start | bytes 1572872 | tf_op jit(solution)/shard_map/ppermute | solution.py:294
  46.5 58.9 %collective-permute-start.26 = (bf16[16,512,128]{2,1,0:T(8,128)(2,1)S(1)}, bf16[16,512,128]{2,1,0:T(8,128)(2,1)S(1)}, u32[]{:S(2)}, u32[]{:S(2)}) collective-permute-start(bf16[16,512,128]{2,1,0:T(8,128)(2,1)S(1)} %shard_map.108.tiles_ref), channel_id=1, source_target_pairs={{16,0},{0,16},{48,32},{32,48},{80,64},{64,80},{112,96},{96,112},{1... | collective-permute-start | bytes 6291464 | tf_op jit(solution)/shard_map/ppermute | solution.py:307
  51.0 16.5 %collective-permute-start.20 = (bf16[4,512,128]{2,1,0:T(8,128)(2,1)S(1)}, bf16[4,512,128]{2,1,0:T(8,128)(2,1)S(1)}, u32[]{:S(2)}, u32[]{:S(2)}) collective-permute-start(bf16[4,512,128]{2,1,0:T(8,128)(2,1)S(1)} %collective-permute-done.10.refs_2_), channel_id=1, source_target_pairs={{4,0},{5,1},{6,2},{7,3},{8,4},{9,5},{10,6},{11,7},{12,8},{13,9},{1... | collective-permute-start | bytes 1572872 | tf_op jit(solution)/shard_map/ppermute | solution.py:294
  53.0 14.5 %collective-permute-start.22 = (bf16[4,512,128]{2,1,0:T(8,128)(2,1)S(1)}, bf16[4,512,128]{2,1,0:T(8,128)(2,1)S(1)}, u32[]{:S(2)}, u32[]{:S(2)}) collective-permute-start(bf16[4,512,128]{2,1,0:T(8,128)(2,1)S(1)} %collective-permute-done.12.refs_8_), channel_id=1, source_target_pairs={{1,0},{2,1},{3,2},{0,3},{5,4},{6,5},{7,6},{4,7},{9,8},{10,9},{11,1... | collective-permute-start | bytes 1572872 | tf_op jit(solution)/shard_map/ppermute | solution.py:294
  58.5 12.2 %collective-permute-start.23 = (bf16[4,512,128]{2,1,0:T(8,128)(2,1)S(1)}, bf16[4,512,128]{2,1,0:T(8,128)(2,1)S(1)}, u32[]{:S(2)}, u32[]{:S(2)}) collective-permute-start(bf16[4,512,128]{2,1,0:T(8,128)(2,1)S(1)} %collective-permute-done.19.refs_11_), channel_id=1, source_target_pairs={{3,0},{0,1},{1,2},{2,3},{7,4},{4,5},{5,6},{6,7},{11,8},{8,9},{9,10... | collective-permute-start | bytes 1572872 | tf_op jit(solution)/shard_map/ppermute | solution.py:294
  74.9 26.1 %collective-permute-start.27 = (s16[8,528,128]{2,1,0:T(8,128)(2,1)S(1)}, s16[8,528,128]{2,1,0:T(8,128)(2,1)S(1)}, u32[]{:S(2)}, u32[]{:S(2)}) collective-permute-start(s16[8,528,128]{2,1,0:T(8,128)(2,1)S(1)} %get-tuple-element.105), channel_id=1, source_target_pairs={{3,0},{0,1},{1,2},{2,3},{7,4},{4,5},{5,6},{6,7},{11,8},{8,9},{9,10... | collective-permute-start | bytes 3244040 | tf_op jit(solution)/shard_map/ppermute | solution.py:294
  75.0 26.1 %collective-permute-start.28 = (s16[8,528,128]{2,1,0:T(8,128)(2,1)S(1)}, s16[8,528,128]{2,1,0:T(8,128)(2,1)S(1)}, u32[]{:S(2)}, u32[]{:S(2)}) collective-permute-start(s16[8,528,128]{2,1,0:T(8,128)(2,1)S(1)} %get-tuple-element.106), channel_id=1, source_target_pairs={{1,0},{2,1},{3,2},{0,3},{5,4},{6,5},{7,6},{4,7},{9,8},{10,9},{11,1... | collective-permute-start | bytes 3244040 | tf_op jit(solution)/shard_map/ppermute | solution.py:294
  82.3 25.0 %collective-permute-start.24 = (s16[8,528,128]{2,1,0:T(8,128)(2,1)S(1)}, s16[8,528,128]{2,1,0:T(8,128)(2,1)S(1)}, u32[]{:S(2)}, u32[]{:S(2)}) collective-permute-start(s16[8,528,128]{2,1,0:T(8,128)(2,1)S(1)} %get-tuple-element.97), channel_id=1, source_target_pairs={{12,0},{13,1},{14,2},{15,3},{0,4},{1,5},{2,6},{3,7},{4,8},{5,9},{6... | collective-permute-start | bytes 3244040 | tf_op jit(solution)/shard_map/ppermute | solution.py:294
  82.3 24.9 %collective-permute-start.25 = (s16[8,528,128]{2,1,0:T(8,128)(2,1)S(1)}, s16[8,528,128]{2,1,0:T(8,128)(2,1)S(1)}, u32[]{:S(2)}, u32[]{:S(2)}) collective-permute-start(s16[8,528,128]{2,1,0:T(8,128)(2,1)S(1)} %get-tuple-element.98), channel_id=1, source_target_pairs={{4,0},{5,1},{6,2},{7,3},{8,4},{9,5},{10,6},{11,7},{12,8},{13,9},{1... | collective-permute-start | bytes 3244040 | tf_op jit(solution)/shard_map/ppermute | solution.py:294
  101.7 13.9 %collective-permute-start.29 = (s16[4,528,128]{2,1,0:T(8,128)(2,1)S(1)}, s16[4,528,128]{2,1,0:T(8,128)(2,1)S(1)}, u32[]{:S(2)}, u32[]{:S(2)}) collective-permute-start(s16[4,528,128]{2,1,0:T(8,128)(2,1)S(1)} %get-tuple-element.107), channel_id=1, source_target_pairs={{3,0},{0,1},{1,2},{2,3},{7,4},{4,5},{5,6},{6,7},{11,8},{8,9},{9,10... | collective-permute-start | bytes 1622024 | tf_op jit(solution)/shard_map/ppermute | solution.py:294
  101.8 13.8 %collective-permute-start.30 = (s16[4,528,128]{2,1,0:T(8,128)(2,1)S(1)}, s16[4,528,128]{2,1,0:T(8,128)(2,1)S(1)}, u32[]{:S(2)}, u32[]{:S(2)}) collective-permute-start(s16[4,528,128]{2,1,0:T(8,128)(2,1)S(1)} %get-tuple-element.108), channel_id=1, source_target_pairs={{1,0},{2,1},{3,2},{0,3},{5,4},{6,5},{7,6},{4,7},{9,8},{10,9},{11,1... | collective-permute-start | bytes 1622024 | tf_op jit(solution)/shard_map/ppermute | solution.py:294
  107.9 12.1 %collective-permute-start.35 = (s16[4,528,128]{2,1,0:T(8,128)(2,1)S(1)}, s16[4,528,128]{2,1,0:T(8,128)(2,1)S(1)}, u32[]{:S(2)}, u32[]{:S(2)}) collective-permute-start(s16[4,528,128]{2,1,0:T(8,128)(2,1)S(1)} %get-tuple-element.116), channel_id=1, source_target_pairs={{12,0},{13,1},{14,2},{15,3},{0,4},{1,5},{2,6},{3,7},{4,8},{5,9},{6... | collective-permute-start | bytes 1622024 | tf_op jit(solution)/shard_map/ppermute | solution.py:294
  108.0 12.0 %collective-permute-start.36 = (s16[4,528,128]{2,1,0:T(8,128)(2,1)S(1)}, s16[4,528,128]{2,1,0:T(8,128)(2,1)S(1)}, u32[]{:S(2)}, u32[]{:S(2)}) collective-permute-start(s16[4,528,128]{2,1,0:T(8,128)(2,1)S(1)} %get-tuple-element.117), channel_id=1, source_target_pairs={{4,0},{5,1},{6,2},{7,3},{8,4},{9,5},{10,6},{11,7},{12,8},{13,9},{1... | collective-permute-start | bytes 1622024 | tf_op jit(solution)/shard_map/ppermute | solution.py:294
  (28 other events, 244.6 us)

commit v5 on v4

--- a/solution.py
+++ b/solution.py
@@ -72,7 +72,7 @@
     same = (target[:, None] == ids[None, :]) & member[:, None]
     held = jnp.sum(same, axis=0, dtype=jnp.int32)
     before = jnp.sum((target[None, :] == target[:, None]) & (order[None, :] < order[:, None]) & member[None, :], axis=1, dtype=jnp.int32)
-    entries = jnp.maximum((held + 1) // 2, 1)
+    entries = jnp.maximum((held + 1) // 2, jnp.where(ids < 32, 1, 0) if late else 1)
     start = jnp.sum(jnp.where(ids[None, :] < ids[:, None], entries[None, :], 0), axis=1)
     mine = jnp.sum(jnp.where(same, start[None, :], 0), axis=1)
     slot = jnp.where(member, (mine + before // 2) * 2 + before % 2, -1)

time: 138 us -> 137 us (level)
  waiting for transfers between devices: 31 us -> 29.4 us
    ppermute x36, waiting for transfers between devices: 31 us -> 29.4 us  [take(): return lax.ppermute(value, 'ints', pairs)]
  transfers between devices with their start and end apart: 41 -> 41, of which waited for: 15 -> 16; matrix products, arithmetic and copies ran while one was open for 3% -> 3% of each run, Pallas kernels for 28% -> 28%
where the time goes in v5:
time: 137 us
  starting transfers between devices  60.5 us (44%)
  Pallas kernels  40.4 us (29%)
  waiting for transfers between devices  29.4 us (21%)
  other arithmetic  4.23 us (3%)
  local copies, waits for them, and re-layouts  1.87 us (1%)
    ppermute x36, starting transfers between devices, take(): return lax.ppermute(value, 'ints', pairs)  53.1 us
    ppermute x36, waiting for transfers between devices, take(): return lax.ppermute(value, 'ints', pairs)  29.4 us
    pallas_call x4, Pallas kernels, ladder(): return kernel(body, plain(count), specs)(*args)  22.7 us
    pallas_call x2, Pallas kernels, ladder(): kernel(body, (coded(count // 2),) * 2, specs + [VMEM_SPEC], (sums,), 7)  8.14 us
    ppermute x5, starting transfers between devices, along_x(): return lax.ppermute(value, 'pair', pairs)  7.35 us
    pallas_call x2, Pallas kernels, cycle_part(): return kernel(body, out, [SMEM_SPEC] + [VMEM_SPEC] * (len(args) - 1))(*args)  3.61 us
  transfers between devices with their start and end apart: 41, of which 16 were waited for; matrix products, arithmetic and copies ran while one was open for 3% of the time, Pallas kernels for 28%

profile of v5, /device:TPU:0, one launch (start us, length us, event | category | flops | bytes accessed | tf_op | source)
XLA Modules:
  0.0 137.0 jit_solution(11966955090433935990)
XLA Ops:
  16.5 2.9 %collective-permute-start.6 = (bf16[1,512,128]{2,1,0:T(8,128)(2,1)S(1)}, bf16[1,512,128]{2,1,0:T(8,128)(2,1)S(1)}, u32[]{:S(2)}, u32[]{:S(2)}) collective-permute-start(bf16[1,512,128]{2,1,0:T(8,128)(2,1)S(1)} %slice.36), channel_id=1, source_target_pairs={{4,0},{5,1},{6,2},{7,3},{8,4},{9,5},{10,6},{11,7},{12,8},{13,9},{1... | collective-permute-start | bytes 393224 | tf_op jit(solution)/shard_map/ppermute | solution.py:294
  25.7 2.4 %collective-permute-start.10 = (bf16[4,512,128]{2,1,0:T(8,128)(2,1)S(1)}, bf16[4,512,128]{2,1,0:T(8,128)(2,1)S(1)}, u32[]{:S(2)}, u32[]{:S(2)}) collective-permute-start(bf16[4,512,128]{2,1,0:T(8,128)(2,1)S(1)} %get-tuple-element.74.refs_0_), channel_id=1, source_target_pairs={{4,0},{5,1},{6,2},{7,3},{8,4},{9,5},{10,6},{11,7},{12,8},{13,9},{1... | collective-permute-start | bytes 1572872 | tf_op jit(solution)/shard_map/ppermute | solution.py:294
  28.1 3.2 %collective-permute-start.12 = (bf16[4,512,128]{2,1,0:T(8,128)(2,1)S(1)}, bf16[4,512,128]{2,1,0:T(8,128)(2,1)S(1)}, u32[]{:S(2)}, u32[]{:S(2)}) collective-permute-start(bf16[4,512,128]{2,1,0:T(8,128)(2,1)S(1)} %get-tuple-element.80.refs_6_), channel_id=1, source_target_pairs={{1,0},{2,1},{3,2},{0,3},{5,4},{6,5},{7,6},{4,7},{9,8},{10,9},{11,1... | collective-permute-start | bytes 1572872 | tf_op jit(solution)/shard_map/ppermute | solution.py:294
  33.7 3.5 %collective-permute-done.11.refs_4_ = bf16[4,512,128]{2,1,0:T(8,128)(2,1)S(1)} collective-permute-done((bf16[4,512,128]{2,1,0:T(8,128)(2,1)S(1)}, bf16[4,512,128]{2,1,0:T(8,128)(2,1)S(1)}, u32[]{:S(2)}, u32[]{:S(2)}) %collective-permute-start.11) | collective-permute-done | bytes 524320 | tf_op jit(solution)/shard_map/ppermute | solution.py:294
  37.2 2.5 %collective-permute-start.14 = (bf16[2,512,128]{2,1,0:T(8,128)(2,1)S(1)}, bf16[2,512,128]{2,1,0:T(8,128)(2,1)S(1)}, u32[]{:S(2)}, u32[]{:S(2)}) collective-permute-start(bf16[2,512,128]{2,1,0:T(8,128)(2,1)S(1)} %slice.38), channel_id=1, source_target_pairs={{32,0},{48,16},{64,32},{80,48},{96,64},{112,80},{0,96},{16,112},{3... | collective-permute-start | bytes 786440 | tf_op jit(solution)/shard_map/ppermute | solution.py:307
  40.2 2.8 %collective-permute-start.16 = (bf16[4,512,128]{2,1,0:T(8,128)(2,1)S(1)}, bf16[4,512,128]{2,1,0:T(8,128)(2,1)S(1)}, u32[]{:S(2)}, u32[]{:S(2)}) collective-permute-start(bf16[4,512,128]{2,1,0:T(8,128)(2,1)S(1)} %get-tuple-element.79.refs_1_), channel_id=1, source_target_pairs={{4,0},{5,1},{6,2},{7,3},{8,4},{9,5},{10,6},{11,7},{12,8},{13,9},{1... | collective-permute-start | bytes 1572872 | tf_op jit(solution)/shard_map/ppermute | solution.py:294
  43.1 3.2 %collective-permute-start.18 = (bf16[4,512,128]{2,1,0:T(8,128)(2,1)S(1)}, bf16[4,512,128]{2,1,0:T(8,128)(2,1)S(1)}, u32[]{:S(2)}, u32[]{:S(2)}) collective-permute-start(bf16[4,512,128]{2,1,0:T(8,128)(2,1)S(1)} %get-tuple-element.84.refs_7_), channel_id=1, source_target_pairs={{1,0},{2,1},{3,2},{0,3},{5,4},{6,5},{7,6},{4,7},{9,8},{10,9},{11,1... | collective-permute-start | bytes 1572872 | tf_op jit(solution)/shard_map/ppermute | solution.py:294
  46.5 4.5 %collective-permute-done.17.refs_5_ = bf16[4,512,128]{2,1,0:T(8,128)(2,1)S(1)} collective-permute-done((bf16[4,512,128]{2,1,0:T(8,128)(2,1)S(1)}, bf16[4,512,128]{2,1,0:T(8,128)(2,1)S(1)}, u32[]{:S(2)}, u32[]{:S(2)}) %collective-permute-start.17) | collective-permute-done | bytes 524320 | tf_op jit(solution)/shard_map/ppermute | solution.py:294
  54.9 3.6 %collective-permute-done.18.refs_9_ = bf16[4,512,128]{2,1,0:T(8,128)(2,1)S(1)} collective-permute-done((bf16[4,512,128]{2,1,0:T(8,128)(2,1)S(1)}, bf16[4,512,128]{2,1,0:T(8,128)(2,1)S(1)}, u32[]{:S(2)}, u32[]{:S(2)}) %collective-permute-start.18) | collective-permute-done | bytes 524320 | tf_op jit(solution)/shard_map/ppermute | solution.py:294
  58.9 4.8 %shard_map.105.refs_5_ = f32[16,512,128]{2,1,0:T(8,128)S(1)} custom-call(s32[448]{0:T(512)S(1)} %select_reduce_fusion.1.refs_0_, s32[224]{0:T(256)S(1)} %fusion.15.refs_1_, s32[65]{0:T(128)S(1)} %pad_add_fusion.refs_2_, bf16[48,512,128]{2,1,0:T(8,128)(2,1)S(1)} %shard_map.103.refs_3_, bf16[320,128,128]{2,1,0:T(8,128)(2,1)S(1)} %bitcast.3), custom_call_target="tpu_custom_call" | custom-call | tf_op jit(solution)/shard_map/pallas_call | solution.py:173
  63.7 4.6 %shard_map.104.refs_5_ = f32[16,512,128]{2,1,0:T(8,128)S(1)} custom-call(s32[448]{0:T(512)S(1)} %select_reduce_fusion.1.refs_0_, s32[224]{0:T(256)S(1)} %fusion.15.refs_1_, s32[65]{0:T(128)S(1)} %pad_add_fusion.refs_2_, bf16[48,512,128]{2,1,0:T(8,128)(2,1)S(1)} %shard_map.103.refs_3_, bf16[320,128,128]{2,1,0:T(8,128)(2,1)S(1)} %bitcast.3), custom_call_target="tpu_custom_call" | custom-call | tf_op jit(solution)/shard_map/pallas_call | solution.py:173
  70.7 4.1 %shard_map.112 = (s16[8,528,128]{2,1,0:T(8,128)(2,1)S(1)}, s16[8,528,128]{2,1,0:T(8,128)(2,1)S(1)}) custom-call(s32[448]{0:T(512)S(1)} %select_reduce_fusion.refs_0_.refs_4_, s32[224]{0:T(256)S(1)} %fusion.16.refs_1_.refs_5_, s32[65]{0:T(128)S(1)} %pad_add_fusion.1.refs_2_.refs_6_, bf16[16,512,128]{2,1,0:T(8,128)(2,1)S(1)} %shard_map.106.refs_3_.refs_7_, ...), custom_call_target="tpu_custom_call" | custom-call | tf_op jit(solution)/shard_map/pallas_call | solution.py:175
  74.9 3.2 %collective-permute-start.28 = (s16[8,528,128]{2,1,0:T(8,128)(2,1)S(1)}, s16[8,528,128]{2,1,0:T(8,128)(2,1)S(1)}, u32[]{:S(2)}, u32[]{:S(2)}) collective-permute-start(s16[8,528,128]{2,1,0:T(8,128)(2,1)S(1)} %get-tuple-element.106), channel_id=1, source_target_pairs={{1,0},{2,1},{3,2},{0,3},{5,4},{6,5},{7,6},{4,7},{9,8},{10,9},{11,1... | collective-permute-start | bytes 3244040 | tf_op jit(solution)/shard_map/ppermute | solution.py:294
  78.1 4.1 %shard_map.107 = (s16[8,528,128]{2,1,0:T(8,128)(2,1)S(1)}, s16[8,528,128]{2,1,0:T(8,128)(2,1)S(1)}) custom-call(s32[448]{0:T(512)S(1)} %select_reduce_fusion.refs_0_.refs_4_, s32[224]{0:T(256)S(1)} %fusion.16.refs_1_.refs_5_, s32[65]{0:T(128)S(1)} %pad_add_fusion.1.refs_2_.refs_6_, bf16[16,512,128]{2,1,0:T(8,128)(2,1)S(1)} %shard_map.106.refs_3_.refs_7_, ...), custom_call_target="tpu_custom_call" | custom-call | tf_op jit(solution)/shard_map/pallas_call | solution.py:175
  82.3 4.3 %collective-permute-start.25 = (s16[8,528,128]{2,1,0:T(8,128)(2,1)S(1)}, s16[8,528,128]{2,1,0:T(8,128)(2,1)S(1)}, u32[]{:S(2)}, u32[]{:S(2)}) collective-permute-start(s16[8,528,128]{2,1,0:T(8,128)(2,1)S(1)} %get-tuple-element.98), channel_id=1, source_target_pairs={{4,0},{5,1},{6,2},{7,3},{8,4},{9,5},{10,6},{11,7},{12,8},{13,9},{1... | collective-permute-start | bytes 3244040 | tf_op jit(solution)/shard_map/ppermute | solution.py:294
  88.4 6.3 %shard_map.117.sums_ref = f32[16,512,128]{2,1,0:T(8,128)S(1)} custom-call(s32[448]{0:T(512)S(1)} %select_reduce_fusion.1.refs_0_, s32[224]{0:T(256)S(1)} %fusion.15.refs_1_, s32[65]{0:T(128)S(1)} %pad_add_fusion.refs_2_, bf16[48,512,128]{2,1,0:T(8,128)(2,1)S(1)} %shard_map.103.refs_3_, s32[448]{0:T(512)S(1)} %select_reduce_fusion.refs_0_.refs_4_, ...), custom_call_target="tpu_custom_call" | custom-call | tf_op jit(solution)/shard_map/pallas_call | solution.py:173
  94.7 7.1 %shard_map.111.sums_ref = f32[16,512,128]{2,1,0:T(8,128)S(1)} custom-call(s32[448]{0:T(512)S(1)} %select_reduce_fusion.1.refs_0_, s32[224]{0:T(256)S(1)} %fusion.15.refs_1_, s32[65]{0:T(128)S(1)} %pad_add_fusion.refs_2_, bf16[48,512,128]{2,1,0:T(8,128)(2,1)S(1)} %shard_map.103.refs_3_, s32[448]{0:T(512)S(1)} %select_reduce_fusion.refs_0_.refs_4_, ...), custom_call_target="tpu_custom_call" | custom-call | tf_op jit(solution)/shard_map/pallas_call | solution.py:173
  102.6 3.2 %collective-permute-start.30 = (s16[4,528,128]{2,1,0:T(8,128)(2,1)S(1)}, s16[4,528,128]{2,1,0:T(8,128)(2,1)S(1)}, u32[]{:S(2)}, u32[]{:S(2)}) collective-permute-start(s16[4,528,128]{2,1,0:T(8,128)(2,1)S(1)} %get-tuple-element.108), channel_id=1, source_target_pairs={{1,0},{2,1},{3,2},{0,3},{5,4},{6,5},{7,6},{4,7},{9,8},{10,9},{11,1... | collective-permute-start | bytes 1622024 | tf_op jit(solution)/shard_map/ppermute | solution.py:294
  108.4 3.2 %collective-permute-start.36 = (s16[4,528,128]{2,1,0:T(8,128)(2,1)S(1)}, s16[4,528,128]{2,1,0:T(8,128)(2,1)S(1)}, u32[]{:S(2)}, u32[]{:S(2)}) collective-permute-start(s16[4,528,128]{2,1,0:T(8,128)(2,1)S(1)} %get-tuple-element.117), channel_id=1, source_target_pairs={{4,0},{5,1},{6,2},{7,3},{8,4},{9,5},{10,6},{11,7},{12,8},{13,9},{1... | collective-permute-start | bytes 1622024 | tf_op jit(solution)/shard_map/ppermute | solution.py:294
  111.6 4.4 %collective-permute-done.29.last_up_ref = s16[4,528,128]{2,1,0:T(8,128)(2,1)S(1)} collective-permute-done((s16[4,528,128]{2,1,0:T(8,128)(2,1)S(1)}, s16[4,528,128]{2,1,0:T(8,128)(2,1)S(1)}, u32[]{:S(2)}, u32[]{:S(2)}) %collective-permute-start.29) | collective-permute-done | bytes 540704 | tf_op jit(solution)/shard_map/ppermute | solution.py:294
  117.0 3.2 %collective-permute-start.32 = (s16[2,528,128]{2,1,0:T(8,128)(2,1)S(1)}, s16[2,528,128]{2,1,0:T(8,128)(2,1)S(1)}, u32[]{:S(2)}, u32[]{:S(2)}) collective-permute-start(s16[2,528,128]{2,1,0:T(8,128)(2,1)S(1)} %get-tuple-element.111), channel_id=1, source_target_pairs={{4,0},{5,1},{6,2},{7,3},{8,4},{9,5},{10,6},{11,7},{12,8},{13,9},{1... | collective-permute-start | bytes 811016 | tf_op jit(solution)/shard_map/ppermute | solution.py:294
  121.4 3.2 %collective-permute-start.38 = (s16[2,528,128]{2,1,0:T(8,128)(2,1)S(1)}, s16[2,528,128]{2,1,0:T(8,128)(2,1)S(1)}, u32[]{:S(2)}, u32[]{:S(2)}) collective-permute-start(s16[2,528,128]{2,1,0:T(8,128)(2,1)S(1)} %get-tuple-element.120), channel_id=1, source_target_pairs={{1,0},{2,1},{3,2},{0,3},{5,4},{6,5},{7,6},{4,7},{9,8},{10,9},{11,1... | collective-permute-start | bytes 811016 | tf_op jit(solution)/shard_map/ppermute | solution.py:294
  125.0 3.2 %collective-permute-start.34 = (s16[1,528,128]{2,1,0:T(8,128)(2,1)S(1)}, s16[1,528,128]{2,1,0:T(8,128)(2,1)S(1)}, u32[]{:S(2)}, u32[]{:S(2)}) collective-permute-start(s16[1,528,128]{2,1,0:T(8,128)(2,1)S(1)} %get-tuple-element.113), channel_id=1, source_target_pairs={{4,0},{5,1},{6,2},{7,3},{8,4},{9,5},{10,6},{11,7},{12,8},{13,9},{1... | collective-permute-start | bytes 405512 | tf_op jit(solution)/shard_map/ppermute | solution.py:294
  132.8 2.7 %collective-permute-done.39.refs_4_ = s16[1,528,128]{2,1,0:T(8,128)(2,1)S(1)} collective-permute-done((s16[1,528,128]{2,1,0:T(8,128)(2,1)S(1)}, s16[1,528,128]{2,1,0:T(8,128)(2,1)S(1)}, u32[]{:S(2)}, u32[]{:S(2)}) %collective-permute-start.39) | collective-permute-done | bytes 135200 | tf_op jit(solution)/shard_map/ppermute | solution.py:294
  (136 shorter events, 46.2 us)
Async XLA Ops:
  1.9 12.3 %collective-permute-start.3 = (bf16[2,512,128]{2,1,0:T(8,128)(2,1)S(1)}, bf16[2,512,128]{2,1,0:T(8,128)(2,1)S(1)}, u32[]{:S(2)}, u32[]{:S(2)}) collective-permute-start(bf16[2,512,128]{2,1,0:T(8,128)(2,1)S(1)} %get-tuple-element.137.refs_2_), channel_id=1, source_target_pairs={{12,0},{13,1},{14,2},{15,3},{0,4},{1,5},{2,6},{3,7},{4,8},{5,9},{6... | collective-permute-start | bytes 786440 | tf_op jit(solution)/shard_map/ppermute | solution.py:294
  3.7 12.3 %collective-permute-start.2 = (bf16[2,512,128]{2,1,0:T(8,128)(2,1)S(1)}, bf16[2,512,128]{2,1,0:T(8,128)(2,1)S(1)}, u32[]{:S(2)}, u32[]{:S(2)}) collective-permute-start(bf16[2,512,128]{2,1,0:T(8,128)(2,1)S(1)} %get-tuple-element.137.refs_2_), channel_id=1, source_target_pairs={{4,0},{5,1},{6,2},{7,3},{8,4},{9,5},{10,6},{11,7},{12,8},{13,9},{1... | collective-permute-start | bytes 786440 | tf_op jit(solution)/shard_map/ppermute | solution.py:294
  9.4 18.7 %collective-permute-start.9 = (bf16[4,512,128]{2,1,0:T(8,128)(2,1)S(1)}, bf16[4,512,128]{2,1,0:T(8,128)(2,1)S(1)}, u32[]{:S(2)}, u32[]{:S(2)}) collective-permute-start(bf16[4,512,128]{2,1,0:T(8,128)(2,1)S(1)} %shard_map.100.refs_0_), channel_id=1, source_target_pairs={{96,0},{112,16},{0,32},{16,48},{32,64},{48,80},{64,96},{80,112},{9... | collective-permute-start | bytes 1572872 | tf_op jit(solution)/shard_map/ppermute | solution.py:307
  14.2 17.9 %collective-permute-start.8 = (bf16[4,512,128]{2,1,0:T(8,128)(2,1)S(1)}, bf16[4,512,128]{2,1,0:T(8,128)(2,1)S(1)}, u32[]{:S(2)}, u32[]{:S(2)}) collective-permute-start(bf16[4,512,128]{2,1,0:T(8,128)(2,1)S(1)} %shard_map.100.refs_0_), channel_id=1, source_target_pairs={{32,0},{48,16},{64,32},{80,48},{96,64},{112,80},{0,96},{16,112},{3... | collective-permute-start | bytes 1572872 | tf_op jit(solution)/shard_map/ppermute | solution.py:307
  24.5 12.7 %collective-permute-start.11 = (bf16[4,512,128]{2,1,0:T(8,128)(2,1)S(1)}, bf16[4,512,128]{2,1,0:T(8,128)(2,1)S(1)}, u32[]{:S(2)}, u32[]{:S(2)}) collective-permute-start(bf16[4,512,128]{2,1,0:T(8,128)(2,1)S(1)} %get-tuple-element.74.refs_0_), channel_id=1, source_target_pairs={{12,0},{13,1},{14,2},{15,3},{0,4},{1,5},{2,6},{3,7},{4,8},{5,9},{6... | collective-permute-start | bytes 1572872 | tf_op jit(solution)/shard_map/ppermute | solution.py:294
  25.7 14.0 %collective-permute-start.10 = (bf16[4,512,128]{2,1,0:T(8,128)(2,1)S(1)}, bf16[4,512,128]{2,1,0:T(8,128)(2,1)S(1)}, u32[]{:S(2)}, u32[]{:S(2)}) collective-permute-start(bf16[4,512,128]{2,1,0:T(8,128)(2,1)S(1)} %get-tuple-element.74.refs_0_), channel_id=1, source_target_pairs={{4,0},{5,1},{6,2},{7,3},{8,4},{9,5},{10,6},{11,7},{12,8},{13,9},{1... | collective-permute-start | bytes 1572872 | tf_op jit(solution)/shard_map/ppermute | solution.py:294
  28.1 12.1 %collective-permute-start.13 = (bf16[4,512,128]{2,1,0:T(8,128)(2,1)S(1)}, bf16[4,512,128]{2,1,0:T(8,128)(2,1)S(1)}, u32[]{:S(2)}, u32[]{:S(2)}) collective-permute-start(bf16[4,512,128]{2,1,0:T(8,128)(2,1)S(1)} %get-tuple-element.80.refs_6_), channel_id=1, source_target_pairs={{3,0},{0,1},{1,2},{2,3},{7,4},{4,5},{5,6},{6,7},{11,8},{8,9},{9,10... | collective-permute-start | bytes 1572872 | tf_op jit(solution)/shard_map/ppermute | solution.py:294
  28.1 14.9 %collective-permute-start.12 = (bf16[4,512,128]{2,1,0:T(8,128)(2,1)S(1)}, bf16[4,512,128]{2,1,0:T(8,128)(2,1)S(1)}, u32[]{:S(2)}, u32[]{:S(2)}) collective-permute-start(bf16[4,512,128]{2,1,0:T(8,128)(2,1)S(1)} %get-tuple-element.80.refs_6_), channel_id=1, source_target_pairs={{1,0},{2,1},{3,2},{0,3},{5,4},{6,5},{7,6},{4,7},{9,8},{10,9},{11,1... | collective-permute-start | bytes 1572872 | tf_op jit(solution)/shard_map/ppermute | solution.py:294
  39.7 11.3 %collective-permute-start.17 = (bf16[4,512,128]{2,1,0:T(8,128)(2,1)S(1)}, bf16[4,512,128]{2,1,0:T(8,128)(2,1)S(1)}, u32[]{:S(2)}, u32[]{:S(2)}) collective-permute-start(bf16[4,512,128]{2,1,0:T(8,128)(2,1)S(1)} %get-tuple-element.79.refs_1_), channel_id=1, source_target_pairs={{12,0},{13,1},{14,2},{15,3},{0,4},{1,5},{2,6},{3,7},{4,8},{5,9},{6... | collective-permute-start | bytes 1572872 | tf_op jit(solution)/shard_map/ppermute | solution.py:294
  40.2 12.8 %collective-permute-start.16 = (bf16[4,512,128]{2,1,0:T(8,128)(2,1)S(1)}, bf16[4,512,128]{2,1,0:T(8,128)(2,1)S(1)}, u32[]{:S(2)}, u32[]{:S(2)}) collective-permute-start(bf16[4,512,128]{2,1,0:T(8,128)(2,1)S(1)} %get-tuple-element.79.refs_1_), channel_id=1, source_target_pairs={{4,0},{5,1},{6,2},{7,3},{8,4},{9,5},{10,6},{11,7},{12,8},{13,9},{1... | collective-permute-start | bytes 1572872 | tf_op jit(solution)/shard_map/ppermute | solution.py:294
  43.1 11.8 %collective-permute-start.19 = (bf16[4,512,128]{2,1,0:T(8,128)(2,1)S(1)}, bf16[4,512,128]{2,1,0:T(8,128)(2,1)S(1)}, u32[]{:S(2)}, u32[]{:S(2)}) collective-permute-start(bf16[4,512,128]{2,1,0:T(8,128)(2,1)S(1)} %get-tuple-element.84.refs_7_), channel_id=1, source_target_pairs={{3,0},{0,1},{1,2},{2,3},{7,4},{4,5},{5,6},{6,7},{11,8},{8,9},{9,10... | collective-permute-start | bytes 1572872 | tf_op jit(solution)/shard_map/ppermute | solution.py:294
  43.1 15.4 %collective-permute-start.18 = (bf16[4,512,128]{2,1,0:T(8,128)(2,1)S(1)}, bf16[4,512,128]{2,1,0:T(8,128)(2,1)S(1)}, u32[]{:S(2)}, u32[]{:S(2)}) collective-permute-start(bf16[4,512,128]{2,1,0:T(8,128)(2,1)S(1)} %get-tuple-element.84.refs_7_), channel_id=1, source_target_pairs={{1,0},{2,1},{3,2},{0,3},{5,4},{6,5},{7,6},{4,7},{9,8},{10,9},{11,1... | collective-permute-start | bytes 1572872 | tf_op jit(solution)/shard_map/ppermute | solution.py:294
  46.5 59.3 %collective-permute-start.26 = (bf16[16,512,128]{2,1,0:T(8,128)(2,1)S(1)}, bf16[16,512,128]{2,1,0:T(8,128)(2,1)S(1)}, u32[]{:S(2)}, u32[]{:S(2)}) collective-permute-start(bf16[16,512,128]{2,1,0:T(8,128)(2,1)S(1)} %shard_map.108.tiles_ref), channel_id=1, source_target_pairs={{16,0},{0,16},{48,32},{32,48},{80,64},{64,80},{112,96},{96,112},{1... | collective-permute-start | bytes 6291464 | tf_op jit(solution)/shard_map/ppermute | solution.py:307
  51.0 17.3 %collective-permute-start.20 = (bf16[4,512,128]{2,1,0:T(8,128)(2,1)S(1)}, bf16[4,512,128]{2,1,0:T(8,128)(2,1)S(1)}, u32[]{:S(2)}, u32[]{:S(2)}) collective-permute-start(bf16[4,512,128]{2,1,0:T(8,128)(2,1)S(1)} %collective-permute-done.10.refs_2_), channel_id=1, source_target_pairs={{4,0},{5,1},{6,2},{7,3},{8,4},{9,5},{10,6},{11,7},{12,8},{13,9},{1... | collective-permute-start | bytes 1572872 | tf_op jit(solution)/shard_map/ppermute | solution.py:294
  53.0 15.3 %collective-permute-start.22 = (bf16[4,512,128]{2,1,0:T(8,128)(2,1)S(1)}, bf16[4,512,128]{2,1,0:T(8,128)(2,1)S(1)}, u32[]{:S(2)}, u32[]{:S(2)}) collective-permute-start(bf16[4,512,128]{2,1,0:T(8,128)(2,1)S(1)} %collective-permute-done.12.refs_8_), channel_id=1, source_target_pairs={{1,0},{2,1},{3,2},{0,3},{5,4},{6,5},{7,6},{4,7},{9,8},{10,9},{11,1... | collective-permute-start | bytes 1572872 | tf_op jit(solution)/shard_map/ppermute | solution.py:294
  58.5 12.1 %collective-permute-start.23 = (bf16[4,512,128]{2,1,0:T(8,128)(2,1)S(1)}, bf16[4,512,128]{2,1,0:T(8,128)(2,1)S(1)}, u32[]{:S(2)}, u32[]{:S(2)}) collective-permute-start(bf16[4,512,128]{2,1,0:T(8,128)(2,1)S(1)} %collective-permute-done.19.refs_11_), channel_id=1, source_target_pairs={{3,0},{0,1},{1,2},{2,3},{7,4},{4,5},{5,6},{6,7},{11,8},{8,9},{9,10... | collective-permute-start | bytes 1572872 | tf_op jit(solution)/shard_map/ppermute | solution.py:294
  74.8 27.0 %collective-permute-start.27 = (s16[8,528,128]{2,1,0:T(8,128)(2,1)S(1)}, s16[8,528,128]{2,1,0:T(8,128)(2,1)S(1)}, u32[]{:S(2)}, u32[]{:S(2)}) collective-permute-start(s16[8,528,128]{2,1,0:T(8,128)(2,1)S(1)} %get-tuple-element.105), channel_id=1, source_target_pairs={{3,0},{0,1},{1,2},{2,3},{7,4},{4,5},{5,6},{6,7},{11,8},{8,9},{9,10... | collective-permute-start | bytes 3244040 | tf_op jit(solution)/shard_map/ppermute | solution.py:294
  74.9 26.9 %collective-permute-start.28 = (s16[8,528,128]{2,1,0:T(8,128)(2,1)S(1)}, s16[8,528,128]{2,1,0:T(8,128)(2,1)S(1)}, u32[]{:S(2)}, u32[]{:S(2)}) collective-permute-start(s16[8,528,128]{2,1,0:T(8,128)(2,1)S(1)} %get-tuple-element.106), channel_id=1, source_target_pairs={{1,0},{2,1},{3,2},{0,3},{5,4},{6,5},{7,6},{4,7},{9,8},{10,9},{11,1... | collective-permute-start | bytes 3244040 | tf_op jit(solution)/shard_map/ppermute | solution.py:294
  82.2 25.4 %collective-permute-start.24 = (s16[8,528,128]{2,1,0:T(8,128)(2,1)S(1)}, s16[8,528,128]{2,1,0:T(8,128)(2,1)S(1)}, u32[]{:S(2)}, u32[]{:S(2)}) collective-permute-start(s16[8,528,128]{2,1,0:T(8,128)(2,1)S(1)} %get-tuple-element.97), channel_id=1, source_target_pairs={{12,0},{13,1},{14,2},{15,3},{0,4},{1,5},{2,6},{3,7},{4,8},{5,9},{6... | collective-permute-start | bytes 3244040 | tf_op jit(solution)/shard_map/ppermute | solution.py:294
  82.3 25.3 %collective-permute-start.25 = (s16[8,528,128]{2,1,0:T(8,128)(2,1)S(1)}, s16[8,528,128]{2,1,0:T(8,128)(2,1)S(1)}, u32[]{:S(2)}, u32[]{:S(2)}) collective-permute-start(s16[8,528,128]{2,1,0:T(8,128)(2,1)S(1)} %get-tuple-element.98), channel_id=1, source_target_pairs={{4,0},{5,1},{6,2},{7,3},{8,4},{9,5},{10,6},{11,7},{12,8},{13,9},{1... | collective-permute-start | bytes 3244040 | tf_op jit(solution)/shard_map/ppermute | solution.py:294
  102.5 13.5 %collective-permute-start.29 = (s16[4,528,128]{2,1,0:T(8,128)(2,1)S(1)}, s16[4,528,128]{2,1,0:T(8,128)(2,1)S(1)}, u32[]{:S(2)}, u32[]{:S(2)}) collective-permute-start(s16[4,528,128]{2,1,0:T(8,128)(2,1)S(1)} %get-tuple-element.107), channel_id=1, source_target_pairs={{3,0},{0,1},{1,2},{2,3},{7,4},{4,5},{5,6},{6,7},{11,8},{8,9},{9,10... | collective-permute-start | bytes 1622024 | tf_op jit(solution)/shard_map/ppermute | solution.py:294
  102.6 13.5 %collective-permute-start.30 = (s16[4,528,128]{2,1,0:T(8,128)(2,1)S(1)}, s16[4,528,128]{2,1,0:T(8,128)(2,1)S(1)}, u32[]{:S(2)}, u32[]{:S(2)}) collective-permute-start(s16[4,528,128]{2,1,0:T(8,128)(2,1)S(1)} %get-tuple-element.108), channel_id=1, source_target_pairs={{1,0},{2,1},{3,2},{0,3},{5,4},{6,5},{7,6},{4,7},{9,8},{10,9},{11,1... | collective-permute-start | bytes 1622024 | tf_op jit(solution)/shard_map/ppermute | solution.py:294
  108.3 12.1 %collective-permute-start.35 = (s16[4,528,128]{2,1,0:T(8,128)(2,1)S(1)}, s16[4,528,128]{2,1,0:T(8,128)(2,1)S(1)}, u32[]{:S(2)}, u32[]{:S(2)}) collective-permute-start(s16[4,528,128]{2,1,0:T(8,128)(2,1)S(1)} %get-tuple-element.116), channel_id=1, source_target_pairs={{12,0},{13,1},{14,2},{15,3},{0,4},{1,5},{2,6},{3,7},{4,8},{5,9},{6... | collective-permute-start | bytes 1622024 | tf_op jit(solution)/shard_map/ppermute | solution.py:294
  108.4 12.0 %collective-permute-start.36 = (s16[4,528,128]{2,1,0:T(8,128)(2,1)S(1)}, s16[4,528,128]{2,1,0:T(8,128)(2,1)S(1)}, u32[]{:S(2)}, u32[]{:S(2)}) collective-permute-start(s16[4,528,128]{2,1,0:T(8,128)(2,1)S(1)} %get-tuple-element.117), channel_id=1, source_target_pairs={{4,0},{5,1},{6,2},{7,3},{8,4},{9,5},{10,6},{11,7},{12,8},{13,9},{1... | collective-permute-start | bytes 1622024 | tf_op jit(solution)/shard_map/ppermute | solution.py:294
  (28 other events, 247.0 us)
